TPU v7x, 32 devices: a whole 2x2x4 slice. The times are simulated.
32 devices in a mesh: ctx: 16 (over z, x, core), head: 2 (over y), ep: 1.
Axes of the slice: x: 2, y: 2, z: 4, core: 2. Of those that a mesh axis runs over, the one named last changes fastest.
Arguments:
- q_latent: bfloat16 [8192, 16, 576], P('ctx', ('head', 'ep')), may hold values from -20 to 20
- kv_latent: bfloat16 [8192, 576], P('ctx'), may hold values from -20 to 20
- w_value: bfloat16 [16, 512, 128], P(('head', 'ep')), may hold values from -0.25 to 0.25
- w_out: bfloat16 [2048, 2048], P(('head', 'ep')), may hold values from -0.125 to 0.125
- resid: bfloat16 [8192, 2048], P(('ctx', 'head', 'ep')), may hold values from -40 to 40
- norm_gain: float32 [2048], replicated, may hold values from 0.1 to 1.9
- w_gate: bfloat16 [16, 2048, 1408], P('ctx', None, 'head'), may hold values from -0.125 to 0.125
- w_up: bfloat16 [16, 2048, 1408], P('ctx', None, 'head'), may hold values from -0.125 to 0.125
- w_down_t: bfloat16 [16, 2048, 1408], P('ctx', None, 'head'), may hold values from -0.15625 to 0.15625
- expert_ids: int32 [8192, 6], P(('ctx', 'head', 'ep')), may hold values from 0 to 15, all different within a row; in each aligned block of 256 rows (0 to 255, 256 to 511, ...) at most 120 rows name the same one
- route_scores: float32 [8192, 6], P(('ctx', 'head', 'ep')), may hold values from 0.1 to 1
Outputs:
- layer_out: bfloat16 [8192, 2048], P(('ctx', 'head', 'ep'))
Inputs may be any that keep to these rules, and one draw needn't show every extreme that they name: `expert_ids`: each row names 6 different experts. In each aligned block of 256 rows (the rows of one device) no expert is named by more than 120 rows, and in some block an expert is named by exactly 120 rows.
All inputs are finite; a program needn't handle non-finite values.
Results may differ from a plain program's by a relative error of at most 0.007.
Values may be sent and summed in bfloat16 or wider, within the bound.
No kernel may reach another device: no remote copies, remote signals or barrier semaphores. Data moves between devices by JAX's collectives and lax.ppermute only.
A program may use at most 256 MiB of HBM per device.

v0:
```python
import jax
import jax.numpy as jnp
from jax import lax
from jax.sharding import PartitionSpec as P

ROPE = 64
NOPE = 128
TOPK = 6


routed_factor = 2.446
norm_epsilon = 1e-06
masked_score = -1e30


def expert_half(inputs, gate_part, up_part, down_part):
    gate = jnp.dot(inputs, gate_part, preferred_element_type=jnp.float32)
    upward = jnp.dot(inputs, up_part, preferred_element_type=jnp.float32)
    hidden = (jax.nn.silu(gate) * upward).astype(jnp.bfloat16)
    return lax.dot_general(
        hidden, down_part, (((1,), (1,)), ((), ())), preferred_element_type=jnp.float32
    )


def make_projection(source, piece):
    return jnp.dot(source, piece, preferred_element_type=jnp.float32)


def per_device(
    q_latent,
    kv_latent,
    w_value,
    w_out,
    resid,
    norm_gain,
    w_gate,
    w_up,
    w_down_t,
    expert_ids,
    route_scores,
):
    tokens_here = q_latent.shape[0]
    heads_here = q_latent.shape[1]
    latent_width = w_value.shape[1]
    width = resid.shape[1]
    rows = resid.shape[0]
    query_rows = tokens_here * heads_here
    score_scale = (NOPE + ROPE) ** (-0.5)
    queries = q_latent.reshape(query_rows, q_latent.shape[2])
    first_token = lax.axis_index("ctx") * tokens_here
    last_token = first_token + tokens_here - 1
    query_pos = first_token + jnp.arange(query_rows, dtype=jnp.int32) // heads_here
    start_state = (
        jnp.full((query_rows,), masked_score, jnp.float32),
        jnp.zeros((query_rows,), jnp.float32),
        jnp.zeros((query_rows, latent_width), jnp.float32),
    )
    keys = lax.all_gather(kv_latent, "ctx", axis=0, tiled=True)
    count = keys.shape[0]

    def compute(state):
        highest, denominator, accum = state
        scores = (
            lax.dot_general(
                queries, keys, (((1,), (1,)), ((), ())), preferred_element_type=jnp.float32
            )
            * score_scale
        )
        key_pos = jnp.arange(count, dtype=jnp.int32)
        visible = key_pos[None, :] <= query_pos[:, None]
        scores = jnp.where(visible, scores, masked_score)
        new_highest = jnp.maximum(highest, jnp.max(scores, axis=1))
        weights = jnp.where(visible, jnp.exp(scores - new_highest[:, None]), 0.0)
        denominator = jnp.sum(weights, axis=1)
        values = keys[:, :latent_width]
        accum = jnp.dot(weights.astype(jnp.bfloat16), values, preferred_element_type=jnp.float32)
        return (new_highest, denominator, accum)

    highest, denominator, accum = lax.cond(
        jnp.int32(0) > last_token, lambda state: state, compute, start_state
    )
    latent_out = (
        (accum / denominator[:, None])
        .astype(jnp.bfloat16)
        .reshape(tokens_here, heads_here, latent_width)
    )
    head_out = jnp.einsum(
        "thl,hlv->thv", latent_out, w_value, preferred_element_type=jnp.float32
    ).astype(jnp.bfloat16)
    grouped = lax.all_to_all(head_out, ("head", "ep"), split_axis=0, concat_axis=1, tiled=True)
    flat_heads = grouped.reshape(rows, grouped.shape[1] * grouped.shape[2])
    attended = make_projection(
        flat_heads, lax.all_gather(w_out, ("head", "ep"), axis=0, tiled=True)
    )
    after_attn = lax.optimization_barrier(
        (resid.astype(jnp.float32) + attended).astype(jnp.bfloat16)
    )
    widened = after_attn.astype(jnp.float32)
    mean_square = jnp.mean(widened * widened, axis=1, keepdims=True)
    normed = (widened * lax.rsqrt(mean_square + norm_epsilon) * norm_gain).astype(jnp.bfloat16)
    experts_here = lax.axis_size("ctx")
    capacity = 5 * rows * TOPK // (4 * experts_here)
    chosen = expert_ids.reshape(rows * TOPK)
    onehot = (chosen[:, None] == jnp.arange(experts_here, dtype=jnp.int32)[None, :]).astype(
        jnp.int32
    )
    ranking = jnp.sum(onehot * (jnp.cumsum(onehot, axis=0) - 1), axis=1)
    slot_ids = chosen * capacity + ranking
    slot_table = jnp.arange(experts_here * capacity, dtype=jnp.int32)
    placing = jnp.any(slot_ids.reshape(rows, TOPK)[None, :, :] == slot_table[:, None, None], axis=2)
    dispatch = jnp.dot(
        placing.astype(jnp.bfloat16), normed, preferred_element_type=jnp.float32
    ).astype(jnp.bfloat16)
    dispatch = dispatch.reshape(experts_here, capacity, width)
    arrived = lax.all_to_all(dispatch, "ctx", split_axis=0, concat_axis=0, tiled=True)
    arrived_rows = arrived.reshape(experts_here * capacity, width)
    produced = expert_half(
        arrived_rows,
        lax.all_gather(w_gate, "head", axis=2, tiled=True)[0],
        lax.all_gather(w_up, "head", axis=2, tiled=True)[0],
        lax.all_gather(w_down_t, "head", axis=2, tiled=True)[0],
    )
    outgoing = produced.astype(jnp.bfloat16).reshape(experts_here, capacity, width)
    returned = lax.all_to_all(outgoing, "ctx", split_axis=0, concat_axis=0, tiled=True)
    picked = returned.reshape(experts_here * capacity, width)[slot_ids].reshape(rows, TOPK, width)
    combine = route_scores / jnp.sum(route_scores, axis=1, keepdims=True)
    combined = jnp.sum(picked.astype(jnp.float32) * combine[:, :, None], axis=1)
    return (widened + routed_factor * combined).astype(jnp.bfloat16)


def solution(mesh):
    placed = (
        P("ctx", ("head", "ep"), None),
        P("ctx", None),
        P(("head", "ep"), None, None),
        P(("head", "ep"), None),
        P(("ctx", "head", "ep"), None),
        P(),
        P("ctx", None, "head"),
        P("ctx", None, "head"),
        P("ctx", None, "head"),
        P(("ctx", "head", "ep"), None),
        P(("ctx", "head", "ep"), None),
    )
    return jax.shard_map(
        per_device,
        mesh=mesh,
        in_specs=placed,
        out_specs=P(("ctx", "head", "ep"), None),
        check_vma=False,
    )
```

profile of v0, /device:TPU:11, one launch (start us, length us, event | category | flops | bytes accessed | tf_op | source)
XLA Modules:
  0.0 807.4 jit_solution(3771787290404247813)
XLA Ops:
  6.5 0.0 copy-start
  6.5 0.0 all-gather.6.cloned.1.call-start
  6.5 2.2 copy.44
  8.8 0.0 all-gather.6.cloned.1.call-update
  8.8 0.0 all-gather.8.cloned.1.call-start
  8.8 0.7 all-gather.8.cloned.1.call-update
  9.5 0.8 copy.49
  10.4 0.0 copy-start.2
  10.4 0.1 eq.42
  10.5 0.7 eq.38
  11.3 4.5 reduce-window.6
  15.8 0.4 slice_reduce_fusion
  16.3 0.2 reduce-window.9
  16.4 0.8 add_add_fusion
  17.2 79.8 %all-gather.6.cloned.1.call-done = bf16[8192,576]{1,0:T(8,128)(2,1)} async-done(((bf16[512,576]{1,0:T(8,128)(2,1)}), bf16[8192,576]{1,0:T(8,128)(2,1)}) %all-gather.6.cloned.1.call-update) | async-done | bytes 9437200 | tf_op jit(solution)/shard_map/all_gather | solution.py:58
  97.0 0.0 copy-done.2
  97.0 180.6 %conditional.1 = (f32[4096]{0:T(1024)S(1)}, f32[4096,512]{1,0:T(8,128)}) conditional(s32[]{:T(128)} %convert_element_type.53, (s32[]{:T(128)}, s32[4096]{0:T(1024)S(1)}, s32[4096]{0:T(1024)S(1)}, bf16[512,8,576]{0,2,1:T(8,128)(2,1)}, bf16[8192,576]{1,0:T(8,128)(2,1)}) %tuple.23, () %tuple.20), branch_computations={%region_0.3_spmd.clone, %region_3.4_spmd} | conditional | flops 73551347712 | bytes 443219968 | solution.py:79
  97.1 9.2 %copy.45 = bf16[512,8,576]{2,1,0:T(8,128)(2,1)} copy(bf16[512,8,576]{0,2,1:T(8,128)(2,1)} %get-tuple-element.100) | data formatting | bytes 9437184 | tf_op jit(solution)/shard_map
  106.3 70.9 %fusion = (f32[4096]{0:T(1024)S(1)}, f32[4096,8192]{1,0:T(8,128)}) fusion(s32[4096]{0:T(1024)S(1)} %fusion.8, bf16[8192,576]{1,0:T(8,128)(2,1)} %get-tuple-element.69, bf16[512,8,576]{2,1,0:T(8,128)(2,1)} %copy.45), kind=kOutput, calls=%fused_computation.4 | convolution fusion | flops 38788919296 | bytes 148406272 | tf_op jit(solution)/shard_map/cond/branch_0_fun/dot_general | solution.py:64
  177.2 46.8 %fusion.2 = f32[4096]{0:T(1024)S(1)} fusion(f32[4096,8192]{1,0:T(8,128)} %get-tuple-element.103, f32[4096]{0:T(1024)S(1)} %broadcast_maximum_fusion, s32[4096]{0:T(1024)S(1)} %fusion.8), kind=kLoop, calls=%fused_computation.6 | loop fusion | flops 201322496 | bytes 134266880 | tf_op jit(solution)/shard_map/cond/branch_0_fun/reduce_sum | solution.py:74
  224.0 53.7 %fusion.3 = f32[4096,512]{1,0:T(8,128)} fusion(f32[4096,8192]{1,0:T(8,128)} %get-tuple-element.103, f32[4096]{0:T(1024)S(1)} %broadcast_maximum_fusion, s32[4096]{0:T(1024)S(1)} %fusion.8, bf16[8192,576]{1,0:T(8,128)(2,1)} %get-tuple-element.69), kind=kOutput, calls=%fused_computation.7 | convolution fusion | flops 34561064960 | bytes 151027712 | tf_op jit(solution)/shard_map/cond/branch_0_fun/dot_general | solution.py:76
  277.7 3.9 fusion.22
  281.5 0.0 copy-done
  281.5 0.0 copy-start.4
  281.5 0.0 copy-start.5
  281.5 0.0 copy-start.3
  281.6 1.4 fusion.31
  283.0 1.7 copy.47
  284.6 3.6 all-to-all-start
  288.2 0.0 copy-done.4
  288.2 0.0 copy-done.5
  288.3 0.1 reduce_sum.51
  288.4 0.0 copy-done.3
  288.5 0.1 copy.52
  288.6 3.0 fusion.13
  291.6 10.1 %all-to-all-done = bf16[512,8,128]{2,1,0:T(8,128)(2,1)S(1)} async-done(((bf16[512,8,128]{2,1,0:T(8,128)(2,1)}), bf16[512,8,128]{2,1,0:T(8,128)(2,1)S(1)}, u32[]{:S(2)}, u32[]{:S(2)}) %all-to-all-start) | async-done | bytes 1048608 | tf_op jit(solution)/shard_map/all_to_all | solution.py:90
  301.7 0.7 copy.48
  302.3 0.0 all-gather.8.cloned.1.call-done
  302.4 0.0 copy-start.1
  302.4 0.0 copy-start.7
  302.4 6.0 fusion.23
  308.4 0.3 fusion.24
  308.7 0.0 copy-done.1
  308.7 5.4 convolution_convert_fusion.1
  314.1 7.3 all-to-all-start.1
  321.4 0.0 all-gather.10.cloned.1.call-start
  321.5 0.7 all-gather.10.cloned.1.call-update
  322.2 0.0 all-gather.14.cloned.1.call-start
  322.2 0.5 all-gather.14.cloned.1.call-update
  322.8 0.0 all-gather.12.cloned.1.call-start
  322.8 0.5 all-gather.12.cloned.1.call-update
  323.3 74.5 %all-gather.10.cloned.1.call-done = bf16[1,2048,1408]{1,2,0:T(8,128)(2,1)} async-done(((bf16[1,2048,704]{1,2,0:T(8,128)(2,1)}), bf16[1,2048,1408]{1,2,0:T(8,128)(2,1)}) %all-gather.10.cloned.1.call-update) | async-done | bytes 5767184 | tf_op jit(solution)/shard_map/all_gather | solution.py:119
  397.8 95.0 %all-to-all-done.1 = bf16[16,120,2048]{2,1,0:T(8,128)(2,1)} async-done(((bf16[16,120,2048]{2,1,0:T(8,128)(2,1)}), bf16[16,120,2048]{2,1,0:T(8,128)(2,1)}, u32[]{:S(2)}, u32[]{:S(2)}) %all-to-all-start.1) | async-done | bytes 7864352 | tf_op jit(solution)/shard_map/all_to_all | solution.py:115
  492.9 18.3 %fusion.17 = f32[1920,1408]{1,0:T(8,128)} fusion(bf16[1920,2048]{1,0:T(8,128)(2,1)} %bitcast.7, bf16[1,2048,1408]{1,2,0:T(8,128)(2,1)} %all-gather.10.cloned.1.call-done), kind=kOutput, calls=%fused_computation.29 | convolution fusion | flops 11072962560 | bytes 24444928 | tf_op jit(solution)/shard_map/dot_general | solution.py:17
  511.2 38.4 %all-gather.12.cloned.1.call-done = bf16[1,2048,1408]{1,2,0:T(8,128)(2,1)} async-done(((bf16[1,2048,704]{1,2,0:T(8,128)(2,1)}), bf16[1,2048,1408]{1,2,0:T(8,128)(2,1)}) %all-gather.12.cloned.1.call-update) | async-done | bytes 5767184 | tf_op jit(solution)/shard_map/all_gather | solution.py:120
  549.6 33.4 %convolution_convert_fusion = bf16[1920,2048]{1,0:T(8,128)(2,1)} fusion(bf16[1,2048,1408]{1,2,0:T(8,128)(2,1)} %all-gather.14.cloned.1.call-done, f32[1920,1408]{1,0:T(8,128)} %fusion.17, bf16[1920,2048]{1,0:T(8,128)(2,1)} %bitcast.7, bf16[1,2048,1408]{1,2,0:T(8,128)(2,1)} %all-gather.12.cloned.1.call-done), kind=kOutput, calls=%fused_computation.25 | convolution fusion | flops 22166077440 | bytes 38076416 | tf_op jit(solution)/shard_map/dot_general | solution.py:20
  583.0 7.0 all-to-all-start.2
  590.0 0.1 mul.79
  590.2 0.1 copy.53
  590.4 170.6 %all-to-all-done.2 = bf16[16,120,2048]{2,1,0:T(8,128)(2,1)} async-done(((bf16[16,120,2048]{2,1,0:T(8,128)(2,1)}), bf16[16,120,2048]{2,1,0:T(8,128)(2,1)}, u32[]{:S(2)}, u32[]{:S(2)}) %all-to-all-start.2) | async-done | bytes 7864352 | tf_op jit(solution)/shard_map/all_to_all | solution.py:124
  761.0 17.0 %gather_fusion = bf16[1536,2048]{1,0:T(8,128)(2,1)} fusion(bf16[1920,2048]{1,0:T(8,128)(2,1)} %bitcast.12, s32[2048]{0:T(1024)S(1)} %pad_clamp_fusion), kind=kCustom, calls=%fused_computation | custom fusion | bytes 12589056 | tf_op jit(solution)/shard_map/gather | solution.py:125
  778.0 11.7 %reshape.106 = f32[256,6,2048]{2,1,0:T(8,128)} reshape(bf16[1536,2048]{1,0:T(8,128)(2,1)} %gather_fusion) | data formatting | bytes 18874368 | tf_op jit(solution)/shard_map/convert_element_type | solution.py:127
  789.7 9.4 %multiply_reduce_fusion = f32[256,2048]{1,0:T(8,128)S(1)} fusion(f32[256,6,2048]{2,1,0:T(8,128)} %reshape.106, f32[256,6]{1,0:T(8,128)S(1)} %copy.53), kind=kLoop, calls=%fused_computation.20 | loop fusion | flops 5767168 | bytes 14686208 | tf_op jit(solution)/shard_map/reduce_sum | solution.py:127
  799.1 1.3 fusion.27
  (15 shorter events, 0.2 us)
Async XLA Ops:
  6.5 275.0 %copy-start = (bf16[8,512,128]{2,1,0:T(8,128)(2,1)S(1)}, bf16[8,512,128]{2,1,0:T(8,128)(2,1)}, u32[]{:S(2)}) copy-start(bf16[8,512,128]{2,1,0:T(8,128)(2,1)} %param.15) | copy-start | bytes 3145732
  6.5 90.5 %all-gather.6.cloned.1.call-start = ((), (), s32[]{:S(2)}) async-start(), calls=%async_computation.3 | async-start | bytes 11141120 | tf_op jit(solution)/shard_map/all_gather | solution.py:58
  8.8 293.6 %all-gather.8.cloned.1.call-start = ((), (), s32[]{:S(2)}) async-start(), calls=%async_computation.4 | async-start | bytes 12582912 | tf_op jit(solution)/shard_map/all_gather | solution.py:93
  10.4 86.7 %copy-start.2 = (s32[256,6]{1,0:T(8,128)}, s32[256,6]{1,0:T(8,128)S(1)}, u32[]{:S(2)}) copy-start(s32[256,6]{1,0:T(8,128)S(1)} %copy.49) | copy-start | bytes 18436
  281.5 6.7 copy-start.4
  281.5 6.7 copy-start.5
  281.5 6.9 copy-start.3
  284.6 17.0 %all-to-all-start = ((bf16[512,8,128]{2,1,0:T(8,128)(2,1)}), bf16[512,8,128]{2,1,0:T(8,128)(2,1)S(1)}, u32[]{:S(2)}, u32[]{:S(2)}) async-start(bf16[512,8,128]{2,1,0:T(8,128)(2,1)} %copy.47), calls=%async_computation | async-start | bytes 2097152 | tf_op jit(solution)/shard_map/all_to_all | solution.py:90
  302.4 6.3 copy-start.1
  302.4 6.3 copy-start.7
  314.1 178.8 %all-to-all-start.1 = ((bf16[16,120,2048]{2,1,0:T(8,128)(2,1)}), bf16[16,120,2048]{2,1,0:T(8,128)(2,1)}, u32[]{:S(2)}, u32[]{:S(2)}) async-start(bf16[16,120,2048]{2,1,0:T(8,128)(2,1)} %bitcast.48), calls=%async_computation.1 | async-start | bytes 15728640 | tf_op jit(solution)/shard_map/all_to_all | solution.py:115
  321.4 76.4 %all-gather.10.cloned.1.call-start = ((), (), s32[]{:S(2)}) async-start(), calls=%async_computation.5 | async-start | bytes 8650752 | tf_op jit(solution)/shard_map/all_gather | solution.py:119
  322.2 189.0 %all-gather.14.cloned.1.call-start = ((), (), s32[]{:S(2)}) async-start(), calls=%async_computation.7 | async-start | bytes 8650752 | tf_op jit(solution)/shard_map/all_gather | solution.py:121
  322.8 226.8 %all-gather.12.cloned.1.call-start = ((), (), s32[]{:S(2)}) async-start(), calls=%async_computation.6 | async-start | bytes 8650752 | tf_op jit(solution)/shard_map/all_gather | solution.py:120
  583.0 7.2 copy-start.6
  583.0 178.0 %all-to-all-start.2 = ((bf16[16,120,2048]{2,1,0:T(8,128)(2,1)}), bf16[16,120,2048]{2,1,0:T(8,128)(2,1)}, u32[]{:S(2)}, u32[]{:S(2)}) async-start(bf16[16,120,2048]{2,1,0:T(8,128)(2,1)} %bitcast.49), calls=%async_computation.2 | async-start | bytes 15728640 | tf_op jit(solution)/shard_map/all_to_all | solution.py:124
Sparse Core Ops, SparseCore 0:
  9.6 87.3 all-gather.5
  98.6 103.3 all-gather.7
  323.8 73.9 all-gather.9
  399.2 74.4 all-gather.13
  475.1 74.4 all-gather.11
where the time goes:
time: 815 us; the launch traced here: 807 us
  waiting for transfers between devices  471 us (58%)
  matrix products  189 us (23%)
  other arithmetic  70.3 us (9%)
  local copies, waits for them, and re-layouts  45.1 us (6%)
  starting transfers between devices  18.1 us (2%)
  between operations  13.8 us (2%)
    all_to_all x1, waiting for transfers between devices, per_device(): lax.all_to_all(outgoing, 'ctx', split_axis=0, concat_axis=0, tiled=True)  171 us
    all_to_all x1, waiting for transfers between devices, per_device(): lax.all_to_all(dispatch, 'ctx', split_axis=0, concat_axis=0, tiled=True)  95 us
    all_gather x1, waiting for transfers between devices, per_device(): keys = lax.all_gather(kv_latent, 'ctx', axis=0, tiled=True)  79.8 us
    all_gather x1, waiting for transfers between devices, per_device(): lax.all_gather(w_gate, 'head', axis=2, tiled=True)[0]  74.5 us
    dot_general x1, matrix products, compute(): lax.dot_general(queries, keys, (((1,), (1,)), ((), ())), preferred_elemen...  70.9 us
    dot_general x1, matrix products, compute(): jnp.dot(weights.astype(jnp.bfloat16), values, preferred_element_type=jnp....  53.7 us
    reduce_sum x1, other arithmetic, compute(): denominator = jnp.sum(weights, axis=1)  46.8 us
    all_gather x1, waiting for transfers between devices, per_device(): lax.all_gather(w_up, 'head', axis=2, tiled=True)[0]  38.4 us
  transfers between devices with their start and end apart: 8, of which 6 were waited for; matrix products, arithmetic and copies ran while one was open for 27% of the time, Pallas kernels for 0%

commit v1 on v0

v1 whole, which is shorter than its diff:
```python
import functools
import math

import jax
import jax.numpy as jnp
from jax import lax
from jax.experimental import pallas as pl
from jax.experimental.pallas import tpu as pltpu
from jax.sharding import PartitionSpec as P

ROPE = 64
NOPE = 128
TOPK = 6

routed_factor = 2.446
norm_epsilon = 1e-06
masked_score = -1e30
LANES = 128
SQUARE = 4


def exp2_scale():
    return (NOPE + ROPE) ** (-0.5) * math.log2(math.e)


def attend_kernel(blocks, merge, first, last, mode_ref, q_ref, *refs):
    key_refs, refs = refs[:blocks], refs[blocks:]
    if not first:
        m_in, l_in, acc_in = refs[:3]
        refs = refs[3:]
    if last:
        wv_ref, out_ref = refs[:2]
        refs = refs[2:]
    m_s, l_s, acc_s, q_s, kt, kk, s0, s1, sems = refs
    heads, _, tokens = q_ref.shape
    units, _, columns = q_s.shape
    block_keys = key_refs[0].shape[1]
    latent = acc_s.shape[1]
    chunk = SQUARE * block_keys
    chunks = blocks // SQUARE
    visible = mode_ref[blocks + 1]
    total = visible * units
    factor = exp2_scale()
    lazy = chunks > 1 and units % 2 == 0

    def columns_of(i, n):
        return pl.ds(pl.multiple_of(i * n, LANES), n)

    def copy_of(i, source=None):
        return pltpu.make_async_copy(
            key_refs[0 if source is None else source], kt.at[:, columns_of(i, block_keys)], sems.at[i]
        )

    def wait_chunk(c):
        for j in range(SQUARE):
            copy_of(c * SQUARE + j).wait()

    def turn(i):
        kk[columns_of(i, block_keys), :] = jnp.transpose(kt[:, columns_of(i, block_keys)])

    for c in range(chunks):

        @pl.when(c < visible)
        def _():
            for j in range(SQUARE):
                copy_of(c * SQUARE + j, c * SQUARE + j).start()

    if first:
        m_s[...] = jnp.full(m_s.shape, masked_score, jnp.float32)
        l_s[...] = jnp.zeros(l_s.shape, jnp.float32)
        acc_s[...] = jnp.zeros(acc_s.shape, jnp.float32)
    else:
        m_s[...] = m_in[...]
        l_s[...] = l_in[...]
        acc_s[...] = acc_in[...]
    for h in range(heads):
        q_s[h // merge, :, (h % merge) * tokens : (h % merge + 1) * tokens] = q_ref[h]

    @pl.when(visible > 0)
    def _():
        wait_chunk(0)
        for i in range(SQUARE):
            turn(i)

    if not lazy:
        for c in range(1, chunks):

            @pl.when(c < visible)
            def _():
                wait_chunk(c)
                for i in range(SQUARE):
                    turn(c * SQUARE + i)

    def scores(t, buffer):
        t = jnp.maximum(jnp.minimum(t, total - 1), 0)
        buffer[...] = jnp.dot(
            kk[columns_of(t // units, chunk), :],
            q_s[t % units],
            preferred_element_type=jnp.float32,
        )

    def use(t, buffer):
        c, u = t // units, t % units
        if first:
            shape = (block_keys, columns)
            token = lax.broadcasted_iota(jnp.int32, shape, 1)
            gap = lax.broadcasted_iota(jnp.int32, shape, 0) - token % tokens
            s = jnp.concatenate(
                [
                    jnp.where(
                        gap <= mode_ref[c * SQUARE + j],
                        buffer[j * block_keys : (j + 1) * block_keys],
                        masked_score,
                    )
                    for j in range(SQUARE)
                ],
                axis=0,
            )
        else:
            s = buffer[...]
        old = m_s[u]
        new = jnp.maximum(old, jnp.max(s, axis=0, keepdims=True))
        alpha = jnp.exp2((old - new) * factor)
        p = jnp.exp2((s - new) * factor)
        l_s[u] = l_s[u] * alpha + jnp.sum(p, axis=0, keepdims=True)
        m_s[u] = new
        acc_s[u] = acc_s[u] * alpha + jnp.dot(
            kt[:latent, columns_of(c, chunk)],
            p.astype(jnp.bfloat16),
            preferred_element_type=jnp.float32,
        )

    scores(0, s0)

    def body(i, unused):
        t = 2 * i
        if lazy:

            @pl.when((t % units == 0) & (t // units + 1 < visible))
            def _():
                wait_chunk(t // units + 1)

        scores(t + 1, s1)
        use(t, s0)
        if lazy:
            each = -(-SQUARE * 2 // units)
            for j in range(each):
                place = jnp.minimum(t % units // 2 * each + j, SQUARE - 1)
                turn(jnp.minimum(t // units + 1, visible - 1) * SQUARE + place)
        scores(t + 2, s0)
        if units % 2 == 0:
            use(t + 1, s1)
        else:

            @pl.when(t + 1 < total)
            def _():
                use(t + 1, s1)

        return unused

    lax.fori_loop(0, (total + 1) // 2, body, 0)

    for h in range(heads if last else 0):
        u, span = h // merge, slice(h % merge * tokens, (h % merge + 1) * tokens)
        result = (acc_s[u][:, span] * (1.0 / l_s[u][:, span])).astype(jnp.bfloat16)
        out_ref[h] = lax.dot_general(
            wv_ref[h], result, (((0,), (0,)), ((), ())), preferred_element_type=jnp.float32
        ).astype(out_ref.dtype)


def attend(queries, key_blocks, mode, w_value, tokens, state=None, last=True):
    heads, depth, _ = queries.shape
    blocks, block_keys = len(key_blocks), key_blocks[0].shape[1]
    latent, value = w_value.shape[1:]
    merge = min(heads, max(1, 2 * LANES // tokens))
    units, columns = heads // merge, merge * tokens
    first = state is None

    def whole(*shape):
        return pl.BlockSpec(shape, lambda g, mode: (0,) * len(shape))

    states = [(units, 1, columns), (units, 1, columns), (units, latent, columns)]
    in_specs = [pl.BlockSpec((heads, depth, tokens), lambda g, mode: (0, 0, mode[blocks]))]
    in_specs += [pl.BlockSpec(memory_space=pl.ANY)] * blocks
    operands = [queries, *key_blocks]
    if not first:
        in_specs += [whole(*shape) for shape in states]
        operands += list(state)
    if last:
        in_specs.append(whole(heads, latent, value))
        operands.append(w_value)
        out_specs = whole(heads, value, tokens)
        out_shape = jax.ShapeDtypeStruct((heads, value, tokens), jnp.bfloat16)
    else:
        out_specs = [whole(*shape) for shape in states]
        out_shape = [jax.ShapeDtypeStruct(shape, jnp.float32) for shape in states]
    pairs = heads * tokens * blocks * block_keys
    made = pl.pallas_call(
        functools.partial(attend_kernel, blocks, merge, first, last),
        grid_spec=pltpu.PrefetchScalarGridSpec(
            num_scalar_prefetch=1,
            grid=(1,),
            in_specs=in_specs,
            out_specs=out_specs,
            scratch_shapes=([pltpu.VMEM(shape, jnp.float32) for shape in states] if last else [])
            + [
                pltpu.VMEM((units, depth, columns), jnp.bfloat16),
                pltpu.VMEM((depth, blocks * block_keys), jnp.bfloat16),
                pltpu.VMEM((blocks * block_keys, depth), jnp.bfloat16),
                pltpu.VMEM((SQUARE * block_keys, columns), jnp.float32),
                pltpu.VMEM((SQUARE * block_keys, columns), jnp.float32),
                pltpu.SemaphoreType.DMA((blocks,)),
            ],
        ),
        out_shape=out_shape,
        cost_estimate=pl.CostEstimate(
            flops=2 * pairs * (depth + latent),
            bytes_accessed=2 * blocks * block_keys * depth,
            transcendentals=pairs,
        ),
        compiler_params=pltpu.CompilerParams(vmem_limit_bytes=58 * 1024 * 1024),
    )(mode, *operands)
    return made.reshape(heads * value, tokens) if last else made


def expert_kernel(sources, batches, parts, slots, rank_ref, rank_t_ref, weight_ref, *refs):
    normed, refs = refs[: sources * batches], refs[sources * batches :]
    shards, refs = refs[: 3 * parts], refs[3 * parts :]
    kept, sent, row_buf, gate_buf, up_buf, down_buf, picked, total, row_sem, weight_sem = refs
    tokens = row_buf.shape[1]
    piece = tokens // batches
    bufs = (gate_buf, up_buf, down_buf)

    def row_copy(j, b):
        return pltpu.make_async_copy(
            normed[j * batches + b], row_buf.at[j, b * piece : (b + 1) * piece], row_sem.at[j, b]
        )

    def shard_copy(n):
        part, which = n // 3, n % 3
        return pltpu.make_async_copy(
            shards[n], bufs[which].at[part], weight_sem.at[part, which]
        )

    for j in range(sources):
        for b in range(batches):
            row_copy(j, b).start()
    early = 2
    for n in range(early):
        shard_copy(n).start()

    for j in range(sources):
        slot = lax.broadcasted_iota(jnp.int32, (slots, tokens), 0)
        place = (slot == rank_ref[j : j + 1, :]).astype(jnp.bfloat16)
        for b in range(batches):
            row_copy(j, b).wait()
        picked[j * slots : (j + 1) * slots, :] = jnp.dot(
            place, row_buf[j], preferred_element_type=jnp.float32
        ).astype(jnp.bfloat16)

    for n in range(early, 3 * parts):
        shard_copy(n).start()
    across = (((1,), (1,)), ((), ()))
    total[...] = jnp.zeros(total.shape, jnp.float32)

    def wait_for(part, which):
        pltpu.make_async_copy(
            shards[which], bufs[which].at[part], weight_sem.at[part, which]
        ).wait()

    def one_part(part, unused):
        rows = picked[...]
        wait_for(part, 0)
        gate = lax.dot_general(rows, gate_buf[part], across, preferred_element_type=jnp.float32)
        wait_for(part, 1)
        upward = lax.dot_general(rows, up_buf[part], across, preferred_element_type=jnp.float32)
        hidden = (gate / (1.0 + jnp.exp(-gate)) * upward).astype(jnp.bfloat16)
        wait_for(part, 2)
        total[...] += jnp.dot(hidden, down_buf[part], preferred_element_type=jnp.float32)
        return unused

    lax.fori_loop(0, parts, one_part, 0)

    for j in range(sources):
        slot = lax.broadcasted_iota(jnp.int32, (slots, tokens), 0)
        weight = jnp.sum(
            jnp.where(slot == rank_ref[j : j + 1, :], weight_ref[j : j + 1, :], 0.0),
            axis=1,
            keepdims=True,
        )
        scaled = (total[j * slots : (j + 1) * slots, :] * weight).astype(jnp.bfloat16)
        lane = lax.broadcasted_iota(jnp.int32, (tokens, slots), 1)
        back = (lane == rank_t_ref[:, j : j + 1]).astype(jnp.bfloat16)
        out_ref = kept if j < sources // 2 else sent
        out_ref[j % (sources // 2)] = jnp.dot(
            back, scaled, preferred_element_type=jnp.float32
        ).astype(jnp.bfloat16)


def experts(normed, shards, rank, weight, slots):
    sources, batches, parts = len(normed), len(normed[0]), len(shards)
    tokens = sum(piece.shape[0] for piece in normed[0])
    units, width = shards[0][0].shape
    flat = [array for shard in shards for array in shard]
    any_spec = pl.BlockSpec(memory_space=pl.ANY)
    vmem = pl.BlockSpec(memory_space=pltpu.VMEM)
    rows = sources * slots
    half = jax.ShapeDtypeStruct((sources // 2, tokens, width), jnp.bfloat16)
    return pl.pallas_call(
        functools.partial(expert_kernel, sources, batches, parts, slots),
        in_specs=[vmem] * 3 + [any_spec] * (sources * batches + len(flat)),
        out_specs=[vmem, vmem],
        out_shape=[half, half],
        scratch_shapes=[
            pltpu.VMEM((sources, tokens, width), jnp.bfloat16),
            pltpu.VMEM((parts, units, width), jnp.bfloat16),
            pltpu.VMEM((parts, units, width), jnp.bfloat16),
            pltpu.VMEM((parts, units, width), jnp.bfloat16),
            pltpu.VMEM((rows, width), jnp.bfloat16),
            pltpu.VMEM((rows, width), jnp.float32),
            pltpu.SemaphoreType.DMA((sources, batches)),
            pltpu.SemaphoreType.DMA((parts, 3)),
        ],
        cost_estimate=pl.CostEstimate(
            flops=6 * rows * width * units * parts,
            bytes_accessed=2 * (3 * parts * width * units + 2 * sources * tokens * width),
            transcendentals=rows * units * parts,
        ),
        compiler_params=pltpu.CompilerParams(vmem_limit_bytes=58 * 1024 * 1024),
    )(rank, rank.T, weight, *[piece for source in normed for piece in source], *flat)


def per_device(
    sizes,
    q_latent,
    kv_latent,
    w_value,
    w_out,
    resid,
    norm_gain,
    w_gate,
    w_up,
    w_down_t,
    expert_ids,
    route_scores,
):
    count, head_parts, group = sizes["ctx"], sizes["head"], sizes["head"] * sizes["ep"]
    tokens_here = q_latent.shape[0]
    rows, _ = resid.shape
    planes = count // SQUARE
    here = lax.axis_index("ctx")
    plane, spot = here // SQUARE, here % SQUARE

    def swap(value, bit):
        return lax.ppermute(value, "ctx", [(c, c ^ bit) for c in range(count)])

    def shift(value, by, wrap=True):
        pairs = []
        for c in range(count):
            to = c // SQUARE + by
            if wrap or 0 <= to < planes:
                pairs.append((c, to % planes * SQUARE + c % SQUARE))
        return lax.ppermute(value, "ctx", pairs)

    first = kv_latent.T
    key_blocks = []
    for by in range(planes):
        if by:
            first = shift(first, 1, wrap=False)
        across = swap(first, 2)
        beside = swap(first, 1)
        corner = swap(across, 1)
        key_blocks += [first, beside, across, corner]

    shards = [(w_gate[0].T, w_up[0].T, w_down_t[0].T)]
    for by in range(1, head_parts):
        pairs = [(i, (i + by) % head_parts) for i in range(head_parts)]
        shard = []
        for which in range(3):
            shard.append(lax.ppermute(shards[0][which], "head", pairs))
        shards.append(tuple(shard))

    combine = route_scores / jnp.sum(route_scores, axis=1, keepdims=True)
    table = jnp.concatenate([expert_ids.T.astype(jnp.float32), combine.T], axis=0)
    tables = lax.all_gather(table, "ctx", axis=0)

    queries = jnp.transpose(q_latent, (1, 2, 0))
    step = jnp.arange(SQUARE, dtype=jnp.int32)
    others = jnp.concatenate([(plane - by) * SQUARE + (spot ^ step) for by in range(planes)])
    far = jnp.int32(1 << 20)

    def mode_of(block, tokens, low, high):
        limit = jnp.where(others == here, block * tokens, jnp.where(others < here, far, -far))
        seen = jnp.clip(plane + 1 - low, 0, high - low)
        tail = jnp.stack([jnp.int32(block), seen])
        return jnp.concatenate([limit[low * SQUARE : high * SQUARE], tail]).astype(jnp.int32)

    def project(made):
        return lax.dot_general(
            made, w_out, (((0,), (0,)), ((), ())), preferred_element_type=jnp.float32
        )

    if group == 2 and rows % LANES == 0 and planes > 1:
        side = lax.axis_index("head") * sizes["ep"] + lax.axis_index("ep")
        halves = {"other": 1 - side, "own": side}
        near, distant = key_blocks[:SQUARE], key_blocks[SQUARE:]
        states = {
            which: attend(queries, near, mode_of(block, rows, 0, 1), w_value, rows, last=False)
            for which, block in halves.items()
        }

        def finish(which):
            mode = mode_of(halves[which], rows, 1, planes)
            return attend(queries, distant, mode, w_value, rows, states[which])

        partial = project(finish("other")).astype(jnp.bfloat16)
        came = lax.ppermute(partial, ("head", "ep"), [(0, 1), (1, 0)])
        attended = project(finish("own")) + came.astype(jnp.float32)
    else:
        made = [
            attend(queries, key_blocks, mode_of(b, LANES, 0, planes), w_value, LANES)
            for b in range(tokens_here // LANES)
        ]
        attended = lax.psum_scatter(
            project(jnp.concatenate(made, axis=1)),
            ("head", "ep"),
            scatter_dimension=0,
            tiled=True,
        )
    after_attn = lax.optimization_barrier(
        (resid.astype(jnp.float32) + attended).astype(jnp.bfloat16)
    )
    widened = after_attn.astype(jnp.float32)
    mean_square = jnp.mean(widened * widened, axis=1, keepdims=True)
    normed = (widened * lax.rsqrt(mean_square + norm_epsilon) * norm_gain).astype(jnp.bfloat16)

    arrived, first = [], normed
    for n in range(planes):
        if n:
            first = shift(first, 1)
        across = swap(first, 2)
        beside = swap(first, 1)
        corner = swap(across, 1)
        arrived.append([[first], [across], [beside], [corner]])

    capacity = 5 * rows * TOPK // (4 * count)
    slots = -(-capacity // 16) * 16
    named = tables[:, :TOPK, :] == here.astype(jnp.float32)
    chosen = jnp.any(named, axis=1)
    weight = jnp.sum(jnp.where(named, tables[:, TOPK:, :], 0.0), axis=1)
    before = jnp.arange(rows)[:, None] <= jnp.arange(rows)[None, :]
    ranking = jnp.dot(
        chosen.astype(jnp.bfloat16), before.astype(jnp.bfloat16), preferred_element_type=jnp.float32
    )
    rank = jnp.where(chosen, ranking - 1.0, -1.0).astype(jnp.int32)

    combined = None
    for n in range(planes):
        order = (plane - n) % planes * SQUARE + (spot ^ jnp.array([0, 2, 1, 3], jnp.int32))
        kept, sent = experts(arrived[n], shards, rank[order], weight[order], slots)
        other = swap(sent, 1)
        crossing = (kept[1].astype(jnp.float32) + other[1].astype(jnp.float32)).astype(jnp.bfloat16)
        crossing = swap(crossing, 2)
        summed = kept[0].astype(jnp.float32) + other[0].astype(jnp.float32) + crossing.astype(jnp.float32)
        if n:
            summed = shift(summed.astype(jnp.bfloat16), -n).astype(jnp.float32)
        combined = summed if combined is None else combined + summed
    return (widened + routed_factor * combined).astype(jnp.bfloat16)


def solution(mesh):
    placed = (
        P("ctx", ("head", "ep"), None),
        P("ctx", None),
        P(("head", "ep"), None, None),
        P(("head", "ep"), None),
        P(("ctx", "head", "ep"), None),
        P(),
        P("ctx", None, "head"),
        P("ctx", None, "head"),
        P("ctx", None, "head"),
        P(("ctx", "head", "ep"), None),
        P(("ctx", "head", "ep"), None),
    )

    def body(*arguments):
        return per_device(dict(mesh.shape), *arguments)

    return jax.shard_map(
        body,
        mesh=mesh,
        in_specs=placed,
        out_specs=P(("ctx", "head", "ep"), None),
        check_vma=False,
    )
```

time: 815 us -> 673 us (0.83)
  matrix products: 189 us -> 6.19 us
  Pallas kernels: 0 us -> 174 us
  waiting for transfers between devices: 471 us -> 356 us
  other arithmetic: 70.3 us -> 12.5 us
  blocking collectives: 0 us -> 52.5 us
  local copies, waits for them, and re-layouts: 45.1 us -> 12.2 us
  starting transfers between devices: 18.1 us -> 48.3 us
  between operations: 13.8 us -> 0.99 us
    ppermute x0 -> x45, waiting for transfers between devices: none -> 356 us  [the longest x1 157 us: per_device(): came = lax.ppermute(partial, ('head', 'ep'), [(0, 1), (1, 0)])]
    all_to_all x3 -> x0, waiting for transfers between devices: 276 us -> none  [the longest x1 171 us: per_device(): lax.all_to_all(outgoing, 'ctx', split_axis=0, concat_axis=0, tiled=True)]
    all_gather x5 -> x0, waiting for transfers between devices: 193 us -> none  [the longest x1 79.8 us: per_device(): keys = lax.all_gather(kv_latent, 'ctx', axis=0, tiled=True)]
    dot_general x7 -> x3, matrix products: 189 us -> 6.19 us  [the longest x2 6.04 us: project(): lax.dot_general(made, w_out, (((0,), (0,)), ((), ())), preferred_element_...]
    pallas_call x0 -> x8, Pallas kernels: none -> 174 us  [the longest x4 90.2 us: attend(): pl.pallas_call(functools.partial(attend_kernel, blocks, merge, first, las...]
    reduce_sum x3 -> x1, other arithmetic: 56.2 us -> 0.07 us  [per_device(): weight = jnp.sum(jnp.where(named, tables[:, TOPK:, :], 0.0), axis=1)]
    all_gather x0 -> x1, blocking collectives: none -> 52.5 us  [per_device(): tables = lax.all_gather(table, 'ctx', axis=0)]
    ppermute x0 -> x45, starting transfers between devices: none -> 48.3 us  [the longest x32 29.5 us: swap(): return lax.ppermute(value, 'ctx', [(c, c ^ bit) for c in range(count)])]
  transfers between devices with their start and end apart: 8 -> 45, of which waited for: 6 -> 11; matrix products, arithmetic and copies ran while one was open for 27% -> 4% of each run, Pallas kernels for 0% -> 26%
where the time goes in v1:
time: 673 us; the launch traced here: 663 us
  waiting for transfers between devices  356 us (53%)
  Pallas kernels  174 us (26%)
  blocking collectives  52.5 us (8%)
  starting transfers between devices  48.3 us (7%)
  other arithmetic  12.5 us (2%)
  local copies, waits for them, and re-layouts  12.2 us (2%)
    ppermute x1, waiting for transfers between devices, per_device(): came = lax.ppermute(partial, ('head', 'ep'), [(0, 1), (1, 0)])  157 us
    ppermute x9, waiting for transfers between devices, shift(): return lax.ppermute(value, 'ctx', pairs)  116 us
    pallas_call x4, Pallas kernels, attend(): pl.pallas_call(functools.partial(attend_kernel, blocks, merge, first, las...  90.2 us
    pallas_call x4, Pallas kernels, experts(): pl.pallas_call(functools.partial(expert_kernel, sources, batches, parts,...  83.7 us
    ppermute x32, waiting for transfers between devices, swap(): return lax.ppermute(value, 'ctx', [(c, c ^ bit) for c in range(count)])  82.8 us
    all_gather x1, blocking collectives, per_device(): tables = lax.all_gather(table, 'ctx', axis=0)  52.5 us
    ppermute x32, starting transfers between devices, swap(): return lax.ppermute(value, 'ctx', [(c, c ^ bit) for c in range(count)])  29.5 us
    ppermute x9, starting transfers between devices, shift(): return lax.ppermute(value, 'ctx', pairs)  15.8 us
  transfers between devices with their start and end apart: 45, of which 11 were waited for; matrix products, arithmetic and copies ran while one was open for 4% of the time, Pallas kernels for 26%

profile of v1, /device:TPU:11, one launch (start us, length us, event | category | flops | bytes accessed | tf_op | source)
XLA Modules:
  0.0 663.0 jit_solution(15578331146109893167)
XLA Ops:
  0.0 3.2 collective-permute-start
  3.5 12.8 %collective-permute-done.refs_0_ = bf16[576,512]{1,0:T(8,128)(2,1)S(1)} collective-permute-done((bf16[576,512]{1,0:T(8,128)(2,1)}, bf16[576,512]{1,0:T(8,128)(2,1)S(1)}, u32[]{:S(2)}, u32[]{:S(2)}) %collective-permute-start) | collective-permute-done | bytes 589856 | tf_op jit(solution)/shard_map/ppermute | solution.py:363
  16.3 3.2 collective-permute-start.4
  19.5 1.9 collective-permute-start.12
  21.4 0.7 compare_select_fusion.3
  22.8 8.7 %collective-permute-done.4.refs_4_ = bf16[576,512]{1,0:T(8,128)(2,1)S(1)} collective-permute-done((bf16[576,512]{1,0:T(8,128)(2,1)S(1)}, bf16[576,512]{1,0:T(8,128)(2,1)S(1)}, u32[]{:S(2)}, u32[]{:S(2)}) %collective-permute-start.4) | collective-permute-done | bytes 589856 | tf_op jit(solution)/shard_map/ppermute | solution.py:363
  31.6 3.2 collective-permute-start.8
  34.9 0.6 add_add_fusion.mode_ref
  35.6 0.6 add_add_fusion.1.mode_ref
  36.1 0.6 add_add_fusion.2.mode_ref
  36.8 0.6 add_add_fusion.3.mode_ref
  37.4 2.7 collective-permute-start.1
  40.4 0.7 collective-permute-start.3
  41.1 5.0 collective-permute-done.8.refs_8_
  46.3 21.6 %shard_map.145 = (f32[8,1,256]{2,1,0:T(1,128)}, f32[8,1,256]{2,1,0:T(1,128)}, f32[8,512,256]{2,1,0:T(8,128)}) custom-call(s32[6]{0:T(128)} %add_add_fusion.1.mode_ref, bf16[8,576,512]{2,1,0:T(8,128)(2,1)} %bitcast.73, bf16[576,512]{1,0:T(8,128)(2,1)} %bitcast.80, bf16[576,512]{1,0:T(8,128)(2,1)} %copy-done.18, bf16[576,512]{1,0:T(8,128)(2,1)} %copy-done.17, ...), custom_call_target="tpu_custom_call" | custom-call | flops 9126805504 | bytes 2359296 | tf_op jit(solution)/shard_map/pallas_call | solution.py:198
  67.9 3.6 collective-permute-start.9
  72.0 21.8 %shard_map.147 = (f32[8,1,256]{2,1,0:T(1,128)}, f32[8,1,256]{2,1,0:T(1,128)}, f32[8,512,256]{2,1,0:T(8,128)}) custom-call(s32[6]{0:T(128)} %add_add_fusion.3.mode_ref, bf16[8,576,512]{2,1,0:T(8,128)(2,1)} %bitcast.74, bf16[576,512]{1,0:T(8,128)(2,1)} %bitcast.81, bf16[576,512]{1,0:T(8,128)(2,1)} %copy-done.18, bf16[576,512]{1,0:T(8,128)(2,1)} %copy-done.17, ...), custom_call_target="tpu_custom_call" | custom-call | flops 9126805504 | bytes 2359296 | tf_op jit(solution)/shard_map/pallas_call | solution.py:198
  93.9 1.3 collective-permute-start.19
  95.4 1.2 collective-permute-start.21
  96.7 0.8 copy-done.26
  97.7 23.4 %shard_map.148 = bf16[8,128,256]{2,1,0:T(8,128)(2,1)} custom-call(s32[14]{0:T(128)} %add_add_fusion.2.mode_ref, bf16[8,576,512]{2,1,0:T(8,128)(2,1)} %bitcast.75, bf16[576,512]{1,0:T(8,128)(2,1)} %copy-done.15, bf16[576,512]{1,0:T(8,128)(2,1)} %copy-done.20, bf16[576,512]{1,0:T(8,128)(2,1)} %copy-done.19, bf16[576,512]{1,0:T(8,128)(2,1)} %copy-done.23, ...), custom_call_target="tpu_custom_call" | custom-call | flops 27380416512 | bytes 7077888 | tf_op jit(solution)/shard_map/pallas_call | solution.py:198
  121.2 2.3 convolution_convert_fusion
  123.8 23.4 %shard_map.146 = bf16[8,128,256]{2,1,0:T(8,128)(2,1)} custom-call(s32[14]{0:T(128)} %add_add_fusion.mode_ref, bf16[8,576,512]{2,1,0:T(8,128)(2,1)} %bitcast.76, bf16[576,512]{1,0:T(8,128)(2,1)} %copy-done.15, bf16[576,512]{1,0:T(8,128)(2,1)} %copy-done.20, bf16[576,512]{1,0:T(8,128)(2,1)} %copy-done.19, bf16[576,512]{1,0:T(8,128)(2,1)} %copy-done.23, ...), custom_call_target="tpu_custom_call" | custom-call | flops 27380416512 | bytes 7077888 | tf_op jit(solution)/shard_map/pallas_call | solution.py:198
  147.2 157.0 %collective-permute-done.15 = bf16[256,2048]{1,0:T(8,128)(2,1)S(1)} collective-permute-done((bf16[256,2048]{1,0:T(8,128)(2,1)S(1)}, bf16[256,2048]{1,0:T(8,128)(2,1)S(1)}, u32[]{:S(2)}, u32[]{:S(2)}) %collective-permute-start.15) | collective-permute-done | bytes 1048608 | tf_op jit(solution)/shard_map/ppermute | solution.py:417
  304.2 3.7 fusion.1
  308.6 1.4 collective-permute-start.24
  309.9 22.6 %collective-permute-done.24.refs_0_ = bf16[256,2048]{1,0:T(8,128)(2,1)} collective-permute-done((bf16[256,2048]{1,0:T(8,128)(2,1)S(1)}, bf16[256,2048]{1,0:T(8,128)(2,1)}, u32[]{:S(2)}, u32[]{:S(2)}) %collective-permute-start.24) | collective-permute-done | bytes 1048608 | tf_op jit(solution)/shard_map/ppermute | solution.py:363
  332.5 1.3 collective-permute-start.31
  333.8 1.2 collective-permute-start.16
  335.1 2.4 collective-permute-start.17
  337.8 19.4 %collective-permute-done.31.refs_0_ = bf16[256,2048]{1,0:T(8,128)(2,1)} collective-permute-done((bf16[256,2048]{1,0:T(8,128)(2,1)}, bf16[256,2048]{1,0:T(8,128)(2,1)}, u32[]{:S(2)}, u32[]{:S(2)}) %collective-permute-start.31) | collective-permute-done | bytes 1048608 | tf_op jit(solution)/shard_map/ppermute | solution.py:363
  357.2 4.9 collective-permute-start.18
  362.0 1.2 collective-permute-start.32
  363.3 52.5 %all-gather.1 = f32[16,12,256]{2,1,0:T(8,128)S(1)} all-gather(f32[1,12,256]{2,1,0:T(8,128)S(1)} %maximum_bitcast_fusion), channel_id=2, replica_groups=mesh['ctx'=16,'head'=2,'ep'=1] {'ctx'}, dimensions={0}, use_global_device_ids=true | all-gather | bytes 208896 | tf_op jit(solution)/shard_map/all_gather | solution.py:385
  416.0 0.6 gather_fusion.6
  416.6 1.1 gather_fusion.7
  417.8 0.6 gather_fusion.4
  418.3 1.1 gather_fusion.5
  420.0 2.6 collective-permute-start.39
  422.6 0.6 gather_fusion.2
  423.2 1.1 gather_fusion.3
  424.3 0.6 gather_fusion
  424.9 1.1 gather_fusion.1
  426.1 0.8 copy.23
  426.9 0.8 copy.22
  427.6 0.8 copy.21
  428.4 0.8 copy.20
  429.8 20.9 %shard_map.149 = (bf16[2,256,2048]{2,1,0:T(8,128)(2,1)}, bf16[2,256,2048]{2,1,0:T(8,128)(2,1)}) custom-call(s32[4,256]{1,0:T(4,128)} %copy-done.11, s32[256,4]{1,0:T(8,128)} %bitcast.70, f32[4,256]{1,0:T(4,128)} %gather_fusion.1, bf16[256,2048]{1,0:T(8,128)(2,1)} %copy-done.5, bf16[256,2048]{1,0:T(8,128)(2,1)} %collective-permute-done.16.refs_1_, ...), custom_call_target="tpu_custom_call" | custom-call | flops 8858370048 | bytes 25690112 | tf_op jit(solution)/shard_map/pallas_call | solution.py:309
  451.8 21.0 %shard_map.150 = (bf16[2,256,2048]{2,1,0:T(8,128)(2,1)}, bf16[2,256,2048]{2,1,0:T(8,128)(2,1)}) custom-call(s32[4,256]{1,0:T(4,128)} %copy-done.10, s32[256,4]{1,0:T(8,128)} %bitcast.69, f32[4,256]{1,0:T(4,128)} %gather_fusion.3, bf16[256,2048]{1,0:T(8,128)(2,1)} %collective-permute-done.24.refs_0_, bf16[256,2048]{1,0:T(8,128)(2,1)} %collective-permute-done.25.refs_1_, ...), custom_call_target="tpu_custom_call" | custom-call | flops 8858370048 | bytes 25690112 | tf_op jit(solution)/shard_map/pallas_call | solution.py:309
  472.8 1.0 copy-done.14
  473.9 20.8 %shard_map.151 = (bf16[2,256,2048]{2,1,0:T(8,128)(2,1)}, bf16[2,256,2048]{2,1,0:T(8,128)(2,1)}) custom-call(s32[4,256]{1,0:T(4,128)} %copy-done.9, s32[256,4]{1,0:T(8,128)} %bitcast.68, f32[4,256]{1,0:T(4,128)} %gather_fusion.5, bf16[256,2048]{1,0:T(8,128)(2,1)} %collective-permute-done.31.refs_0_, bf16[256,2048]{1,0:T(8,128)(2,1)} %collective-permute-done.32.refs_1_, ...), custom_call_target="tpu_custom_call" | custom-call | flops 8858370048 | bytes 25690112 | tf_op jit(solution)/shard_map/pallas_call | solution.py:309
  495.1 21.1 %shard_map.152 = (bf16[2,256,2048]{2,1,0:T(8,128)(2,1)}, bf16[2,256,2048]{2,1,0:T(8,128)(2,1)}) custom-call(s32[4,256]{1,0:T(4,128)} %copy-done.8, s32[256,4]{1,0:T(8,128)} %bitcast.67, f32[4,256]{1,0:T(4,128)} %gather_fusion.7, bf16[256,2048]{1,0:T(8,128)(2,1)} %collective-permute-done.38.refs_0_, bf16[256,2048]{1,0:T(8,128)(2,1)} %collective-permute-done.39.refs_1_, ...), custom_call_target="tpu_custom_call" | custom-call | flops 8858370048 | bytes 25690112 | tf_op jit(solution)/shard_map/pallas_call | solution.py:309
  516.4 2.0 fusion.15
  519.0 1.5 collective-permute-start.29
  521.4 1.5 collective-permute-start.43
  522.8 42.4 %collective-permute-done.29 = bf16[256,2048]{1,0:T(8,128)(2,1)S(1)} collective-permute-done((bf16[256,2048]{1,0:T(8,128)(2,1)S(1)}, bf16[256,2048]{1,0:T(8,128)(2,1)S(1)}, u32[]{:S(2)}, u32[]{:S(2)}) %collective-permute-start.29) | collective-permute-done | bytes 1048608 | tf_op jit(solution)/shard_map/ppermute | solution.py:355
  565.8 3.0 collective-permute-start.30
  568.8 18.9 %collective-permute-done.36 = bf16[256,2048]{1,0:T(8,128)(2,1)S(1)} collective-permute-done((bf16[256,2048]{1,0:T(8,128)(2,1)S(1)}, bf16[256,2048]{1,0:T(8,128)(2,1)S(1)}, u32[]{:S(2)}, u32[]{:S(2)}) %collective-permute-start.36) | collective-permute-done | bytes 1048608 | tf_op jit(solution)/shard_map/ppermute | solution.py:355
  587.7 0.5 fusion.7
  588.7 21.4 %collective-permute-done.43 = bf16[256,2048]{1,0:T(8,128)(2,1)S(1)} collective-permute-done((bf16[256,2048]{1,0:T(8,128)(2,1)S(1)}, bf16[256,2048]{1,0:T(8,128)(2,1)S(1)}, u32[]{:S(2)}, u32[]{:S(2)}) %collective-permute-start.43) | collective-permute-done | bytes 1048608 | tf_op jit(solution)/shard_map/ppermute | solution.py:355
  610.2 0.6 fusion.6
  610.8 25.6 %collective-permute-done.37 = bf16[256,2048]{1,0:T(8,128)(2,1)S(1)} collective-permute-done((bf16[256,2048]{1,0:T(8,128)(2,1)S(1)}, bf16[256,2048]{1,0:T(8,128)(2,1)S(1)}, u32[]{:S(2)}, u32[]{:S(2)}) %collective-permute-start.37) | collective-permute-done | bytes 1048608 | tf_op jit(solution)/shard_map/ppermute | solution.py:363
  636.4 22.5 %collective-permute-done.44 = bf16[256,2048]{1,0:T(8,128)(2,1)S(1)} collective-permute-done((bf16[256,2048]{1,0:T(8,128)(2,1)S(1)}, bf16[256,2048]{1,0:T(8,128)(2,1)S(1)}, u32[]{:S(2)}, u32[]{:S(2)}) %collective-permute-start.44) | collective-permute-done | bytes 1048608 | tf_op jit(solution)/shard_map/ppermute | solution.py:363
  658.9 3.7 fusion.5
  (136 shorter events, 9.7 us)
Async XLA Ops:
  0.0 16.3 %collective-permute-start = (bf16[576,512]{1,0:T(8,128)(2,1)}, bf16[576,512]{1,0:T(8,128)(2,1)S(1)}, u32[]{:S(2)}, u32[]{:S(2)}) collective-permute-start(bf16[576,512]{1,0:T(8,128)(2,1)} %bitcast.77), channel_id=1, source_target_pairs={{0,8},{2,10},{4,12},{6,14},{8,16},{10,18},{12,20},{14,22},{16,24},... | collective-permute-start | bytes 1769480 | tf_op jit(solution)/shard_map/ppermute | solution.py:363
  3.2 19.2 %collective-permute-start.13 = (bf16[576,512]{1,0:T(8,128)(2,1)}, bf16[576,512]{1,0:T(8,128)(2,1)S(1)}, u32[]{:S(2)}, u32[]{:S(2)}) collective-permute-start(bf16[576,512]{1,0:T(8,128)(2,1)} %bitcast.78), channel_id=1, source_target_pairs={{0,4},{2,6},{4,0},{6,2},{8,12},{10,14},{12,8},{14,10},{16,20},{18,... | collective-permute-start | bytes 1769480 | tf_op jit(solution)/shard_map/ppermute | solution.py:355
  16.3 51.6 %copy-start.15 = (bf16[576,512]{1,0:T(8,128)(2,1)}, bf16[576,512]{1,0:T(8,128)(2,1)S(1)}, u32[]{:S(2)}) copy-start(bf16[576,512]{1,0:T(8,128)(2,1)S(1)} %collective-permute-done.refs_0_) | copy-start | bytes 1769476
  16.3 15.2 %collective-permute-start.4 = (bf16[576,512]{1,0:T(8,128)(2,1)S(1)}, bf16[576,512]{1,0:T(8,128)(2,1)S(1)}, u32[]{:S(2)}, u32[]{:S(2)}) collective-permute-start(bf16[576,512]{1,0:T(8,128)(2,1)S(1)} %collective-permute-done.refs_0_), channel_id=1, source_target_pairs={{0,8},{2,10},{4,12},{6,14},{8,16},{10,18},{12,20},{14,22},{16,24},... | collective-permute-start | bytes 1769480 | tf_op jit(solution)/shard_map/ppermute | solution.py:363
  19.5 20.5 %collective-permute-start.12 = (bf16[576,512]{1,0:T(8,128)(2,1)}, bf16[576,512]{1,0:T(8,128)(2,1)S(1)}, u32[]{:S(2)}, u32[]{:S(2)}) collective-permute-start(bf16[576,512]{1,0:T(8,128)(2,1)} %bitcast.79), channel_id=1, source_target_pairs={{0,2},{2,0},{4,6},{6,4},{8,10},{10,8},{12,14},{14,12},{16,18},{18,... | collective-permute-start | bytes 1769480 | tf_op jit(solution)/shard_map/ppermute | solution.py:355
  22.1 18.0 %collective-permute-start.2 = (bf16[576,512]{1,0:T(8,128)(2,1)S(1)}, bf16[576,512]{1,0:T(8,128)(2,1)S(1)}, u32[]{:S(2)}, u32[]{:S(2)}) collective-permute-start(bf16[576,512]{1,0:T(8,128)(2,1)S(1)} %collective-permute-done.refs_0_), channel_id=1, source_target_pairs={{0,4},{2,6},{4,0},{6,2},{8,12},{10,14},{12,8},{14,10},{16,20},{18,... | collective-permute-start | bytes 1769480 | tf_op jit(solution)/shard_map/ppermute | solution.py:355
  22.4 23.9 %copy-start.17 = (bf16[576,512]{1,0:T(8,128)(2,1)}, bf16[576,512]{1,0:T(8,128)(2,1)S(1)}, u32[]{:S(2)}) copy-start(bf16[576,512]{1,0:T(8,128)(2,1)S(1)} %collective-permute-done.13.refs_2_) | copy-start | bytes 1769476
  22.4 18.0 %collective-permute-start.14 = (bf16[576,512]{1,0:T(8,128)(2,1)S(1)}, bf16[576,512]{1,0:T(8,128)(2,1)}, u32[]{:S(2)}, u32[]{:S(2)}) collective-permute-start(bf16[576,512]{1,0:T(8,128)(2,1)S(1)} %collective-permute-done.13.refs_2_), channel_id=1, source_target_pairs={{0,2},{2,0},{4,6},{6,4},{8,10},{10,8},{12,14},{14,12},{16,18},{18,... | collective-permute-start | bytes 1769480 | tf_op jit(solution)/shard_map/ppermute | solution.py:355
  31.5 36.3 %copy-start.16 = (bf16[576,512]{1,0:T(8,128)(2,1)}, bf16[576,512]{1,0:T(8,128)(2,1)S(1)}, u32[]{:S(2)}) copy-start(bf16[576,512]{1,0:T(8,128)(2,1)S(1)} %collective-permute-done.4.refs_4_) | copy-start | bytes 1769476
  31.6 14.5 %collective-permute-start.8 = (bf16[576,512]{1,0:T(8,128)(2,1)S(1)}, bf16[576,512]{1,0:T(8,128)(2,1)}, u32[]{:S(2)}, u32[]{:S(2)}) collective-permute-start(bf16[576,512]{1,0:T(8,128)(2,1)S(1)} %collective-permute-done.4.refs_4_), channel_id=1, source_target_pairs={{0,8},{2,10},{4,12},{6,14},{8,16},{10,18},{12,20},{14,22},{16,24},... | collective-permute-start | bytes 1769480 | tf_op jit(solution)/shard_map/ppermute | solution.py:363
  37.4 30.6 %collective-permute-start.1 = (bf16[576,512]{1,0:T(8,128)(2,1)S(1)}, bf16[576,512]{1,0:T(8,128)(2,1)S(1)}, u32[]{:S(2)}, u32[]{:S(2)}) collective-permute-start(bf16[576,512]{1,0:T(8,128)(2,1)S(1)} %collective-permute-done.refs_0_), channel_id=1, source_target_pairs={{0,2},{2,0},{4,6},{6,4},{8,10},{10,8},{12,14},{14,12},{16,18},{18,... | collective-permute-start | bytes 1769480 | tf_op jit(solution)/shard_map/ppermute | solution.py:355
  40.0 6.3 copy-start.18
  40.0 55.2 %collective-permute-start.5 = (bf16[576,512]{1,0:T(8,128)(2,1)S(1)}, bf16[576,512]{1,0:T(8,128)(2,1)S(1)}, u32[]{:S(2)}, u32[]{:S(2)}) collective-permute-start(bf16[576,512]{1,0:T(8,128)(2,1)S(1)} %collective-permute-done.4.refs_4_), channel_id=1, source_target_pairs={{0,2},{2,0},{4,6},{6,4},{8,10},{10,8},{12,14},{14,12},{16,18},{18,... | collective-permute-start | bytes 1769480 | tf_op jit(solution)/shard_map/ppermute | solution.py:355
  40.1 27.8 %copy-start.19 = (bf16[576,512]{1,0:T(8,128)(2,1)}, bf16[576,512]{1,0:T(8,128)(2,1)S(1)}, u32[]{:S(2)}) copy-start(bf16[576,512]{1,0:T(8,128)(2,1)S(1)} %collective-permute-done.2.refs_2_) | copy-start | bytes 1769476
  40.1 31.4 %collective-permute-start.6 = (bf16[576,512]{1,0:T(8,128)(2,1)S(1)}, bf16[576,512]{1,0:T(8,128)(2,1)S(1)}, u32[]{:S(2)}, u32[]{:S(2)}) collective-permute-start(bf16[576,512]{1,0:T(8,128)(2,1)S(1)} %collective-permute-done.4.refs_4_), channel_id=1, source_target_pairs={{0,4},{2,6},{4,0},{6,2},{8,12},{10,14},{12,8},{14,10},{16,20},{18,... | collective-permute-start | bytes 1769480 | tf_op jit(solution)/shard_map/ppermute | solution.py:355
  40.4 53.5 %collective-permute-start.3 = (bf16[576,512]{1,0:T(8,128)(2,1)S(1)}, bf16[576,512]{1,0:T(8,128)(2,1)S(1)}, u32[]{:S(2)}, u32[]{:S(2)}) collective-permute-start(bf16[576,512]{1,0:T(8,128)(2,1)S(1)} %collective-permute-done.2.refs_2_), channel_id=1, source_target_pairs={{0,2},{2,0},{4,6},{6,4},{8,10},{10,8},{12,14},{14,12},{16,18},{18,... | collective-permute-start | bytes 1769480 | tf_op jit(solution)/shard_map/ppermute | solution.py:355
  46.0 25.6 %collective-permute-start.10 = (bf16[576,512]{1,0:T(8,128)(2,1)}, bf16[576,512]{1,0:T(8,128)(2,1)}, u32[]{:S(2)}, u32[]{:S(2)}) collective-permute-start(bf16[576,512]{1,0:T(8,128)(2,1)} %collective-permute-done.8.refs_8_), channel_id=1, source_target_pairs={{0,4},{2,6},{4,0},{6,2},{8,12},{10,14},{12,8},{14,10},{16,20},{18,... | collective-permute-start | bytes 1769480 | tf_op jit(solution)/shard_map/ppermute | solution.py:355
  67.9 25.9 %copy-start.20 = (bf16[576,512]{1,0:T(8,128)(2,1)}, bf16[576,512]{1,0:T(8,128)(2,1)S(1)}, u32[]{:S(2)}) copy-start(bf16[576,512]{1,0:T(8,128)(2,1)S(1)} %collective-permute-done.1.refs_1_) | copy-start | bytes 1769476
  67.9 28.7 %collective-permute-start.9 = (bf16[576,512]{1,0:T(8,128)(2,1)}, bf16[576,512]{1,0:T(8,128)(2,1)S(1)}, u32[]{:S(2)}, u32[]{:S(2)}) collective-permute-start(bf16[576,512]{1,0:T(8,128)(2,1)} %collective-permute-done.8.refs_8_), channel_id=1, source_target_pairs={{0,2},{2,0},{4,6},{6,4},{8,10},{10,8},{12,14},{14,12},{16,18},{18,... | collective-permute-start | bytes 1769480 | tf_op jit(solution)/shard_map/ppermute | solution.py:355
  71.5 22.3 %copy-start.22 = (bf16[576,512]{1,0:T(8,128)(2,1)}, bf16[576,512]{1,0:T(8,128)(2,1)S(1)}, u32[]{:S(2)}) copy-start(bf16[576,512]{1,0:T(8,128)(2,1)S(1)} %collective-permute-done.6.refs_6_) | copy-start | bytes 1769476
  71.5 23.9 %collective-permute-start.7 = (bf16[576,512]{1,0:T(8,128)(2,1)S(1)}, bf16[576,512]{1,0:T(8,128)(2,1)S(1)}, u32[]{:S(2)}, u32[]{:S(2)}) collective-permute-start(bf16[576,512]{1,0:T(8,128)(2,1)S(1)} %collective-permute-done.6.refs_6_), channel_id=1, source_target_pairs={{0,2},{2,0},{4,6},{6,4},{8,10},{10,8},{12,14},{14,12},{16,18},{18,... | collective-permute-start | bytes 1769480 | tf_op jit(solution)/shard_map/ppermute | solution.py:355
  71.6 25.1 %collective-permute-start.11 = (bf16[576,512]{1,0:T(8,128)(2,1)}, bf16[576,512]{1,0:T(8,128)(2,1)S(1)}, u32[]{:S(2)}, u32[]{:S(2)}) collective-permute-start(bf16[576,512]{1,0:T(8,128)(2,1)} %collective-permute-done.10.refs_10_), channel_id=1, source_target_pairs={{0,2},{2,0},{4,6},{6,4},{8,10},{10,8},{12,14},{14,12},{16,18},{18,... | collective-permute-start | bytes 1769480 | tf_op jit(solution)/shard_map/ppermute | solution.py:355
  93.9 2.8 copy-start.23
  93.9 241.2 %collective-permute-start.19 = (bf16[704,2048]{1,0:T(8,128)(2,1)}, bf16[704,2048]{1,0:T(8,128)(2,1)}, u32[]{:S(2)}, u32[]{:S(2)}) collective-permute-start(bf16[704,2048]{1,0:T(8,128)(2,1)} %bitcast.13.refs_4_), channel_id=1, source_target_pairs={{0,1},{1,0},{2,3},{3,2},{4,5},{5,4},{6,7},{7,6},{8,9},{9,8},{10,11... | collective-permute-start | bytes 8650760 | tf_op jit(solution)/shard_map/ppermute | solution.py:380
  95.2 242.3 %collective-permute-start.20 = (bf16[704,2048]{1,0:T(8,128)(2,1)}, bf16[704,2048]{1,0:T(8,128)(2,1)}, u32[]{:S(2)}, u32[]{:S(2)}) collective-permute-start(bf16[704,2048]{1,0:T(8,128)(2,1)} %bitcast.15.refs_5_), channel_id=1, source_target_pairs={{0,1},{1,0},{2,3},{3,2},{4,5},{5,4},{6,7},{7,6},{8,9},{9,8},{10,11... | collective-permute-start | bytes 8650760 | tf_op jit(solution)/shard_map/ppermute | solution.py:380
  95.4 266.6 %collective-permute-start.21 = (bf16[704,2048]{1,0:T(8,128)(2,1)}, bf16[704,2048]{1,0:T(8,128)(2,1)}, u32[]{:S(2)}, u32[]{:S(2)}) collective-permute-start(bf16[704,2048]{1,0:T(8,128)(2,1)} %bitcast.17.refs_6_), channel_id=1, source_target_pairs={{0,1},{1,0},{2,3},{3,2},{4,5},{5,4},{6,7},{7,6},{8,9},{9,8},{10,11... | collective-permute-start | bytes 8650760 | tf_op jit(solution)/shard_map/ppermute | solution.py:380
  97.7 23.4 %copy-start = (bf16[1024,2048]{1,0:T(8,128)(2,1)S(1)}, bf16[1024,2048]{1,0:T(8,128)(2,1)}, u32[]{:S(2)}) copy-start(bf16[1024,2048]{1,0:T(8,128)(2,1)} %param.18) | copy-start | bytes 12582916
  123.5 180.7 %collective-permute-start.15 = (bf16[256,2048]{1,0:T(8,128)(2,1)S(1)}, bf16[256,2048]{1,0:T(8,128)(2,1)S(1)}, u32[]{:S(2)}, u32[]{:S(2)}) collective-permute-start(bf16[256,2048]{1,0:T(8,128)(2,1)S(1)} %convolution_convert_fusion), channel_id=1, source_target_pairs={{0,1},{1,0},{2,3},{3,2},{4,5},{5,4},{6,7},{7,6},{8,9},{9,8},{10,11... | collective-permute-start | bytes 3145736 | tf_op jit(solution)/shard_map/ppermute | solution.py:417
  123.8 180.4 %copy-start.6 = (bf16[256,2048]{1,0:T(8,128)(2,1)S(1)}, bf16[256,2048]{1,0:T(8,128)(2,1)}, u32[]{:S(2)}) copy-start(bf16[256,2048]{1,0:T(8,128)(2,1)} %param.19) | copy-start | bytes 3145732
  304.2 4.1 copy-start.12
  307.9 27.1 %copy-start.7 = (f32[256,6]{0,1:T(8,128)S(1)}, f32[256,6]{0,1:T(8,128)}, u32[]{:S(2)}) copy-start(f32[256,6]{0,1:T(8,128)} %param.25) | copy-start | bytes 18436
  307.9 49.2 %copy-start.13 = (s32[256,6]{0,1:T(8,128)S(1)}, s32[256,6]{0,1:T(8,128)}, u32[]{:S(2)}) copy-start(s32[256,6]{0,1:T(8,128)} %param.24) | copy-start | bytes 18436
  308.6 121.2 %copy-start.5 = (bf16[256,2048]{1,0:T(8,128)(2,1)}, bf16[256,2048]{1,0:T(8,128)(2,1)S(1)}, u32[]{:S(2)}) copy-start(bf16[256,2048]{1,0:T(8,128)(2,1)S(1)} %fusion.4.refs_0_) | copy-start | bytes 3145732
  308.6 23.9 %collective-permute-start.24 = (bf16[256,2048]{1,0:T(8,128)(2,1)S(1)}, bf16[256,2048]{1,0:T(8,128)(2,1)}, u32[]{:S(2)}, u32[]{:S(2)}) collective-permute-start(bf16[256,2048]{1,0:T(8,128)(2,1)S(1)} %fusion.4.refs_0_), channel_id=1, source_target_pairs={{0,8},{2,10},{4,12},{6,14},{8,16},{10,18},{12,20},{14,22},{16,24},... | collective-permute-start | bytes 3145736 | tf_op jit(solution)/shard_map/ppermute | solution.py:363
  332.5 24.6 %collective-permute-start.31 = (bf16[256,2048]{1,0:T(8,128)(2,1)}, bf16[256,2048]{1,0:T(8,128)(2,1)}, u32[]{:S(2)}, u32[]{:S(2)}) collective-permute-start(bf16[256,2048]{1,0:T(8,128)(2,1)} %collective-permute-done.24.refs_0_), channel_id=1, source_target_pairs={{0,8},{2,10},{4,12},{6,14},{8,16},{10,18},{12,20},{14,22},{16,24},... | collective-permute-start | bytes 3145736 | tf_op jit(solution)/shard_map/ppermute | solution.py:363
  333.8 23.4 %collective-permute-start.16 = (bf16[256,2048]{1,0:T(8,128)(2,1)S(1)}, bf16[256,2048]{1,0:T(8,128)(2,1)}, u32[]{:S(2)}, u32[]{:S(2)}) collective-permute-start(bf16[256,2048]{1,0:T(8,128)(2,1)S(1)} %fusion.4.refs_0_), channel_id=1, source_target_pairs={{0,4},{2,6},{4,0},{6,2},{8,12},{10,14},{12,8},{14,10},{16,20},{18,... | collective-permute-start | bytes 3145736 | tf_op jit(solution)/shard_map/ppermute | solution.py:355
  335.1 84.4 %collective-permute-start.17 = (bf16[256,2048]{1,0:T(8,128)(2,1)S(1)}, bf16[256,2048]{1,0:T(8,128)(2,1)}, u32[]{:S(2)}, u32[]{:S(2)}) collective-permute-start(bf16[256,2048]{1,0:T(8,128)(2,1)S(1)} %fusion.4.refs_0_), channel_id=1, source_target_pairs={{0,2},{2,0},{4,6},{6,4},{8,10},{10,8},{12,14},{14,12},{16,18},{18,... | collective-permute-start | bytes 3145736 | tf_op jit(solution)/shard_map/ppermute | solution.py:355
  337.5 82.1 %collective-permute-start.25 = (bf16[256,2048]{1,0:T(8,128)(2,1)}, bf16[256,2048]{1,0:T(8,128)(2,1)}, u32[]{:S(2)}, u32[]{:S(2)}) collective-permute-start(bf16[256,2048]{1,0:T(8,128)(2,1)} %collective-permute-done.24.refs_0_), channel_id=1, source_target_pairs={{0,4},{2,6},{4,0},{6,2},{8,12},{10,14},{12,8},{14,10},{16,20},{18,... | collective-permute-start | bytes 3145736 | tf_op jit(solution)/shard_map/ppermute | solution.py:355
  357.2 62.8 %collective-permute-start.38 = (bf16[256,2048]{1,0:T(8,128)(2,1)}, bf16[256,2048]{1,0:T(8,128)(2,1)}, u32[]{:S(2)}, u32[]{:S(2)}) collective-permute-start(bf16[256,2048]{1,0:T(8,128)(2,1)} %collective-permute-done.31.refs_0_), channel_id=1, source_target_pairs={{0,8},{2,10},{4,12},{6,14},{8,16},{10,18},{12,20},{14,22},{16,24},... | collective-permute-start | bytes 3145736 | tf_op jit(solution)/shard_map/ppermute | solution.py:363
  357.2 72.1 %collective-permute-start.18 = (bf16[256,2048]{1,0:T(8,128)(2,1)}, bf16[256,2048]{1,0:T(8,128)(2,1)}, u32[]{:S(2)}, u32[]{:S(2)}) collective-permute-start(bf16[256,2048]{1,0:T(8,128)(2,1)} %collective-permute-done.16.refs_1_), channel_id=1, source_target_pairs={{0,2},{2,0},{4,6},{6,4},{8,10},{10,8},{12,14},{14,12},{16,18},{18,... | collective-permute-start | bytes 3145736 | tf_op jit(solution)/shard_map/ppermute | solution.py:355
  362.0 67.7 %collective-permute-start.32 = (bf16[256,2048]{1,0:T(8,128)(2,1)}, bf16[256,2048]{1,0:T(8,128)(2,1)}, u32[]{:S(2)}, u32[]{:S(2)}) collective-permute-start(bf16[256,2048]{1,0:T(8,128)(2,1)} %collective-permute-done.31.refs_0_), channel_id=1, source_target_pairs={{0,4},{2,6},{4,0},{6,2},{8,12},{10,14},{12,8},{14,10},{16,20},{18,... | collective-permute-start | bytes 3145736 | tf_op jit(solution)/shard_map/ppermute | solution.py:355
  416.6 34.1 %copy-start.8 = (s32[4,256]{1,0:T(4,128)}, s32[4,256]{1,0:T(4,128)S(1)}, u32[]{:S(2)}) copy-start(s32[4,256]{1,0:T(4,128)S(1)} %gather_fusion.6) | copy-start | bytes 12292
  418.3 32.4 %copy-start.9 = (s32[4,256]{1,0:T(4,128)}, s32[4,256]{1,0:T(4,128)S(1)}, u32[]{:S(2)}) copy-start(s32[4,256]{1,0:T(4,128)S(1)} %gather_fusion.4) | copy-start | bytes 12292
  419.5 31.3 %collective-permute-start.26 = (bf16[256,2048]{1,0:T(8,128)(2,1)}, bf16[256,2048]{1,0:T(8,128)(2,1)}, u32[]{:S(2)}, u32[]{:S(2)}) collective-permute-start(bf16[256,2048]{1,0:T(8,128)(2,1)} %collective-permute-done.24.refs_0_), channel_id=1, source_target_pairs={{0,2},{2,0},{4,6},{6,4},{8,10},{10,8},{12,14},{14,12},{16,18},{18,... | collective-permute-start | bytes 3145736 | tf_op jit(solution)/shard_map/ppermute | solution.py:355
  419.6 31.6 %collective-permute-start.27 = (bf16[256,2048]{1,0:T(8,128)(2,1)}, bf16[256,2048]{1,0:T(8,128)(2,1)}, u32[]{:S(2)}, u32[]{:S(2)}) collective-permute-start(bf16[256,2048]{1,0:T(8,128)(2,1)} %collective-permute-done.25.refs_1_), channel_id=1, source_target_pairs={{0,2},{2,0},{4,6},{6,4},{8,10},{10,8},{12,14},{14,12},{16,18},{18,... | collective-permute-start | bytes 3145736 | tf_op jit(solution)/shard_map/ppermute | solution.py:355
  420.0 31.3 %collective-permute-start.39 = (bf16[256,2048]{1,0:T(8,128)(2,1)}, bf16[256,2048]{1,0:T(8,128)(2,1)}, u32[]{:S(2)}, u32[]{:S(2)}) collective-permute-start(bf16[256,2048]{1,0:T(8,128)(2,1)} %collective-permute-done.38.refs_0_), channel_id=1, source_target_pairs={{0,4},{2,6},{4,0},{6,2},{8,12},{10,14},{12,8},{14,10},{16,20},{18,... | collective-permute-start | bytes 3145736 | tf_op jit(solution)/shard_map/ppermute | solution.py:355
  423.2 27.6 %copy-start.10 = (s32[4,256]{1,0:T(4,128)}, s32[4,256]{1,0:T(4,128)S(1)}, u32[]{:S(2)}) copy-start(s32[4,256]{1,0:T(4,128)S(1)} %gather_fusion.2) | copy-start | bytes 12292
  424.9 4.9 copy-start.11
  429.2 43.5 %collective-permute-start.33 = (bf16[256,2048]{1,0:T(8,128)(2,1)}, bf16[256,2048]{1,0:T(8,128)(2,1)S(1)}, u32[]{:S(2)}, u32[]{:S(2)}) collective-permute-start(bf16[256,2048]{1,0:T(8,128)(2,1)} %collective-permute-done.31.refs_0_), channel_id=1, source_target_pairs={{0,2},{2,0},{4,6},{6,4},{8,10},{10,8},{12,14},{14,12},{16,18},{18,... | collective-permute-start | bytes 3145736 | tf_op jit(solution)/shard_map/ppermute | solution.py:355
  429.7 44.2 %collective-permute-start.34 = (bf16[256,2048]{1,0:T(8,128)(2,1)}, bf16[256,2048]{1,0:T(8,128)(2,1)}, u32[]{:S(2)}, u32[]{:S(2)}) collective-permute-start(bf16[256,2048]{1,0:T(8,128)(2,1)} %collective-permute-done.32.refs_1_), channel_id=1, source_target_pairs={{0,2},{2,0},{4,6},{6,4},{8,10},{10,8},{12,14},{14,12},{16,18},{18,... | collective-permute-start | bytes 3145736 | tf_op jit(solution)/shard_map/ppermute | solution.py:355
  450.7 65.6 %collective-permute-start.22 = (bf16[2,256,2048]{2,1,0:T(8,128)(2,1)}, bf16[2,256,2048]{2,1,0:T(8,128)(2,1)}, u32[]{:S(2)}, u32[]{:S(2)}) collective-permute-start(bf16[2,256,2048]{2,1,0:T(8,128)(2,1)} %get-tuple-element.26), channel_id=1, source_target_pairs={{0,2},{2,0},{4,6},{6,4},{8,10},{10,8},{12,14},{14,12},{16,18},{18,... | collective-permute-start | bytes 6291464 | tf_op jit(solution)/shard_map/ppermute | solution.py:355
  451.3 43.9 %collective-permute-start.40 = (bf16[256,2048]{1,0:T(8,128)(2,1)}, bf16[256,2048]{1,0:T(8,128)(2,1)}, u32[]{:S(2)}, u32[]{:S(2)}) collective-permute-start(bf16[256,2048]{1,0:T(8,128)(2,1)} %collective-permute-done.38.refs_0_), channel_id=1, source_target_pairs={{0,2},{2,0},{4,6},{6,4},{8,10},{10,8},{12,14},{14,12},{16,18},{18,... | collective-permute-start | bytes 3145736 | tf_op jit(solution)/shard_map/ppermute | solution.py:355
  451.3 43.8 %collective-permute-start.41 = (bf16[256,2048]{1,0:T(8,128)(2,1)}, bf16[256,2048]{1,0:T(8,128)(2,1)}, u32[]{:S(2)}, u32[]{:S(2)}) collective-permute-start(bf16[256,2048]{1,0:T(8,128)(2,1)} %collective-permute-done.39.refs_1_), channel_id=1, source_target_pairs={{0,2},{2,0},{4,6},{6,4},{8,10},{10,8},{12,14},{14,12},{16,18},{18,... | collective-permute-start | bytes 3145736 | tf_op jit(solution)/shard_map/ppermute | solution.py:355
  473.8 44.8 %collective-permute-start.28 = (bf16[2,256,2048]{2,1,0:T(8,128)(2,1)}, bf16[2,256,2048]{2,1,0:T(8,128)(2,1)S(1)}, u32[]{:S(2)}, u32[]{:S(2)}) collective-permute-start(bf16[2,256,2048]{2,1,0:T(8,128)(2,1)} %get-tuple-element.28), channel_id=1, source_target_pairs={{0,2},{2,0},{4,6},{6,4},{8,10},{10,8},{12,14},{14,12},{16,18},{18,... | collective-permute-start | bytes 6291464 | tf_op jit(solution)/shard_map/ppermute | solution.py:355
  494.6 25.8 %collective-permute-start.35 = (bf16[2,256,2048]{2,1,0:T(8,128)(2,1)}, bf16[2,256,2048]{2,1,0:T(8,128)(2,1)S(1)}, u32[]{:S(2)}, u32[]{:S(2)}) collective-permute-start(bf16[2,256,2048]{2,1,0:T(8,128)(2,1)} %get-tuple-element.30), channel_id=1, source_target_pairs={{0,2},{2,0},{4,6},{6,4},{8,10},{10,8},{12,14},{14,12},{16,18},{18,... | collective-permute-start | bytes 6291464 | tf_op jit(solution)/shard_map/ppermute | solution.py:355
  516.2 4.8 collective-permute-start.42
  518.4 92.4 %collective-permute-start.23 = (bf16[256,2048]{1,0:T(8,128)(2,1)S(1)}, bf16[256,2048]{1,0:T(8,128)(2,1)S(1)}, u32[]{:S(2)}, u32[]{:S(2)}) collective-permute-start(bf16[256,2048]{1,0:T(8,128)(2,1)S(1)} %fusion.15), channel_id=1, source_target_pairs={{0,4},{2,6},{4,0},{6,2},{8,12},{10,14},{12,8},{14,10},{16,20},{18,... | collective-permute-start | bytes 3145736 | tf_op jit(solution)/shard_map/ppermute | solution.py:355
  519.0 46.3 %collective-permute-start.29 = (bf16[256,2048]{1,0:T(8,128)(2,1)S(1)}, bf16[256,2048]{1,0:T(8,128)(2,1)S(1)}, u32[]{:S(2)}, u32[]{:S(2)}) collective-permute-start(bf16[256,2048]{1,0:T(8,128)(2,1)S(1)} %fusion.16), channel_id=1, source_target_pairs={{0,4},{2,6},{4,0},{6,2},{8,12},{10,14},{12,8},{14,10},{16,20},{18,... | collective-permute-start | bytes 3145736 | tf_op jit(solution)/shard_map/ppermute | solution.py:355
  520.8 66.9 %collective-permute-start.36 = (bf16[256,2048]{1,0:T(8,128)(2,1)S(1)}, bf16[256,2048]{1,0:T(8,128)(2,1)S(1)}, u32[]{:S(2)}, u32[]{:S(2)}) collective-permute-start(bf16[256,2048]{1,0:T(8,128)(2,1)S(1)} %fusion.17), channel_id=1, source_target_pairs={{0,4},{2,6},{4,0},{6,2},{8,12},{10,14},{12,8},{14,10},{16,20},{18,... | collective-permute-start | bytes 3145736 | tf_op jit(solution)/shard_map/ppermute | solution.py:355
  521.4 88.8 %collective-permute-start.43 = (bf16[256,2048]{1,0:T(8,128)(2,1)S(1)}, bf16[256,2048]{1,0:T(8,128)(2,1)S(1)}, u32[]{:S(2)}, u32[]{:S(2)}) collective-permute-start(bf16[256,2048]{1,0:T(8,128)(2,1)S(1)} %fusion.18), channel_id=1, source_target_pairs={{0,4},{2,6},{4,0},{6,2},{8,12},{10,14},{12,8},{14,10},{16,20},{18,... | collective-permute-start | bytes 3145736 | tf_op jit(solution)/shard_map/ppermute | solution.py:355
  565.8 45.1 %collective-permute-start.30 = (bf16[256,2048]{1,0:T(8,128)(2,1)S(1)}, bf16[256,2048]{1,0:T(8,128)(2,1)S(1)}, u32[]{:S(2)}, u32[]{:S(2)}) collective-permute-start(bf16[256,2048]{1,0:T(8,128)(2,1)S(1)} %fusion.8), channel_id=1, source_target_pairs={{0,24},{2,26},{4,28},{6,30},{8,0},{10,2},{12,4},{14,6},{16,8},{18,... | collective-permute-start | bytes 3145736 | tf_op jit(solution)/shard_map/ppermute | solution.py:363
  588.3 70.6 %copy-start.4 = (bf16[2,256,2048]{2,1,0:T(8,128)(2,1)S(1)}, bf16[2,256,2048]{2,1,0:T(8,128)(2,1)}, u32[]{:S(2)}) copy-start(bf16[2,256,2048]{2,1,0:T(8,128)(2,1)} %get-tuple-element.25) | copy-start | bytes 6291460
  588.3 48.1 %collective-permute-start.37 = (bf16[256,2048]{1,0:T(8,128)(2,1)S(1)}, bf16[256,2048]{1,0:T(8,128)(2,1)S(1)}, u32[]{:S(2)}, u32[]{:S(2)}) collective-permute-start(bf16[256,2048]{1,0:T(8,128)(2,1)S(1)} %fusion.7), channel_id=1, source_target_pairs={{0,16},{2,18},{4,20},{6,22},{8,24},{10,26},{12,28},{14,30},{16,0},... | collective-permute-start | bytes 3145736 | tf_op jit(solution)/shard_map/ppermute | solution.py:363
  610.8 48.1 %collective-permute-start.44 = (bf16[256,2048]{1,0:T(8,128)(2,1)S(1)}, bf16[256,2048]{1,0:T(8,128)(2,1)S(1)}, u32[]{:S(2)}, u32[]{:S(2)}) collective-permute-start(bf16[256,2048]{1,0:T(8,128)(2,1)S(1)} %fusion.6), channel_id=1, source_target_pairs={{0,8},{2,10},{4,12},{6,14},{8,16},{10,18},{12,20},{14,22},{16,24},... | collective-permute-start | bytes 3145736 | tf_op jit(solution)/shard_map/ppermute | solution.py:363
  (8 other events, 12.1 us)

commit v2 on v1

--- a/solution.py
+++ b/solution.py
@@ -23,15 +23,15 @@
     return (NOPE + ROPE) ** (-0.5) * math.log2(math.e)
 
 
-def attend_kernel(blocks, merge, first, last, mode_ref, q_ref, *refs):
+def attend_kernel(blocks, merge, given, last, mode_ref, q_ref, *refs):
     key_refs, refs = refs[:blocks], refs[blocks:]
-    if not first:
-        m_in, l_in, acc_in = refs[:3]
-        refs = refs[3:]
+    if given:
+        states_in, refs = refs[: 3 * given], refs[3 * given :]
     if last:
         wv_ref, out_ref = refs[:2]
         refs = refs[2:]
     m_s, l_s, acc_s, q_s, kt, kk, s0, s1, sems = refs
+    first = given == 0
     heads, _, tokens = q_ref.shape
     units, _, columns = q_s.shape
     block_keys = key_refs[0].shape[1]
@@ -70,9 +70,10 @@
         l_s[...] = jnp.zeros(l_s.shape, jnp.float32)
         acc_s[...] = jnp.zeros(acc_s.shape, jnp.float32)
     else:
-        m_s[...] = m_in[...]
-        l_s[...] = l_in[...]
-        acc_s[...] = acc_in[...]
+        each = units // given
+        for g in range(given):
+            for ref, source in zip((m_s, l_s, acc_s), states_in[3 * g : 3 * g + 3]):
+                ref[g * each : (g + 1) * each] = source[...]
     for h in range(heads):
         q_s[h // merge, :, (h % merge) * tokens : (h % merge + 1) * tokens] = q_ref[h]
 
@@ -168,23 +169,23 @@
         ).astype(out_ref.dtype)
 
 
-def attend(queries, key_blocks, mode, w_value, tokens, state=None, last=True):
+def attend(queries, key_blocks, mode, w_value, tokens, given=(), last=True, part=0, parts=1):
     heads, depth, _ = queries.shape
+    heads = heads // parts
     blocks, block_keys = len(key_blocks), key_blocks[0].shape[1]
     latent, value = w_value.shape[1:]
     merge = min(heads, max(1, 2 * LANES // tokens))
     units, columns = heads // merge, merge * tokens
-    first = state is None
 
     def whole(*shape):
         return pl.BlockSpec(shape, lambda g, mode: (0,) * len(shape))
 
     states = [(units, 1, columns), (units, 1, columns), (units, latent, columns)]
-    in_specs = [pl.BlockSpec((heads, depth, tokens), lambda g, mode: (0, 0, mode[blocks]))]
+    in_specs = [pl.BlockSpec((heads, depth, tokens), lambda g, mode: (part, 0, mode[blocks]))]
     in_specs += [pl.BlockSpec(memory_space=pl.ANY)] * blocks
     operands = [queries, *key_blocks]
-    if not first:
-        in_specs += [whole(*shape) for shape in states]
+    for state in given:
+        in_specs += [whole(units // len(given), *shape[1:]) for shape in states]
         operands += list(state)
     if last:
         in_specs.append(whole(heads, latent, value))
@@ -196,7 +197,7 @@
         out_shape = [jax.ShapeDtypeStruct(shape, jnp.float32) for shape in states]
     pairs = heads * tokens * blocks * block_keys
     made = pl.pallas_call(
-        functools.partial(attend_kernel, blocks, merge, first, last),
+        functools.partial(attend_kernel, blocks, merge, len(given), last),
         grid_spec=pltpu.PrefetchScalarGridSpec(
             num_scalar_prefetch=1,
             grid=(1,),
@@ -345,7 +346,7 @@
     route_scores,
 ):
     count, head_parts, group = sizes["ctx"], sizes["head"], sizes["head"] * sizes["ep"]
-    tokens_here = q_latent.shape[0]
+    tokens_here, heads_here = q_latent.shape[:2]
     rows, _ = resid.shape
     planes = count // SQUARE
     here = lax.axis_index("ctx")
@@ -381,8 +382,20 @@
         shards.append(tuple(shard))
 
     combine = route_scores / jnp.sum(route_scores, axis=1, keepdims=True)
-    table = jnp.concatenate([expert_ids.T.astype(jnp.float32), combine.T], axis=0)
-    tables = lax.all_gather(table, "ctx", axis=0)
+    named = expert_ids.T[None] == jnp.arange(count, dtype=jnp.int32)[:, None, None]
+    chosen = jnp.any(named, axis=1)
+    before = jnp.arange(rows)[:, None] <= jnp.arange(rows)[None, :]
+    ranking = jnp.dot(
+        chosen.astype(jnp.bfloat16), before.astype(jnp.bfloat16), preferred_element_type=jnp.float32
+    )
+    table = jnp.stack(
+        [
+            jnp.where(chosen, ranking - 1.0, -1.0),
+            jnp.sum(jnp.where(named, combine.T[None], 0.0), axis=1),
+        ],
+        axis=1,
+    )
+    tables = lax.all_to_all(table, "ctx", split_axis=0, concat_axis=0, tiled=True)
 
     queries = jnp.transpose(q_latent, (1, 2, 0))
     step = jnp.arange(SQUARE, dtype=jnp.int32)
@@ -404,8 +417,14 @@
         side = lax.axis_index("head") * sizes["ep"] + lax.axis_index("ep")
         halves = {"other": 1 - side, "own": side}
         near, distant = key_blocks[:SQUARE], key_blocks[SQUARE:]
+        cuts = {"other": 2 if heads_here % 4 == 0 else 1, "own": 1}
         states = {
-            which: attend(queries, near, mode_of(block, rows, 0, 1), w_value, rows, last=False)
+            which: [
+                attend(
+                    queries, near, mode_of(block, rows, 0, 1), w_value, rows, last=False, part=part, parts=cuts[which]
+                )
+                for part in range(cuts[which])
+            ]
             for which, block in halves.items()
         }
 
@@ -445,27 +464,22 @@
 
     capacity = 5 * rows * TOPK // (4 * count)
     slots = -(-capacity // 16) * 16
-    named = tables[:, :TOPK, :] == here.astype(jnp.float32)
-    chosen = jnp.any(named, axis=1)
-    weight = jnp.sum(jnp.where(named, tables[:, TOPK:, :], 0.0), axis=1)
-    before = jnp.arange(rows)[:, None] <= jnp.arange(rows)[None, :]
-    ranking = jnp.dot(
-        chosen.astype(jnp.bfloat16), before.astype(jnp.bfloat16), preferred_element_type=jnp.float32
-    )
-    rank = jnp.where(chosen, ranking - 1.0, -1.0).astype(jnp.int32)
-
-    combined = None
-    for n in range(planes):
+    rank = tables[:, 0].astype(jnp.int32)
+    weight = tables[:, 1]
+
+    carried = summed = None
+    for n in list(range(1, planes)) + [0]:
         order = (plane - n) % planes * SQUARE + (spot ^ jnp.array([0, 2, 1, 3], jnp.int32))
         kept, sent = experts(arrived[n], shards, rank[order], weight[order], slots)
         other = swap(sent, 1)
         crossing = (kept[1].astype(jnp.float32) + other[1].astype(jnp.float32)).astype(jnp.bfloat16)
         crossing = swap(crossing, 2)
         summed = kept[0].astype(jnp.float32) + other[0].astype(jnp.float32) + crossing.astype(jnp.float32)
+        if carried is not None:
+            summed = summed + carried.astype(jnp.float32)
         if n:
-            summed = shift(summed.astype(jnp.bfloat16), -n).astype(jnp.float32)
-        combined = summed if combined is None else combined + summed
-    return (widened + routed_factor * combined).astype(jnp.bfloat16)
+            carried = shift(summed.astype(jnp.bfloat16), 1)
+    return (widened + routed_factor * summed).astype(jnp.bfloat16)
 
 
 def solution(mesh):

time: 673 us -> 544 us (0.81)
  the two profiles are of different devices: /device:TPU:11 before, /device:TPU:0 now
where the time goes in v2:
time: 544 us; the launch traced here: 535 us
  waiting for transfers between devices  299 us (55%)
  Pallas kernels  147 us (27%)
  starting transfers between devices  47.7 us (9%)
  other arithmetic  20.7 us (4%)
  local copies, waits for them, and re-layouts  12.3 us (2%)
  matrix products  6.19 us (1%)
    ppermute x9, waiting for transfers between devices, shift(): return lax.ppermute(value, 'ctx', pairs)  118 us
    pallas_call x4, Pallas kernels, experts(): pl.pallas_call(functools.partial(expert_kernel, sources, batches, parts,...  83.8 us
    ppermute x32, waiting for transfers between devices, swap(): return lax.ppermute(value, 'ctx', [(c, c ^ bit) for c in range(count)])  68.4 us
    ppermute x1, waiting for transfers between devices, per_device(): came = lax.ppermute(partial, ('head', 'ep'), [(0, 1), (1, 0)])  67.2 us
    pallas_call x5, Pallas kernels, attend(): pl.pallas_call(functools.partial(attend_kernel, blocks, merge, len(given)...  63.6 us
    ppermute x3, waiting for transfers between devices, per_device(): shard.append(lax.ppermute(shards[0][which], 'head', pairs))  38.8 us
    ppermute x9, starting transfers between devices, shift(): return lax.ppermute(value, 'ctx', pairs)  23.3 us
    ppermute x32, starting transfers between devices, swap(): return lax.ppermute(value, 'ctx', [(c, c ^ bit) for c in range(count)])  16.7 us
  transfers between devices with their start and end apart: 46, of which 15 were waited for; matrix products, arithmetic and copies ran while one was open for 7% of the time, Pallas kernels for 28%

profile of v2, /device:TPU:0, one launch (start us, length us, event | category | flops | bytes accessed | tf_op | source)
XLA Modules:
  0.0 534.7 jit_solution(16032810742851704221)
XLA Ops:
  0.0 5.0 collective-permute-start
  5.0 1.6 collective-permute-start.13
  6.5 11.3 %collective-permute-done.refs_0_ = bf16[576,512]{1,0:T(8,128)(2,1)S(1)} collective-permute-done((bf16[576,512]{1,0:T(8,128)(2,1)}, bf16[576,512]{1,0:T(8,128)(2,1)S(1)}, u32[]{:S(2)}, u32[]{:S(2)}) %collective-permute-start) | collective-permute-done | bytes 589856 | tf_op jit(solution)/shard_map/ppermute | solution.py:364
  17.8 4.3 collective-permute-start.4
  22.4 0.7 compare_select_fusion.3
  23.1 1.5 collective-permute-start.2
  24.7 9.1 %collective-permute-done.4.refs_4_ = bf16[576,512]{1,0:T(8,128)(2,1)S(1)} collective-permute-done((bf16[576,512]{1,0:T(8,128)(2,1)S(1)}, bf16[576,512]{1,0:T(8,128)(2,1)S(1)}, u32[]{:S(2)}, u32[]{:S(2)}) %collective-permute-start.4) | collective-permute-done | bytes 589856 | tf_op jit(solution)/shard_map/ppermute | solution.py:364
  33.8 5.2 collective-permute-start.8
  39.2 0.7 add_add_fusion.mode_ref
  39.8 0.7 add_add_fusion.1.mode_ref
  40.5 0.7 add_add_fusion.2.mode_ref
  41.1 0.7 add_add_fusion.3.mode_ref
  42.3 1.5 collective-permute-start.6
  43.8 5.4 %collective-permute-done.8.refs_8_ = bf16[576,512]{1,0:T(8,128)(2,1)} collective-permute-done((bf16[576,512]{1,0:T(8,128)(2,1)S(1)}, bf16[576,512]{1,0:T(8,128)(2,1)}, u32[]{:S(2)}, u32[]{:S(2)}) %collective-permute-start.8) | collective-permute-done | bytes 589856 | tf_op jit(solution)/shard_map/ppermute | solution.py:364
  49.2 1.5 collective-permute-start.10
  50.7 21.6 %shard_map.145 = (f32[8,1,256]{2,1,0:T(1,128)}, f32[8,1,256]{2,1,0:T(1,128)}, f32[8,512,256]{2,1,0:T(8,128)}) custom-call(s32[6]{0:T(128)} %add_add_fusion.1.mode_ref, bf16[8,576,512]{2,1,0:T(8,128)(2,1)} %bitcast.80, bf16[576,512]{1,0:T(8,128)(2,1)} %bitcast.88, bf16[576,512]{1,0:T(8,128)(2,1)} %copy-done.17, bf16[576,512]{1,0:T(8,128)(2,1)} %copy-done.16, ...), custom_call_target="tpu_custom_call" | custom-call | flops 9126805504 | bytes 2359296 | tf_op jit(solution)/shard_map/pallas_call | solution.py:199
  73.0 13.9 %shard_map.147 = (f32[4,1,256]{2,1,0:T(1,128)}, f32[4,1,256]{2,1,0:T(1,128)}, f32[4,512,256]{2,1,0:T(8,128)}) custom-call(s32[6]{0:T(128)} %add_add_fusion.3.mode_ref, bf16[8,576,512]{2,1,0:T(8,128)(2,1)} %bitcast.81, bf16[576,512]{1,0:T(8,128)(2,1)} %bitcast.89, bf16[576,512]{1,0:T(8,128)(2,1)} %copy-done.17, bf16[576,512]{1,0:T(8,128)(2,1)} %copy-done.16, ...), custom_call_target="tpu_custom_call" | custom-call | flops 4563402752 | bytes 2359296 | tf_op jit(solution)/shard_map/pallas_call | solution.py:199
  86.9 13.6 %shard_map.148 = (f32[4,1,256]{2,1,0:T(1,128)}, f32[4,1,256]{2,1,0:T(1,128)}, f32[4,512,256]{2,1,0:T(8,128)}) custom-call(s32[6]{0:T(128)} %add_add_fusion.3.mode_ref, bf16[8,576,512]{2,1,0:T(8,128)(2,1)} %bitcast.82, bf16[576,512]{1,0:T(8,128)(2,1)} %bitcast.90, bf16[576,512]{1,0:T(8,128)(2,1)} %copy-done.17, bf16[576,512]{1,0:T(8,128)(2,1)} %copy-done.16, ...), custom_call_target="tpu_custom_call" | custom-call | flops 4563402752 | bytes 2359296 | tf_op jit(solution)/shard_map/pallas_call | solution.py:199
  100.6 1.6 collective-permute-start.19
  102.2 1.0 copy-done.19
  103.6 7.6 %shard_map.149 = bf16[8,128,256]{2,1,0:T(8,128)(2,1)} custom-call(s32[14]{0:T(128)} %add_add_fusion.2.mode_ref, bf16[8,576,512]{2,1,0:T(8,128)(2,1)} %bitcast.83, bf16[576,512]{1,0:T(8,128)(2,1)} %copy-done.14, bf16[576,512]{1,0:T(8,128)(2,1)} %copy-done.18, bf16[576,512]{1,0:T(8,128)(2,1)} %collective-permute-done.2.refs_2_, bf16[576,512]{1,0:T(8,128)(2,1)} %copy-done.21, ...), custom_call_target="tpu_custom_call" | custom-call | flops 27380416512 | bytes 7077888 | tf_op jit(solution)/shard_map/pallas_call | solution.py:199
  111.2 2.3 convolution_convert_fusion
  114.1 6.9 %shard_map.146 = bf16[8,128,256]{2,1,0:T(8,128)(2,1)} custom-call(s32[14]{0:T(128)} %add_add_fusion.mode_ref, bf16[8,576,512]{2,1,0:T(8,128)(2,1)} %bitcast.84, bf16[576,512]{1,0:T(8,128)(2,1)} %copy-done.14, bf16[576,512]{1,0:T(8,128)(2,1)} %copy-done.18, bf16[576,512]{1,0:T(8,128)(2,1)} %collective-permute-done.2.refs_2_, bf16[576,512]{1,0:T(8,128)(2,1)} %copy-done.21, ...), custom_call_target="tpu_custom_call" | custom-call | flops 27380416512 | bytes 7077888 | tf_op jit(solution)/shard_map/pallas_call | solution.py:199
  120.9 67.2 %collective-permute-done.15 = bf16[256,2048]{1,0:T(8,128)(2,1)S(1)} collective-permute-done((bf16[256,2048]{1,0:T(8,128)(2,1)S(1)}, bf16[256,2048]{1,0:T(8,128)(2,1)S(1)}, u32[]{:S(2)}, u32[]{:S(2)}) %collective-permute-start.15) | collective-permute-done | bytes 1048608 | tf_op jit(solution)/shard_map/ppermute | solution.py:436
  188.1 3.7 fusion.1
  192.2 1.3 fusion.4.refs_0_
  193.5 2.6 collective-permute-start.24
  196.1 1.5 collective-permute-start.20
  198.1 45.8 %collective-permute-done.24.refs_0_ = bf16[256,2048]{1,0:T(8,128)(2,1)} collective-permute-done((bf16[256,2048]{1,0:T(8,128)(2,1)}, bf16[256,2048]{1,0:T(8,128)(2,1)}, u32[]{:S(2)}, u32[]{:S(2)}) %collective-permute-start.24) | collective-permute-done | bytes 1048608 | tf_op jit(solution)/shard_map/ppermute | solution.py:364
  244.6 23.9 %collective-permute-done.37.refs_1_ = bf16[256,2048]{1,0:T(8,128)(2,1)} collective-permute-done((bf16[256,2048]{1,0:T(8,128)(2,1)}, bf16[256,2048]{1,0:T(8,128)(2,1)}, u32[]{:S(2)}, u32[]{:S(2)}) %collective-permute-start.37) | collective-permute-done | bytes 1048608 | tf_op jit(solution)/shard_map/ppermute | solution.py:356
  269.5 3.5 all-to-all-start
  273.0 6.6 %all-to-all-done = f32[16,2,256]{2,1,0:T(2,128)S(1)} async-done(((f32[16,2,256]{2,1,0:T(2,128)}), f32[16,2,256]{2,1,0:T(2,128)S(1)}, u32[]{:S(2)}, u32[]{:S(2)}) %all-to-all-start) | async-done | bytes 32800 | tf_op jit(solution)/shard_map/all_to_all | solution.py:398
  280.2 0.8 copy.33
  281.0 1.1 gather_fusion.7
  283.1 38.8 %collective-permute-done.21.refs_9_ = bf16[704,2048]{1,0:T(8,128)(2,1)} collective-permute-done((bf16[704,2048]{1,0:T(8,128)(2,1)}, bf16[704,2048]{1,0:T(8,128)(2,1)}, u32[]{:S(2)}, u32[]{:S(2)}) %collective-permute-start.21) | collective-permute-done | bytes 2883616 | tf_op jit(solution)/shard_map/ppermute | solution.py:381
  321.9 20.9 %shard_map.153 = (bf16[2,256,2048]{2,1,0:T(8,128)(2,1)}, bf16[2,256,2048]{2,1,0:T(8,128)(2,1)}) custom-call(s32[4,256]{1,0:T(4,128)} %copy-done.9, s32[256,4]{1,0:T(8,128)} %bitcast.72, f32[4,256]{1,0:T(4,128)} %gather_fusion.7, bf16[256,2048]{1,0:T(8,128)(2,1)} %collective-permute-done.24.refs_0_, bf16[256,2048]{1,0:T(8,128)(2,1)} %collective-permute-done.37.refs_1_, ...), custom_call_target="tpu_custom_call" | custom-call | flops 8858370048 | bytes 25690112 | tf_op jit(solution)/shard_map/pallas_call | solution.py:310
  344.5 1.1 gather_fusion.5
  345.6 0.8 copy.32
  346.4 1.5 collective-permute-start.16
  347.9 0.9 collective-permute-done.33.refs_2_
  349.0 20.7 %collective-permute-done.27.refs_1_ = bf16[256,2048]{1,0:T(8,128)(2,1)} collective-permute-done((bf16[256,2048]{1,0:T(8,128)(2,1)}, bf16[256,2048]{1,0:T(8,128)(2,1)}, u32[]{:S(2)}, u32[]{:S(2)}) %collective-permute-start.27) | collective-permute-done | bytes 1048608 | tf_op jit(solution)/shard_map/ppermute | solution.py:356
  369.7 21.1 %shard_map.152 = (bf16[2,256,2048]{2,1,0:T(8,128)(2,1)}, bf16[2,256,2048]{2,1,0:T(8,128)(2,1)}) custom-call(s32[4,256]{1,0:T(4,128)} %copy-done.11, s32[256,4]{1,0:T(8,128)} %bitcast.73, f32[4,256]{1,0:T(4,128)} %gather_fusion.5, bf16[256,2048]{1,0:T(8,128)(2,1)} %copy-done.13, bf16[256,2048]{1,0:T(8,128)(2,1)} %collective-permute-done.32.refs_1_, ...), custom_call_target="tpu_custom_call" | custom-call | flops 8858370048 | bytes 25690112 | tf_op jit(solution)/shard_map/pallas_call | solution.py:310
  391.4 2.6 fusion.18
  395.1 1.1 gather_fusion.3
  396.9 1.1 gather_fusion.1
  398.0 0.8 copy.31
  398.8 0.8 copy.29
  400.1 20.8 %shard_map.151 = (bf16[2,256,2048]{2,1,0:T(8,128)(2,1)}, bf16[2,256,2048]{2,1,0:T(8,128)(2,1)}) custom-call(s32[4,256]{1,0:T(4,128)} %copy-done.10, s32[256,4]{1,0:T(8,128)} %bitcast.74, f32[4,256]{1,0:T(4,128)} %gather_fusion.3, bf16[256,2048]{1,0:T(8,128)(2,1)} %collective-permute-done.26.refs_0_, bf16[256,2048]{1,0:T(8,128)(2,1)} %collective-permute-done.27.refs_1_, ...), custom_call_target="tpu_custom_call" | custom-call | flops 8858370048 | bytes 25690112 | tf_op jit(solution)/shard_map/pallas_call | solution.py:310
  421.0 3.5 fusion.6
  424.6 1.6 collective-permute-start.42
  426.2 1.4 fusion.17
  427.5 1.5 collective-permute-start.36
  429.0 21.1 %shard_map.150 = (bf16[2,256,2048]{2,1,0:T(8,128)(2,1)}, bf16[2,256,2048]{2,1,0:T(8,128)(2,1)}) custom-call(s32[4,256]{1,0:T(4,128)} %copy-done.8, s32[256,4]{1,0:T(8,128)} %bitcast.71, f32[4,256]{1,0:T(4,128)} %gather_fusion.1, bf16[256,2048]{1,0:T(8,128)(2,1)} %fusion.4.refs_0_, bf16[256,2048]{1,0:T(8,128)(2,1)} %collective-permute-done.16.refs_1_, ...), custom_call_target="tpu_custom_call" | custom-call | flops 8858370048 | bytes 25690112 | tf_op jit(solution)/shard_map/pallas_call | solution.py:310
  450.2 23.4 %collective-permute-done.42 = bf16[256,2048]{1,0:T(8,128)(2,1)} collective-permute-done((bf16[256,2048]{1,0:T(8,128)(2,1)}, bf16[256,2048]{1,0:T(8,128)(2,1)}, u32[]{:S(2)}, u32[]{:S(2)}) %collective-permute-start.42) | collective-permute-done | bytes 1048608 | tf_op jit(solution)/shard_map/ppermute | solution.py:364
  473.6 2.2 fusion.8
  475.8 3.7 collective-permute-start.43
  479.6 1.6 fusion.16
  481.2 1.6 collective-permute-start.31
  483.8 18.8 %collective-permute-done.43 = bf16[256,2048]{1,0:T(8,128)(2,1)S(1)} collective-permute-done((bf16[256,2048]{1,0:T(8,128)(2,1)S(1)}, bf16[256,2048]{1,0:T(8,128)(2,1)S(1)}, u32[]{:S(2)}, u32[]{:S(2)}) %collective-permute-start.43) | collective-permute-done | bytes 1048608 | tf_op jit(solution)/shard_map/ppermute | solution.py:364
  502.6 4.7 collective-permute-done.31
  507.3 1.9 fusion.10
  509.8 18.1 %collective-permute-done.23 = bf16[256,2048]{1,0:T(8,128)(2,1)S(1)} collective-permute-done((bf16[256,2048]{1,0:T(8,128)(2,1)S(1)}, bf16[256,2048]{1,0:T(8,128)(2,1)S(1)}, u32[]{:S(2)}, u32[]{:S(2)}) %collective-permute-start.23) | collective-permute-done | bytes 1048608 | tf_op jit(solution)/shard_map/ppermute | solution.py:356
  527.8 4.5 collective-permute-done.44
  532.4 1.9 fusion.5
  (136 shorter events, 12.8 us)
Async XLA Ops:
  0.0 17.8 %collective-permute-start = (bf16[576,512]{1,0:T(8,128)(2,1)}, bf16[576,512]{1,0:T(8,128)(2,1)S(1)}, u32[]{:S(2)}, u32[]{:S(2)}) collective-permute-start(bf16[576,512]{1,0:T(8,128)(2,1)} %bitcast.85), channel_id=1, source_target_pairs={{0,8},{2,10},{4,12},{6,14},{8,16},{10,18},{12,20},{14,22},{16,24},... | collective-permute-start | bytes 1769480 | tf_op jit(solution)/shard_map/ppermute | solution.py:364
  5.0 19.6 %collective-permute-start.13 = (bf16[576,512]{1,0:T(8,128)(2,1)}, bf16[576,512]{1,0:T(8,128)(2,1)S(1)}, u32[]{:S(2)}, u32[]{:S(2)}) collective-permute-start(bf16[576,512]{1,0:T(8,128)(2,1)} %bitcast.86), channel_id=1, source_target_pairs={{0,4},{2,6},{4,0},{6,2},{8,12},{10,14},{12,8},{14,10},{16,20},{18,... | collective-permute-start | bytes 1769480 | tf_op jit(solution)/shard_map/ppermute | solution.py:356
  17.8 54.4 %copy-start.14 = (bf16[576,512]{1,0:T(8,128)(2,1)}, bf16[576,512]{1,0:T(8,128)(2,1)S(1)}, u32[]{:S(2)}) copy-start(bf16[576,512]{1,0:T(8,128)(2,1)S(1)} %collective-permute-done.refs_0_) | copy-start | bytes 1769476
  17.8 16.0 %collective-permute-start.4 = (bf16[576,512]{1,0:T(8,128)(2,1)S(1)}, bf16[576,512]{1,0:T(8,128)(2,1)S(1)}, u32[]{:S(2)}, u32[]{:S(2)}) collective-permute-start(bf16[576,512]{1,0:T(8,128)(2,1)S(1)} %collective-permute-done.refs_0_), channel_id=1, source_target_pairs={{0,8},{2,10},{4,12},{6,14},{8,16},{10,18},{12,20},{14,22},{16,24},... | collective-permute-start | bytes 1769480 | tf_op jit(solution)/shard_map/ppermute | solution.py:364
  22.2 19.7 %collective-permute-start.12 = (bf16[576,512]{1,0:T(8,128)(2,1)}, bf16[576,512]{1,0:T(8,128)(2,1)S(1)}, u32[]{:S(2)}, u32[]{:S(2)}) collective-permute-start(bf16[576,512]{1,0:T(8,128)(2,1)} %bitcast.87), channel_id=1, source_target_pairs={{0,2},{2,0},{4,6},{6,4},{8,10},{10,8},{12,14},{14,12},{16,18},{18,... | collective-permute-start | bytes 1769480 | tf_op jit(solution)/shard_map/ppermute | solution.py:356
  23.1 19.2 %collective-permute-start.2 = (bf16[576,512]{1,0:T(8,128)(2,1)S(1)}, bf16[576,512]{1,0:T(8,128)(2,1)}, u32[]{:S(2)}, u32[]{:S(2)}) collective-permute-start(bf16[576,512]{1,0:T(8,128)(2,1)S(1)} %collective-permute-done.refs_0_), channel_id=1, source_target_pairs={{0,4},{2,6},{4,0},{6,2},{8,12},{10,14},{12,8},{14,10},{16,20},{18,... | collective-permute-start | bytes 1769480 | tf_op jit(solution)/shard_map/ppermute | solution.py:356
  24.6 26.1 %copy-start.16 = (bf16[576,512]{1,0:T(8,128)(2,1)}, bf16[576,512]{1,0:T(8,128)(2,1)S(1)}, u32[]{:S(2)}) copy-start(bf16[576,512]{1,0:T(8,128)(2,1)S(1)} %collective-permute-done.13.refs_2_) | copy-start | bytes 1769476
  24.6 19.2 %collective-permute-start.14 = (bf16[576,512]{1,0:T(8,128)(2,1)S(1)}, bf16[576,512]{1,0:T(8,128)(2,1)}, u32[]{:S(2)}, u32[]{:S(2)}) collective-permute-start(bf16[576,512]{1,0:T(8,128)(2,1)S(1)} %collective-permute-done.13.refs_2_), channel_id=1, source_target_pairs={{0,2},{2,0},{4,6},{6,4},{8,10},{10,8},{12,14},{14,12},{16,18},{18,... | collective-permute-start | bytes 1769480 | tf_op jit(solution)/shard_map/ppermute | solution.py:356
  33.8 38.4 %copy-start.15 = (bf16[576,512]{1,0:T(8,128)(2,1)}, bf16[576,512]{1,0:T(8,128)(2,1)S(1)}, u32[]{:S(2)}) copy-start(bf16[576,512]{1,0:T(8,128)(2,1)S(1)} %collective-permute-done.4.refs_4_) | copy-start | bytes 1769476
  33.8 15.3 %collective-permute-start.8 = (bf16[576,512]{1,0:T(8,128)(2,1)S(1)}, bf16[576,512]{1,0:T(8,128)(2,1)}, u32[]{:S(2)}, u32[]{:S(2)}) collective-permute-start(bf16[576,512]{1,0:T(8,128)(2,1)S(1)} %collective-permute-done.4.refs_4_), channel_id=1, source_target_pairs={{0,8},{2,10},{4,12},{6,14},{8,16},{10,18},{12,20},{14,22},{16,24},... | collective-permute-start | bytes 1769480 | tf_op jit(solution)/shard_map/ppermute | solution.py:364
  41.8 30.5 %collective-permute-start.1 = (bf16[576,512]{1,0:T(8,128)(2,1)S(1)}, bf16[576,512]{1,0:T(8,128)(2,1)S(1)}, u32[]{:S(2)}, u32[]{:S(2)}) collective-permute-start(bf16[576,512]{1,0:T(8,128)(2,1)S(1)} %collective-permute-done.refs_0_), channel_id=1, source_target_pairs={{0,2},{2,0},{4,6},{6,4},{8,10},{10,8},{12,14},{14,12},{16,18},{18,... | collective-permute-start | bytes 1769480 | tf_op jit(solution)/shard_map/ppermute | solution.py:356
  41.8 8.9 %copy-start.17 = (bf16[576,512]{1,0:T(8,128)(2,1)}, bf16[576,512]{1,0:T(8,128)(2,1)S(1)}, u32[]{:S(2)}) copy-start(bf16[576,512]{1,0:T(8,128)(2,1)S(1)} %collective-permute-done.12.refs_1_) | copy-start | bytes 1769476
  41.8 60.4 %collective-permute-start.5 = (bf16[576,512]{1,0:T(8,128)(2,1)S(1)}, bf16[576,512]{1,0:T(8,128)(2,1)S(1)}, u32[]{:S(2)}, u32[]{:S(2)}) collective-permute-start(bf16[576,512]{1,0:T(8,128)(2,1)S(1)} %collective-permute-done.4.refs_4_), channel_id=1, source_target_pairs={{0,2},{2,0},{4,6},{6,4},{8,10},{10,8},{12,14},{14,12},{16,18},{18,... | collective-permute-start | bytes 1769480 | tf_op jit(solution)/shard_map/ppermute | solution.py:356
  42.3 30.0 %collective-permute-start.6 = (bf16[576,512]{1,0:T(8,128)(2,1)S(1)}, bf16[576,512]{1,0:T(8,128)(2,1)S(1)}, u32[]{:S(2)}, u32[]{:S(2)}) collective-permute-start(bf16[576,512]{1,0:T(8,128)(2,1)S(1)} %collective-permute-done.4.refs_4_), channel_id=1, source_target_pairs={{0,4},{2,6},{4,0},{6,2},{8,12},{10,14},{12,8},{14,10},{16,20},{18,... | collective-permute-start | bytes 1769480 | tf_op jit(solution)/shard_map/ppermute | solution.py:356
  43.8 56.7 %collective-permute-start.3 = (bf16[576,512]{1,0:T(8,128)(2,1)}, bf16[576,512]{1,0:T(8,128)(2,1)S(1)}, u32[]{:S(2)}, u32[]{:S(2)}) collective-permute-start(bf16[576,512]{1,0:T(8,128)(2,1)} %collective-permute-done.2.refs_2_), channel_id=1, source_target_pairs={{0,2},{2,0},{4,6},{6,4},{8,10},{10,8},{12,14},{14,12},{16,18},{18,... | collective-permute-start | bytes 1769480 | tf_op jit(solution)/shard_map/ppermute | solution.py:356
  49.2 23.7 %collective-permute-start.10 = (bf16[576,512]{1,0:T(8,128)(2,1)}, bf16[576,512]{1,0:T(8,128)(2,1)}, u32[]{:S(2)}, u32[]{:S(2)}) collective-permute-start(bf16[576,512]{1,0:T(8,128)(2,1)} %collective-permute-done.8.refs_8_), channel_id=1, source_target_pairs={{0,4},{2,6},{4,0},{6,2},{8,12},{10,14},{12,8},{14,10},{16,20},{18,... | collective-permute-start | bytes 1769480 | tf_op jit(solution)/shard_map/ppermute | solution.py:356
  72.3 14.6 %copy-start.18 = (bf16[576,512]{1,0:T(8,128)(2,1)}, bf16[576,512]{1,0:T(8,128)(2,1)S(1)}, u32[]{:S(2)}) copy-start(bf16[576,512]{1,0:T(8,128)(2,1)S(1)} %collective-permute-done.1.refs_1_) | copy-start | bytes 1769476
  72.3 29.9 %collective-permute-start.9 = (bf16[576,512]{1,0:T(8,128)(2,1)}, bf16[576,512]{1,0:T(8,128)(2,1)S(1)}, u32[]{:S(2)}, u32[]{:S(2)}) collective-permute-start(bf16[576,512]{1,0:T(8,128)(2,1)} %collective-permute-done.8.refs_8_), channel_id=1, source_target_pairs={{0,2},{2,0},{4,6},{6,4},{8,10},{10,8},{12,14},{14,12},{16,18},{18,... | collective-permute-start | bytes 1769480 | tf_op jit(solution)/shard_map/ppermute | solution.py:356
  72.4 14.5 %copy-start.20 = (bf16[576,512]{1,0:T(8,128)(2,1)}, bf16[576,512]{1,0:T(8,128)(2,1)S(1)}, u32[]{:S(2)}) copy-start(bf16[576,512]{1,0:T(8,128)(2,1)S(1)} %collective-permute-done.6.refs_6_) | copy-start | bytes 1769476
  72.4 29.8 %collective-permute-start.7 = (bf16[576,512]{1,0:T(8,128)(2,1)S(1)}, bf16[576,512]{1,0:T(8,128)(2,1)S(1)}, u32[]{:S(2)}, u32[]{:S(2)}) collective-permute-start(bf16[576,512]{1,0:T(8,128)(2,1)S(1)} %collective-permute-done.6.refs_6_), channel_id=1, source_target_pairs={{0,2},{2,0},{4,6},{6,4},{8,10},{10,8},{12,14},{14,12},{16,18},{18,... | collective-permute-start | bytes 1769480 | tf_op jit(solution)/shard_map/ppermute | solution.py:356
  72.9 29.3 %collective-permute-start.11 = (bf16[576,512]{1,0:T(8,128)(2,1)}, bf16[576,512]{1,0:T(8,128)(2,1)S(1)}, u32[]{:S(2)}, u32[]{:S(2)}) collective-permute-start(bf16[576,512]{1,0:T(8,128)(2,1)} %collective-permute-done.10.refs_10_), channel_id=1, source_target_pairs={{0,2},{2,0},{4,6},{6,4},{8,10},{10,8},{12,14},{14,12},{16,18},{18,... | collective-permute-start | bytes 1769480 | tf_op jit(solution)/shard_map/ppermute | solution.py:356
  100.6 144.0 %collective-permute-start.19 = (bf16[704,2048]{1,0:T(8,128)(2,1)}, bf16[704,2048]{1,0:T(8,128)(2,1)}, u32[]{:S(2)}, u32[]{:S(2)}) collective-permute-start(bf16[704,2048]{1,0:T(8,128)(2,1)} %bitcast.16.refs_4_), channel_id=1, source_target_pairs={{0,1},{1,0},{2,3},{3,2},{4,5},{5,4},{6,7},{7,6},{8,9},{9,8},{10,11... | collective-permute-start | bytes 8650760 | tf_op jit(solution)/shard_map/ppermute | solution.py:381
  103.6 7.6 %copy-start = (bf16[1024,2048]{1,0:T(8,128)(2,1)S(1)}, bf16[1024,2048]{1,0:T(8,128)(2,1)}, u32[]{:S(2)}) copy-start(bf16[1024,2048]{1,0:T(8,128)(2,1)} %param.18) | copy-start | bytes 12582916
  113.5 74.6 %collective-permute-start.15 = (bf16[256,2048]{1,0:T(8,128)(2,1)S(1)}, bf16[256,2048]{1,0:T(8,128)(2,1)S(1)}, u32[]{:S(2)}, u32[]{:S(2)}) collective-permute-start(bf16[256,2048]{1,0:T(8,128)(2,1)S(1)} %convolution_convert_fusion), channel_id=1, source_target_pairs={{0,1},{1,0},{2,3},{3,2},{4,5},{5,4},{6,7},{7,6},{8,9},{9,8},{10,11... | collective-permute-start | bytes 3145736 | tf_op jit(solution)/shard_map/ppermute | solution.py:436
  114.1 74.1 %copy-start.5 = (bf16[256,2048]{1,0:T(8,128)(2,1)S(1)}, bf16[256,2048]{1,0:T(8,128)(2,1)}, u32[]{:S(2)}) copy-start(bf16[256,2048]{1,0:T(8,128)(2,1)} %param.19) | copy-start | bytes 3145732
  191.9 52.6 %copy-start.7 = (s32[256,6]{0,1:T(8,128)S(1)}, s32[256,6]{0,1:T(8,128)}, u32[]{:S(2)}) copy-start(s32[256,6]{0,1:T(8,128)} %param.24) | copy-start | bytes 18436
  191.9 76.8 %copy-start.6 = (f32[256,6]{0,1:T(8,128)S(1)}, f32[256,6]{0,1:T(8,128)}, u32[]{:S(2)}) copy-start(f32[256,6]{0,1:T(8,128)} %param.25) | copy-start | bytes 18436
  193.5 50.4 %collective-permute-start.24 = (bf16[256,2048]{1,0:T(8,128)(2,1)}, bf16[256,2048]{1,0:T(8,128)(2,1)}, u32[]{:S(2)}, u32[]{:S(2)}) collective-permute-start(bf16[256,2048]{1,0:T(8,128)(2,1)} %fusion.4.refs_0_), channel_id=1, source_target_pairs={{0,8},{2,10},{4,12},{6,14},{8,16},{10,18},{12,20},{14,22},{16,24},... | collective-permute-start | bytes 3145736 | tf_op jit(solution)/shard_map/ppermute | solution.py:364
  196.1 86.4 %collective-permute-start.20 = (bf16[704,2048]{1,0:T(8,128)(2,1)}, bf16[704,2048]{1,0:T(8,128)(2,1)}, u32[]{:S(2)}, u32[]{:S(2)}) collective-permute-start(bf16[704,2048]{1,0:T(8,128)(2,1)} %bitcast.18.refs_5_), channel_id=1, source_target_pairs={{0,1},{1,0},{2,3},{3,2},{4,5},{5,4},{6,7},{7,6},{8,9},{9,8},{10,11... | collective-permute-start | bytes 8650760 | tf_op jit(solution)/shard_map/ppermute | solution.py:381
  197.6 124.3 %collective-permute-start.21 = (bf16[704,2048]{1,0:T(8,128)(2,1)}, bf16[704,2048]{1,0:T(8,128)(2,1)}, u32[]{:S(2)}, u32[]{:S(2)}) collective-permute-start(bf16[704,2048]{1,0:T(8,128)(2,1)} %bitcast.20.refs_6_), channel_id=1, source_target_pairs={{0,1},{1,0},{2,3},{3,2},{4,5},{5,4},{6,7},{7,6},{8,9},{9,8},{10,11... | collective-permute-start | bytes 8650760 | tf_op jit(solution)/shard_map/ppermute | solution.py:381
  243.9 24.7 %collective-permute-start.37 = (bf16[256,2048]{1,0:T(8,128)(2,1)}, bf16[256,2048]{1,0:T(8,128)(2,1)}, u32[]{:S(2)}, u32[]{:S(2)}) collective-permute-start(bf16[256,2048]{1,0:T(8,128)(2,1)} %collective-permute-done.24.refs_0_), channel_id=1, source_target_pairs={{0,4},{2,6},{4,0},{6,2},{8,12},{10,14},{12,8},{14,10},{16,20},{18,... | collective-permute-start | bytes 3145736 | tf_op jit(solution)/shard_map/ppermute | solution.py:356
  244.5 77.4 %collective-permute-start.38 = (bf16[256,2048]{1,0:T(8,128)(2,1)}, bf16[256,2048]{1,0:T(8,128)(2,1)}, u32[]{:S(2)}, u32[]{:S(2)}) collective-permute-start(bf16[256,2048]{1,0:T(8,128)(2,1)} %collective-permute-done.24.refs_0_), channel_id=1, source_target_pairs={{0,2},{2,0},{4,6},{6,4},{8,10},{10,8},{12,14},{14,12},{16,18},{18,... | collective-permute-start | bytes 3145736 | tf_op jit(solution)/shard_map/ppermute | solution.py:356
  244.6 37.5 %collective-permute-start.25 = (bf16[256,2048]{1,0:T(8,128)(2,1)}, bf16[256,2048]{1,0:T(8,128)(2,1)S(1)}, u32[]{:S(2)}, u32[]{:S(2)}) collective-permute-start(bf16[256,2048]{1,0:T(8,128)(2,1)} %collective-permute-done.24.refs_0_), channel_id=1, source_target_pairs={{0,8},{2,10},{4,12},{6,14},{8,16},{10,18},{12,20},{14,22},{16,24},... | collective-permute-start | bytes 3145736 | tf_op jit(solution)/shard_map/ppermute | solution.py:364
  268.6 53.3 %collective-permute-start.39 = (bf16[256,2048]{1,0:T(8,128)(2,1)}, bf16[256,2048]{1,0:T(8,128)(2,1)}, u32[]{:S(2)}, u32[]{:S(2)}) collective-permute-start(bf16[256,2048]{1,0:T(8,128)(2,1)} %collective-permute-done.37.refs_1_), channel_id=1, source_target_pairs={{0,2},{2,0},{4,6},{6,4},{8,10},{10,8},{12,14},{14,12},{16,18},{18,... | collective-permute-start | bytes 3145736 | tf_op jit(solution)/shard_map/ppermute | solution.py:356
  269.5 10.1 %all-to-all-start = ((f32[16,2,256]{2,1,0:T(2,128)}), f32[16,2,256]{2,1,0:T(2,128)S(1)}, u32[]{:S(2)}, u32[]{:S(2)}) async-start(f32[16,2,256]{2,1,0:T(2,128)} %copy.27), calls=%async_computation | async-start | bytes 65536 | tf_op jit(solution)/shard_map/all_to_all | solution.py:398
  280.2 41.7 %copy-start.9 = (s32[4,256]{1,0:T(4,128)}, s32[4,256]{1,0:T(4,128)S(1)}, u32[]{:S(2)}) copy-start(s32[4,256]{1,0:T(4,128)S(1)} %gather_fusion.6) | copy-start | bytes 12292
  282.1 60.7 %copy-start.13 = (bf16[256,2048]{1,0:T(8,128)(2,1)}, bf16[256,2048]{1,0:T(8,128)(2,1)S(1)}, u32[]{:S(2)}) copy-start(bf16[256,2048]{1,0:T(8,128)(2,1)S(1)} %collective-permute-done.25.refs_0_) | copy-start | bytes 3145732
  282.1 61.2 %collective-permute-start.26 = (bf16[256,2048]{1,0:T(8,128)(2,1)S(1)}, bf16[256,2048]{1,0:T(8,128)(2,1)}, u32[]{:S(2)}, u32[]{:S(2)}) collective-permute-start(bf16[256,2048]{1,0:T(8,128)(2,1)S(1)} %collective-permute-done.25.refs_0_), channel_id=1, source_target_pairs={{0,8},{2,10},{4,12},{6,14},{8,16},{10,18},{12,20},{14,22},{16,24},... | collective-permute-start | bytes 3145736 | tf_op jit(solution)/shard_map/ppermute | solution.py:364
  282.5 61.4 %collective-permute-start.32 = (bf16[256,2048]{1,0:T(8,128)(2,1)S(1)}, bf16[256,2048]{1,0:T(8,128)(2,1)}, u32[]{:S(2)}, u32[]{:S(2)}) collective-permute-start(bf16[256,2048]{1,0:T(8,128)(2,1)S(1)} %collective-permute-done.25.refs_0_), channel_id=1, source_target_pairs={{0,4},{2,6},{4,0},{6,2},{8,12},{10,14},{12,8},{14,10},{16,20},{18,... | collective-permute-start | bytes 3145736 | tf_op jit(solution)/shard_map/ppermute | solution.py:356
  342.8 48.6 %collective-permute-start.40 = (bf16[2,256,2048]{2,1,0:T(8,128)(2,1)}, bf16[2,256,2048]{2,1,0:T(8,128)(2,1)}, u32[]{:S(2)}, u32[]{:S(2)}) collective-permute-start(bf16[2,256,2048]{2,1,0:T(8,128)(2,1)} %get-tuple-element.38), channel_id=1, source_target_pairs={{0,2},{2,0},{4,6},{6,4},{8,10},{10,8},{12,14},{14,12},{16,18},{18,... | collective-permute-start | bytes 6291464 | tf_op jit(solution)/shard_map/ppermute | solution.py:356
  342.9 6.0 %collective-permute-start.33 = (bf16[256,2048]{1,0:T(8,128)(2,1)S(1)}, bf16[256,2048]{1,0:T(8,128)(2,1)}, u32[]{:S(2)}, u32[]{:S(2)}) collective-permute-start(bf16[256,2048]{1,0:T(8,128)(2,1)S(1)} %collective-permute-done.25.refs_0_), channel_id=1, source_target_pairs={{0,2},{2,0},{4,6},{6,4},{8,10},{10,8},{12,14},{14,12},{16,18},{18,... | collective-permute-start | bytes 3145736 | tf_op jit(solution)/shard_map/ppermute | solution.py:356
  343.4 26.3 %collective-permute-start.27 = (bf16[256,2048]{1,0:T(8,128)(2,1)}, bf16[256,2048]{1,0:T(8,128)(2,1)}, u32[]{:S(2)}, u32[]{:S(2)}) collective-permute-start(bf16[256,2048]{1,0:T(8,128)(2,1)} %collective-permute-done.26.refs_0_), channel_id=1, source_target_pairs={{0,4},{2,6},{4,0},{6,2},{8,12},{10,14},{12,8},{14,10},{16,20},{18,... | collective-permute-start | bytes 3145736 | tf_op jit(solution)/shard_map/ppermute | solution.py:356
  343.9 25.8 %collective-permute-start.34 = (bf16[256,2048]{1,0:T(8,128)(2,1)}, bf16[256,2048]{1,0:T(8,128)(2,1)}, u32[]{:S(2)}, u32[]{:S(2)}) collective-permute-start(bf16[256,2048]{1,0:T(8,128)(2,1)} %collective-permute-done.32.refs_1_), channel_id=1, source_target_pairs={{0,2},{2,0},{4,6},{6,4},{8,10},{10,8},{12,14},{14,12},{16,18},{18,... | collective-permute-start | bytes 3145736 | tf_op jit(solution)/shard_map/ppermute | solution.py:356
  344.5 25.2 %copy-start.11 = (s32[4,256]{1,0:T(4,128)}, s32[4,256]{1,0:T(4,128)S(1)}, u32[]{:S(2)}) copy-start(s32[4,256]{1,0:T(4,128)S(1)} %gather_fusion.4) | copy-start | bytes 12292
  346.4 53.2 %collective-permute-start.16 = (bf16[256,2048]{1,0:T(8,128)(2,1)}, bf16[256,2048]{1,0:T(8,128)(2,1)}, u32[]{:S(2)}, u32[]{:S(2)}) collective-permute-start(bf16[256,2048]{1,0:T(8,128)(2,1)} %fusion.4.refs_0_), channel_id=1, source_target_pairs={{0,4},{2,6},{4,0},{6,2},{8,12},{10,14},{12,8},{14,10},{16,20},{18,... | collective-permute-start | bytes 3145736 | tf_op jit(solution)/shard_map/ppermute | solution.py:356
  348.8 50.7 %collective-permute-start.28 = (bf16[256,2048]{1,0:T(8,128)(2,1)}, bf16[256,2048]{1,0:T(8,128)(2,1)}, u32[]{:S(2)}, u32[]{:S(2)}) collective-permute-start(bf16[256,2048]{1,0:T(8,128)(2,1)} %collective-permute-done.26.refs_0_), channel_id=1, source_target_pairs={{0,2},{2,0},{4,6},{6,4},{8,10},{10,8},{12,14},{14,12},{16,18},{18,... | collective-permute-start | bytes 3145736 | tf_op jit(solution)/shard_map/ppermute | solution.py:356
  369.7 30.4 %collective-permute-start.29 = (bf16[256,2048]{1,0:T(8,128)(2,1)}, bf16[256,2048]{1,0:T(8,128)(2,1)}, u32[]{:S(2)}, u32[]{:S(2)}) collective-permute-start(bf16[256,2048]{1,0:T(8,128)(2,1)} %collective-permute-done.27.refs_1_), channel_id=1, source_target_pairs={{0,2},{2,0},{4,6},{6,4},{8,10},{10,8},{12,14},{14,12},{16,18},{18,... | collective-permute-start | bytes 3145736 | tf_op jit(solution)/shard_map/ppermute | solution.py:356
  369.7 21.7 %copy-start.3 = (bf16[2,256,2048]{2,1,0:T(8,128)(2,1)S(1)}, bf16[2,256,2048]{2,1,0:T(8,128)(2,1)}, u32[]{:S(2)}) copy-start(bf16[2,256,2048]{2,1,0:T(8,128)(2,1)} %get-tuple-element.37) | copy-start | bytes 6291460
  390.8 35.4 %collective-permute-start.35 = (bf16[2,256,2048]{2,1,0:T(8,128)(2,1)}, bf16[2,256,2048]{2,1,0:T(8,128)(2,1)S(1)}, u32[]{:S(2)}, u32[]{:S(2)}) collective-permute-start(bf16[2,256,2048]{2,1,0:T(8,128)(2,1)} %get-tuple-element.36), channel_id=1, source_target_pairs={{0,2},{2,0},{4,6},{6,4},{8,10},{10,8},{12,14},{14,12},{16,18},{18,... | collective-permute-start | bytes 6291464 | tf_op jit(solution)/shard_map/ppermute | solution.py:356
  394.0 27.0 %collective-permute-start.41 = (bf16[256,2048]{1,0:T(8,128)(2,1)}, bf16[256,2048]{1,0:T(8,128)(2,1)}, u32[]{:S(2)}, u32[]{:S(2)}) collective-permute-start(bf16[256,2048]{1,0:T(8,128)(2,1)} %fusion.18), channel_id=1, source_target_pairs={{0,4},{2,6},{4,0},{6,2},{8,12},{10,14},{12,8},{14,10},{16,20},{18,... | collective-permute-start | bytes 3145736 | tf_op jit(solution)/shard_map/ppermute | solution.py:356
  396.8 24.1 %copy-start.8 = (s32[4,256]{1,0:T(4,128)}, s32[4,256]{1,0:T(4,128)S(1)}, u32[]{:S(2)}) copy-start(s32[4,256]{1,0:T(4,128)S(1)} %gather_fusion) | copy-start | bytes 12292
  399.6 29.4 %collective-permute-start.17 = (bf16[256,2048]{1,0:T(8,128)(2,1)}, bf16[256,2048]{1,0:T(8,128)(2,1)}, u32[]{:S(2)}, u32[]{:S(2)}) collective-permute-start(bf16[256,2048]{1,0:T(8,128)(2,1)} %fusion.4.refs_0_), channel_id=1, source_target_pairs={{0,2},{2,0},{4,6},{6,4},{8,10},{10,8},{12,14},{14,12},{16,18},{18,... | collective-permute-start | bytes 3145736 | tf_op jit(solution)/shard_map/ppermute | solution.py:356
  399.6 29.4 %collective-permute-start.18 = (bf16[256,2048]{1,0:T(8,128)(2,1)}, bf16[256,2048]{1,0:T(8,128)(2,1)}, u32[]{:S(2)}, u32[]{:S(2)}) collective-permute-start(bf16[256,2048]{1,0:T(8,128)(2,1)} %collective-permute-done.16.refs_1_), channel_id=1, source_target_pairs={{0,2},{2,0},{4,6},{6,4},{8,10},{10,8},{12,14},{14,12},{16,18},{18,... | collective-permute-start | bytes 3145736 | tf_op jit(solution)/shard_map/ppermute | solution.py:356
  420.9 5.3 copy-start.1
  420.9 58.7 %collective-permute-start.30 = (bf16[2,256,2048]{2,1,0:T(8,128)(2,1)}, bf16[2,256,2048]{2,1,0:T(8,128)(2,1)}, u32[]{:S(2)}, u32[]{:S(2)}) collective-permute-start(bf16[2,256,2048]{2,1,0:T(8,128)(2,1)} %get-tuple-element.34), channel_id=1, source_target_pairs={{0,2},{2,0},{4,6},{6,4},{8,10},{10,8},{12,14},{14,12},{16,18},{18,... | collective-permute-start | bytes 6291464 | tf_op jit(solution)/shard_map/ppermute | solution.py:356
  424.6 49.0 %collective-permute-start.42 = (bf16[256,2048]{1,0:T(8,128)(2,1)}, bf16[256,2048]{1,0:T(8,128)(2,1)}, u32[]{:S(2)}, u32[]{:S(2)}) collective-permute-start(bf16[256,2048]{1,0:T(8,128)(2,1)} %fusion.6), channel_id=1, source_target_pairs={{0,8},{2,10},{4,12},{6,14},{8,16},{10,18},{12,20},{14,22},{16,24},... | collective-permute-start | bytes 3145736 | tf_op jit(solution)/shard_map/ppermute | solution.py:364
  427.5 46.0 %collective-permute-start.36 = (bf16[256,2048]{1,0:T(8,128)(2,1)}, bf16[256,2048]{1,0:T(8,128)(2,1)}, u32[]{:S(2)}, u32[]{:S(2)}) collective-permute-start(bf16[256,2048]{1,0:T(8,128)(2,1)} %fusion.17), channel_id=1, source_target_pairs={{0,4},{2,6},{4,0},{6,2},{8,12},{10,14},{12,8},{14,10},{16,20},{18,... | collective-permute-start | bytes 3145736 | tf_op jit(solution)/shard_map/ppermute | solution.py:356
  450.1 29.4 %copy-start.2 = (bf16[2,256,2048]{2,1,0:T(8,128)(2,1)S(1)}, bf16[2,256,2048]{2,1,0:T(8,128)(2,1)}, u32[]{:S(2)}) copy-start(bf16[2,256,2048]{2,1,0:T(8,128)(2,1)} %get-tuple-element.33) | copy-start | bytes 6291460
  450.1 32.6 %collective-permute-start.22 = (bf16[2,256,2048]{2,1,0:T(8,128)(2,1)}, bf16[2,256,2048]{2,1,0:T(8,128)(2,1)S(1)}, u32[]{:S(2)}, u32[]{:S(2)}) collective-permute-start(bf16[2,256,2048]{2,1,0:T(8,128)(2,1)} %get-tuple-element.32), channel_id=1, source_target_pairs={{0,2},{2,0},{4,6},{6,4},{8,10},{10,8},{12,14},{14,12},{16,18},{18,... | collective-permute-start | bytes 6291464 | tf_op jit(solution)/shard_map/ppermute | solution.py:356
  475.8 6.9 %copy-start.4 = (bf16[2,256,2048]{2,1,0:T(8,128)(2,1)S(1)}, bf16[2,256,2048]{2,1,0:T(8,128)(2,1)}, u32[]{:S(2)}) copy-start(bf16[2,256,2048]{2,1,0:T(8,128)(2,1)} %get-tuple-element.31) | copy-start | bytes 6291460
  475.8 26.8 %collective-permute-start.43 = (bf16[256,2048]{1,0:T(8,128)(2,1)S(1)}, bf16[256,2048]{1,0:T(8,128)(2,1)S(1)}, u32[]{:S(2)}, u32[]{:S(2)}) collective-permute-start(bf16[256,2048]{1,0:T(8,128)(2,1)S(1)} %fusion.8), channel_id=1, source_target_pairs={{0,8},{2,10},{4,12},{6,14},{8,16},{10,18},{12,20},{14,22},{16,24},... | collective-permute-start | bytes 3145736 | tf_op jit(solution)/shard_map/ppermute | solution.py:364
  481.2 26.1 %collective-permute-start.31 = (bf16[256,2048]{1,0:T(8,128)(2,1)S(1)}, bf16[256,2048]{1,0:T(8,128)(2,1)S(1)}, u32[]{:S(2)}, u32[]{:S(2)}) collective-permute-start(bf16[256,2048]{1,0:T(8,128)(2,1)S(1)} %fusion.16), channel_id=1, source_target_pairs={{0,4},{2,6},{4,0},{6,2},{8,12},{10,14},{12,8},{14,10},{16,20},{18,... | collective-permute-start | bytes 3145736 | tf_op jit(solution)/shard_map/ppermute | solution.py:356
  483.2 44.7 %collective-permute-start.23 = (bf16[256,2048]{1,0:T(8,128)(2,1)S(1)}, bf16[256,2048]{1,0:T(8,128)(2,1)S(1)}, u32[]{:S(2)}, u32[]{:S(2)}) collective-permute-start(bf16[256,2048]{1,0:T(8,128)(2,1)S(1)} %fusion.15), channel_id=1, source_target_pairs={{0,4},{2,6},{4,0},{6,2},{8,12},{10,14},{12,8},{14,10},{16,20},{18,... | collective-permute-start | bytes 3145736 | tf_op jit(solution)/shard_map/ppermute | solution.py:356
  509.2 23.1 %collective-permute-start.44 = (bf16[256,2048]{1,0:T(8,128)(2,1)S(1)}, bf16[256,2048]{1,0:T(8,128)(2,1)S(1)}, u32[]{:S(2)}, u32[]{:S(2)}) collective-permute-start(bf16[256,2048]{1,0:T(8,128)(2,1)S(1)} %fusion.10), channel_id=1, source_target_pairs={{0,8},{2,10},{4,12},{6,14},{8,16},{10,18},{12,20},{14,22},{16,24},... | collective-permute-start | bytes 3145736 | tf_op jit(solution)/shard_map/ppermute | solution.py:364
  (7 other events, 15.5 us)

commit v3 on v2

--- a/solution.py
+++ b/solution.py
@@ -227,10 +227,9 @@
 def expert_kernel(sources, batches, parts, slots, rank_ref, rank_t_ref, weight_ref, *refs):
     normed, refs = refs[: sources * batches], refs[sources * batches :]
     shards, refs = refs[: 3 * parts], refs[3 * parts :]
-    kept, sent, row_buf, gate_buf, up_buf, down_buf, picked, total, row_sem, weight_sem = refs
+    kept, sent, row_buf, in_buf, down_buf, picked, made_buf, total, row_sem, weight_sem = refs
     tokens = row_buf.shape[1]
     piece = tokens // batches
-    bufs = (gate_buf, up_buf, down_buf)
 
     def row_copy(j, b):
         return pltpu.make_async_copy(
@@ -239,44 +238,42 @@
 
     def shard_copy(n):
         part, which = n // 3, n % 3
-        return pltpu.make_async_copy(
-            shards[n], bufs[which].at[part], weight_sem.at[part, which]
-        )
+        place = in_buf.at[part, which] if which < 2 else down_buf.at[part]
+        return pltpu.make_async_copy(shards[n], place, weight_sem.at[part, which])
 
     for j in range(sources):
         for b in range(batches):
             row_copy(j, b).start()
-    early = 2
-    for n in range(early):
-        shard_copy(n).start()
-
     for j in range(sources):
         slot = lax.broadcasted_iota(jnp.int32, (slots, tokens), 0)
         place = (slot == rank_ref[j : j + 1, :]).astype(jnp.bfloat16)
         for b in range(batches):
             row_copy(j, b).wait()
+        if 0 < j <= 3:
+            shard_copy(j - 1).start()
         picked[j * slots : (j + 1) * slots, :] = jnp.dot(
             place, row_buf[j], preferred_element_type=jnp.float32
         ).astype(jnp.bfloat16)
 
-    for n in range(early, 3 * parts):
+    for n in range(min(3, sources - 1), 3 * parts):
         shard_copy(n).start()
     across = (((1,), (1,)), ((), ()))
     total[...] = jnp.zeros(total.shape, jnp.float32)
 
-    def wait_for(part, which):
-        pltpu.make_async_copy(
-            shards[which], bufs[which].at[part], weight_sem.at[part, which]
-        ).wait()
-
     def one_part(part, unused):
-        rows = picked[...]
-        wait_for(part, 0)
-        gate = lax.dot_general(rows, gate_buf[part], across, preferred_element_type=jnp.float32)
-        wait_for(part, 1)
-        upward = lax.dot_general(rows, up_buf[part], across, preferred_element_type=jnp.float32)
-        hidden = (gate / (1.0 + jnp.exp(-gate)) * upward).astype(jnp.bfloat16)
-        wait_for(part, 2)
+        def one_input(which, inner):
+            pltpu.make_async_copy(
+                shards[0], in_buf.at[part, which], weight_sem.at[part, which]
+            ).wait()
+            made_buf[which] = lax.dot_general(
+                picked[...], in_buf[part, which], across, preferred_element_type=jnp.float32
+            )
+            return inner
+
+        lax.fori_loop(0, 2, one_input, 0)
+        gate = made_buf[0]
+        hidden = (gate / (1.0 + jnp.exp(-gate)) * made_buf[1]).astype(jnp.bfloat16)
+        pltpu.make_async_copy(shards[2], down_buf.at[part], weight_sem.at[part, 2]).wait()
         total[...] += jnp.dot(hidden, down_buf[part], preferred_element_type=jnp.float32)
         return unused
 
@@ -314,10 +311,10 @@
         out_shape=[half, half],
         scratch_shapes=[
             pltpu.VMEM((sources, tokens, width), jnp.bfloat16),
-            pltpu.VMEM((parts, units, width), jnp.bfloat16),
-            pltpu.VMEM((parts, units, width), jnp.bfloat16),
+            pltpu.VMEM((parts, 2, units, width), jnp.bfloat16),
             pltpu.VMEM((parts, units, width), jnp.bfloat16),
             pltpu.VMEM((rows, width), jnp.bfloat16),
+            pltpu.VMEM((2, rows, units), jnp.float32),
             pltpu.VMEM((rows, width), jnp.float32),
             pltpu.SemaphoreType.DMA((sources, batches)),
             pltpu.SemaphoreType.DMA((parts, 3)),
@@ -421,7 +418,14 @@
         states = {
             which: [
                 attend(
-                    queries, near, mode_of(block, rows, 0, 1), w_value, rows, last=False, part=part, parts=cuts[which]
+                    queries,
+                    near,
+                    mode_of(block, rows, 0, 1),
+                    w_value,
+                    rows,
+                    last=False,
+                    part=part,
+                    parts=cuts[which],
                 )
                 for part in range(cuts[which])
             ]

time: 544 us -> 540 us (level)
  transfers between devices with their start and end apart: 46 -> 46, of which waited for: 15 -> 15; matrix products, arithmetic and copies ran while one was open for 7% -> 7% of each run, Pallas kernels for 28% -> 27%
where the time goes in v3:
time: 540 us; the launch traced here: 531 us
  waiting for transfers between devices  301 us (56%)
  Pallas kernels  143 us (26%)
  starting transfers between devices  47.9 us (9%)
  other arithmetic  20.7 us (4%)
  local copies, waits for them, and re-layouts  12.3 us (2%)
  matrix products  6.19 us (1%)
    ppermute x9, waiting for transfers between devices, shift(): return lax.ppermute(value, 'ctx', pairs)  120 us
    pallas_call x4, Pallas kernels, experts(): pl.pallas_call(functools.partial(expert_kernel, sources, batches, parts,...  79 us
    ppermute x32, waiting for transfers between devices, swap(): return lax.ppermute(value, 'ctx', [(c, c ^ bit) for c in range(count)])  68.4 us
    ppermute x1, waiting for transfers between devices, per_device(): came = lax.ppermute(partial, ('head', 'ep'), [(0, 1), (1, 0)])  67.2 us
    pallas_call x5, Pallas kernels, attend(): pl.pallas_call(functools.partial(attend_kernel, blocks, merge, len(given)...  63.6 us
    ppermute x3, waiting for transfers between devices, per_device(): shard.append(lax.ppermute(shards[0][which], 'head', pairs))  38.7 us
    ppermute x9, starting transfers between devices, shift(): return lax.ppermute(value, 'ctx', pairs)  23.4 us
    ppermute x32, starting transfers between devices, swap(): return lax.ppermute(value, 'ctx', [(c, c ^ bit) for c in range(count)])  16.7 us
  transfers between devices with their start and end apart: 46, of which 15 were waited for; matrix products, arithmetic and copies ran while one was open for 7% of the time, Pallas kernels for 27%

profile of v3, /device:TPU:0, one launch (start us, length us, event | category | flops | bytes accessed | tf_op | source)
XLA Modules:
  0.0 531.3 jit_solution(4995282011710927496)
XLA Ops:
  0.0 5.0 collective-permute-start
  5.0 1.6 collective-permute-start.13
  6.5 11.3 %collective-permute-done.refs_0_ = bf16[576,512]{1,0:T(8,128)(2,1)S(1)} collective-permute-done((bf16[576,512]{1,0:T(8,128)(2,1)}, bf16[576,512]{1,0:T(8,128)(2,1)S(1)}, u32[]{:S(2)}, u32[]{:S(2)}) %collective-permute-start) | collective-permute-done | bytes 589856 | tf_op jit(solution)/shard_map/ppermute | solution.py:361
  17.8 4.3 collective-permute-start.4
  22.4 0.7 compare_select_fusion.3
  23.1 1.5 collective-permute-start.2
  24.7 9.1 %collective-permute-done.4.refs_4_ = bf16[576,512]{1,0:T(8,128)(2,1)S(1)} collective-permute-done((bf16[576,512]{1,0:T(8,128)(2,1)S(1)}, bf16[576,512]{1,0:T(8,128)(2,1)S(1)}, u32[]{:S(2)}, u32[]{:S(2)}) %collective-permute-start.4) | collective-permute-done | bytes 589856 | tf_op jit(solution)/shard_map/ppermute | solution.py:361
  33.8 5.2 collective-permute-start.8
  39.2 0.7 add_add_fusion.mode_ref
  39.8 0.7 add_add_fusion.1.mode_ref
  40.5 0.7 add_add_fusion.2.mode_ref
  41.1 0.7 add_add_fusion.3.mode_ref
  42.3 1.5 collective-permute-start.6
  43.8 5.4 %collective-permute-done.8.refs_8_ = bf16[576,512]{1,0:T(8,128)(2,1)} collective-permute-done((bf16[576,512]{1,0:T(8,128)(2,1)S(1)}, bf16[576,512]{1,0:T(8,128)(2,1)}, u32[]{:S(2)}, u32[]{:S(2)}) %collective-permute-start.8) | collective-permute-done | bytes 589856 | tf_op jit(solution)/shard_map/ppermute | solution.py:361
  49.2 1.5 collective-permute-start.10
  50.7 21.6 %shard_map.145 = (f32[8,1,256]{2,1,0:T(1,128)}, f32[8,1,256]{2,1,0:T(1,128)}, f32[8,512,256]{2,1,0:T(8,128)}) custom-call(s32[6]{0:T(128)} %add_add_fusion.1.mode_ref, bf16[8,576,512]{2,1,0:T(8,128)(2,1)} %bitcast.80, bf16[576,512]{1,0:T(8,128)(2,1)} %bitcast.88, bf16[576,512]{1,0:T(8,128)(2,1)} %copy-done.17, bf16[576,512]{1,0:T(8,128)(2,1)} %copy-done.16, ...), custom_call_target="tpu_custom_call" | custom-call | flops 9126805504 | bytes 2359296 | tf_op jit(solution)/shard_map/pallas_call | solution.py:199
  73.0 13.9 %shard_map.147 = (f32[4,1,256]{2,1,0:T(1,128)}, f32[4,1,256]{2,1,0:T(1,128)}, f32[4,512,256]{2,1,0:T(8,128)}) custom-call(s32[6]{0:T(128)} %add_add_fusion.3.mode_ref, bf16[8,576,512]{2,1,0:T(8,128)(2,1)} %bitcast.81, bf16[576,512]{1,0:T(8,128)(2,1)} %bitcast.89, bf16[576,512]{1,0:T(8,128)(2,1)} %copy-done.17, bf16[576,512]{1,0:T(8,128)(2,1)} %copy-done.16, ...), custom_call_target="tpu_custom_call" | custom-call | flops 4563402752 | bytes 2359296 | tf_op jit(solution)/shard_map/pallas_call | solution.py:199
  86.9 13.6 %shard_map.148 = (f32[4,1,256]{2,1,0:T(1,128)}, f32[4,1,256]{2,1,0:T(1,128)}, f32[4,512,256]{2,1,0:T(8,128)}) custom-call(s32[6]{0:T(128)} %add_add_fusion.3.mode_ref, bf16[8,576,512]{2,1,0:T(8,128)(2,1)} %bitcast.82, bf16[576,512]{1,0:T(8,128)(2,1)} %bitcast.90, bf16[576,512]{1,0:T(8,128)(2,1)} %copy-done.17, bf16[576,512]{1,0:T(8,128)(2,1)} %copy-done.16, ...), custom_call_target="tpu_custom_call" | custom-call | flops 4563402752 | bytes 2359296 | tf_op jit(solution)/shard_map/pallas_call | solution.py:199
  100.6 1.6 collective-permute-start.19
  102.2 1.0 copy-done.19
  103.6 7.6 %shard_map.149 = bf16[8,128,256]{2,1,0:T(8,128)(2,1)} custom-call(s32[14]{0:T(128)} %add_add_fusion.2.mode_ref, bf16[8,576,512]{2,1,0:T(8,128)(2,1)} %bitcast.83, bf16[576,512]{1,0:T(8,128)(2,1)} %copy-done.14, bf16[576,512]{1,0:T(8,128)(2,1)} %copy-done.18, bf16[576,512]{1,0:T(8,128)(2,1)} %collective-permute-done.2.refs_2_, bf16[576,512]{1,0:T(8,128)(2,1)} %copy-done.21, ...), custom_call_target="tpu_custom_call" | custom-call | flops 27380416512 | bytes 7077888 | tf_op jit(solution)/shard_map/pallas_call | solution.py:199
  111.2 2.3 convolution_convert_fusion
  114.1 6.9 %shard_map.146 = bf16[8,128,256]{2,1,0:T(8,128)(2,1)} custom-call(s32[14]{0:T(128)} %add_add_fusion.mode_ref, bf16[8,576,512]{2,1,0:T(8,128)(2,1)} %bitcast.84, bf16[576,512]{1,0:T(8,128)(2,1)} %copy-done.14, bf16[576,512]{1,0:T(8,128)(2,1)} %copy-done.18, bf16[576,512]{1,0:T(8,128)(2,1)} %collective-permute-done.2.refs_2_, bf16[576,512]{1,0:T(8,128)(2,1)} %copy-done.21, ...), custom_call_target="tpu_custom_call" | custom-call | flops 27380416512 | bytes 7077888 | tf_op jit(solution)/shard_map/pallas_call | solution.py:199
  120.9 67.2 %collective-permute-done.15 = bf16[256,2048]{1,0:T(8,128)(2,1)S(1)} collective-permute-done((bf16[256,2048]{1,0:T(8,128)(2,1)S(1)}, bf16[256,2048]{1,0:T(8,128)(2,1)S(1)}, u32[]{:S(2)}, u32[]{:S(2)}) %collective-permute-start.15) | collective-permute-done | bytes 1048608 | tf_op jit(solution)/shard_map/ppermute | solution.py:440
  188.1 3.7 fusion.1
  192.2 1.3 fusion.4.refs_0_
  193.5 2.6 collective-permute-start.24
  196.1 1.5 collective-permute-start.20
  198.1 45.8 %collective-permute-done.24.refs_0_ = bf16[256,2048]{1,0:T(8,128)(2,1)} collective-permute-done((bf16[256,2048]{1,0:T(8,128)(2,1)}, bf16[256,2048]{1,0:T(8,128)(2,1)}, u32[]{:S(2)}, u32[]{:S(2)}) %collective-permute-start.24) | collective-permute-done | bytes 1048608 | tf_op jit(solution)/shard_map/ppermute | solution.py:361
  244.6 23.9 %collective-permute-done.37.refs_1_ = bf16[256,2048]{1,0:T(8,128)(2,1)} collective-permute-done((bf16[256,2048]{1,0:T(8,128)(2,1)}, bf16[256,2048]{1,0:T(8,128)(2,1)}, u32[]{:S(2)}, u32[]{:S(2)}) %collective-permute-start.37) | collective-permute-done | bytes 1048608 | tf_op jit(solution)/shard_map/ppermute | solution.py:353
  269.5 3.5 all-to-all-start
  273.0 6.6 %all-to-all-done = f32[16,2,256]{2,1,0:T(2,128)S(1)} async-done(((f32[16,2,256]{2,1,0:T(2,128)}), f32[16,2,256]{2,1,0:T(2,128)S(1)}, u32[]{:S(2)}, u32[]{:S(2)}) %all-to-all-start) | async-done | bytes 32800 | tf_op jit(solution)/shard_map/all_to_all | solution.py:395
  280.2 0.8 copy.33
  281.0 1.1 gather_fusion.7
  283.2 38.7 %collective-permute-done.21.refs_9_ = bf16[704,2048]{1,0:T(8,128)(2,1)} collective-permute-done((bf16[704,2048]{1,0:T(8,128)(2,1)}, bf16[704,2048]{1,0:T(8,128)(2,1)}, u32[]{:S(2)}, u32[]{:S(2)}) %collective-permute-start.21) | collective-permute-done | bytes 2883616 | tf_op jit(solution)/shard_map/ppermute | solution.py:378
  321.9 19.6 %shard_map.153 = (bf16[2,256,2048]{2,1,0:T(8,128)(2,1)}, bf16[2,256,2048]{2,1,0:T(8,128)(2,1)}) custom-call(s32[4,256]{1,0:T(4,128)} %copy-done.9, s32[256,4]{1,0:T(8,128)} %bitcast.72, f32[4,256]{1,0:T(4,128)} %gather_fusion.7, bf16[256,2048]{1,0:T(8,128)(2,1)} %collective-permute-done.24.refs_0_, bf16[256,2048]{1,0:T(8,128)(2,1)} %collective-permute-done.37.refs_1_, ...), custom_call_target="tpu_custom_call" | custom-call | flops 8858370048 | bytes 25690112 | tf_op jit(solution)/shard_map/pallas_call | solution.py:307
  343.2 1.1 gather_fusion.5
  344.4 0.8 copy.32
  345.2 1.5 collective-permute-start.16
  346.7 0.9 collective-permute-done.33.refs_2_
  347.7 20.7 %collective-permute-done.27.refs_1_ = bf16[256,2048]{1,0:T(8,128)(2,1)} collective-permute-done((bf16[256,2048]{1,0:T(8,128)(2,1)}, bf16[256,2048]{1,0:T(8,128)(2,1)}, u32[]{:S(2)}, u32[]{:S(2)}) %collective-permute-start.27) | collective-permute-done | bytes 1048608 | tf_op jit(solution)/shard_map/ppermute | solution.py:353
  368.5 20.0 %shard_map.152 = (bf16[2,256,2048]{2,1,0:T(8,128)(2,1)}, bf16[2,256,2048]{2,1,0:T(8,128)(2,1)}) custom-call(s32[4,256]{1,0:T(4,128)} %copy-done.11, s32[256,4]{1,0:T(8,128)} %bitcast.73, f32[4,256]{1,0:T(4,128)} %gather_fusion.5, bf16[256,2048]{1,0:T(8,128)(2,1)} %copy-done.13, bf16[256,2048]{1,0:T(8,128)(2,1)} %collective-permute-done.32.refs_1_, ...), custom_call_target="tpu_custom_call" | custom-call | flops 8858370048 | bytes 25690112 | tf_op jit(solution)/shard_map/pallas_call | solution.py:307
  389.0 2.6 fusion.18
  392.8 1.1 gather_fusion.3
  394.5 1.1 gather_fusion.1
  395.6 0.8 copy.31
  396.4 0.8 copy.29
  397.8 19.7 %shard_map.151 = (bf16[2,256,2048]{2,1,0:T(8,128)(2,1)}, bf16[2,256,2048]{2,1,0:T(8,128)(2,1)}) custom-call(s32[4,256]{1,0:T(4,128)} %copy-done.10, s32[256,4]{1,0:T(8,128)} %bitcast.74, f32[4,256]{1,0:T(4,128)} %gather_fusion.3, bf16[256,2048]{1,0:T(8,128)(2,1)} %collective-permute-done.26.refs_0_, bf16[256,2048]{1,0:T(8,128)(2,1)} %collective-permute-done.27.refs_1_, ...), custom_call_target="tpu_custom_call" | custom-call | flops 8858370048 | bytes 25690112 | tf_op jit(solution)/shard_map/pallas_call | solution.py:307
  417.6 3.5 fusion.6
  421.1 1.6 collective-permute-start.42
  422.7 1.4 fusion.17
  424.1 1.5 collective-permute-start.36
  425.6 19.7 %shard_map.150 = (bf16[2,256,2048]{2,1,0:T(8,128)(2,1)}, bf16[2,256,2048]{2,1,0:T(8,128)(2,1)}) custom-call(s32[4,256]{1,0:T(4,128)} %copy-done.8, s32[256,4]{1,0:T(8,128)} %bitcast.71, f32[4,256]{1,0:T(4,128)} %gather_fusion.1, bf16[256,2048]{1,0:T(8,128)(2,1)} %fusion.4.refs_0_, bf16[256,2048]{1,0:T(8,128)(2,1)} %collective-permute-done.16.refs_1_, ...), custom_call_target="tpu_custom_call" | custom-call | flops 8858370048 | bytes 25690112 | tf_op jit(solution)/shard_map/pallas_call | solution.py:307
  445.4 24.7 %collective-permute-done.42 = bf16[256,2048]{1,0:T(8,128)(2,1)} collective-permute-done((bf16[256,2048]{1,0:T(8,128)(2,1)}, bf16[256,2048]{1,0:T(8,128)(2,1)}, u32[]{:S(2)}, u32[]{:S(2)}) %collective-permute-start.42) | collective-permute-done | bytes 1048608 | tf_op jit(solution)/shard_map/ppermute | solution.py:361
  470.1 2.2 fusion.8
  472.4 3.7 collective-permute-start.43
  476.1 1.6 fusion.16
  477.8 1.5 collective-permute-start.31
  480.3 18.8 %collective-permute-done.43 = bf16[256,2048]{1,0:T(8,128)(2,1)S(1)} collective-permute-done((bf16[256,2048]{1,0:T(8,128)(2,1)S(1)}, bf16[256,2048]{1,0:T(8,128)(2,1)S(1)}, u32[]{:S(2)}, u32[]{:S(2)}) %collective-permute-start.43) | collective-permute-done | bytes 1048608 | tf_op jit(solution)/shard_map/ppermute | solution.py:361
  499.2 4.7 collective-permute-done.31
  503.9 1.9 fusion.10
  506.3 18.0 %collective-permute-done.23 = bf16[256,2048]{1,0:T(8,128)(2,1)S(1)} collective-permute-done((bf16[256,2048]{1,0:T(8,128)(2,1)S(1)}, bf16[256,2048]{1,0:T(8,128)(2,1)S(1)}, u32[]{:S(2)}, u32[]{:S(2)}) %collective-permute-start.23) | collective-permute-done | bytes 1048608 | tf_op jit(solution)/shard_map/ppermute | solution.py:353
  524.4 4.5 collective-permute-done.44
  528.9 1.9 fusion.5
  (136 shorter events, 13.0 us)
Async XLA Ops:
  0.0 17.8 %collective-permute-start = (bf16[576,512]{1,0:T(8,128)(2,1)}, bf16[576,512]{1,0:T(8,128)(2,1)S(1)}, u32[]{:S(2)}, u32[]{:S(2)}) collective-permute-start(bf16[576,512]{1,0:T(8,128)(2,1)} %bitcast.85), channel_id=1, source_target_pairs={{0,8},{2,10},{4,12},{6,14},{8,16},{10,18},{12,20},{14,22},{16,24},... | collective-permute-start | bytes 1769480 | tf_op jit(solution)/shard_map/ppermute | solution.py:361
  5.0 19.6 %collective-permute-start.13 = (bf16[576,512]{1,0:T(8,128)(2,1)}, bf16[576,512]{1,0:T(8,128)(2,1)S(1)}, u32[]{:S(2)}, u32[]{:S(2)}) collective-permute-start(bf16[576,512]{1,0:T(8,128)(2,1)} %bitcast.86), channel_id=1, source_target_pairs={{0,4},{2,6},{4,0},{6,2},{8,12},{10,14},{12,8},{14,10},{16,20},{18,... | collective-permute-start | bytes 1769480 | tf_op jit(solution)/shard_map/ppermute | solution.py:353
  17.8 54.4 %copy-start.14 = (bf16[576,512]{1,0:T(8,128)(2,1)}, bf16[576,512]{1,0:T(8,128)(2,1)S(1)}, u32[]{:S(2)}) copy-start(bf16[576,512]{1,0:T(8,128)(2,1)S(1)} %collective-permute-done.refs_0_) | copy-start | bytes 1769476
  17.8 16.0 %collective-permute-start.4 = (bf16[576,512]{1,0:T(8,128)(2,1)S(1)}, bf16[576,512]{1,0:T(8,128)(2,1)S(1)}, u32[]{:S(2)}, u32[]{:S(2)}) collective-permute-start(bf16[576,512]{1,0:T(8,128)(2,1)S(1)} %collective-permute-done.refs_0_), channel_id=1, source_target_pairs={{0,8},{2,10},{4,12},{6,14},{8,16},{10,18},{12,20},{14,22},{16,24},... | collective-permute-start | bytes 1769480 | tf_op jit(solution)/shard_map/ppermute | solution.py:361
  22.2 19.7 %collective-permute-start.12 = (bf16[576,512]{1,0:T(8,128)(2,1)}, bf16[576,512]{1,0:T(8,128)(2,1)S(1)}, u32[]{:S(2)}, u32[]{:S(2)}) collective-permute-start(bf16[576,512]{1,0:T(8,128)(2,1)} %bitcast.87), channel_id=1, source_target_pairs={{0,2},{2,0},{4,6},{6,4},{8,10},{10,8},{12,14},{14,12},{16,18},{18,... | collective-permute-start | bytes 1769480 | tf_op jit(solution)/shard_map/ppermute | solution.py:353
  23.1 19.2 %collective-permute-start.2 = (bf16[576,512]{1,0:T(8,128)(2,1)S(1)}, bf16[576,512]{1,0:T(8,128)(2,1)}, u32[]{:S(2)}, u32[]{:S(2)}) collective-permute-start(bf16[576,512]{1,0:T(8,128)(2,1)S(1)} %collective-permute-done.refs_0_), channel_id=1, source_target_pairs={{0,4},{2,6},{4,0},{6,2},{8,12},{10,14},{12,8},{14,10},{16,20},{18,... | collective-permute-start | bytes 1769480 | tf_op jit(solution)/shard_map/ppermute | solution.py:353
  24.6 26.1 %copy-start.16 = (bf16[576,512]{1,0:T(8,128)(2,1)}, bf16[576,512]{1,0:T(8,128)(2,1)S(1)}, u32[]{:S(2)}) copy-start(bf16[576,512]{1,0:T(8,128)(2,1)S(1)} %collective-permute-done.13.refs_2_) | copy-start | bytes 1769476
  24.6 19.2 %collective-permute-start.14 = (bf16[576,512]{1,0:T(8,128)(2,1)S(1)}, bf16[576,512]{1,0:T(8,128)(2,1)}, u32[]{:S(2)}, u32[]{:S(2)}) collective-permute-start(bf16[576,512]{1,0:T(8,128)(2,1)S(1)} %collective-permute-done.13.refs_2_), channel_id=1, source_target_pairs={{0,2},{2,0},{4,6},{6,4},{8,10},{10,8},{12,14},{14,12},{16,18},{18,... | collective-permute-start | bytes 1769480 | tf_op jit(solution)/shard_map/ppermute | solution.py:353
  33.8 38.4 %copy-start.15 = (bf16[576,512]{1,0:T(8,128)(2,1)}, bf16[576,512]{1,0:T(8,128)(2,1)S(1)}, u32[]{:S(2)}) copy-start(bf16[576,512]{1,0:T(8,128)(2,1)S(1)} %collective-permute-done.4.refs_4_) | copy-start | bytes 1769476
  33.8 15.3 %collective-permute-start.8 = (bf16[576,512]{1,0:T(8,128)(2,1)S(1)}, bf16[576,512]{1,0:T(8,128)(2,1)}, u32[]{:S(2)}, u32[]{:S(2)}) collective-permute-start(bf16[576,512]{1,0:T(8,128)(2,1)S(1)} %collective-permute-done.4.refs_4_), channel_id=1, source_target_pairs={{0,8},{2,10},{4,12},{6,14},{8,16},{10,18},{12,20},{14,22},{16,24},... | collective-permute-start | bytes 1769480 | tf_op jit(solution)/shard_map/ppermute | solution.py:361
  41.8 30.5 %collective-permute-start.1 = (bf16[576,512]{1,0:T(8,128)(2,1)S(1)}, bf16[576,512]{1,0:T(8,128)(2,1)S(1)}, u32[]{:S(2)}, u32[]{:S(2)}) collective-permute-start(bf16[576,512]{1,0:T(8,128)(2,1)S(1)} %collective-permute-done.refs_0_), channel_id=1, source_target_pairs={{0,2},{2,0},{4,6},{6,4},{8,10},{10,8},{12,14},{14,12},{16,18},{18,... | collective-permute-start | bytes 1769480 | tf_op jit(solution)/shard_map/ppermute | solution.py:353
  41.8 8.9 %copy-start.17 = (bf16[576,512]{1,0:T(8,128)(2,1)}, bf16[576,512]{1,0:T(8,128)(2,1)S(1)}, u32[]{:S(2)}) copy-start(bf16[576,512]{1,0:T(8,128)(2,1)S(1)} %collective-permute-done.12.refs_1_) | copy-start | bytes 1769476
  41.8 60.4 %collective-permute-start.5 = (bf16[576,512]{1,0:T(8,128)(2,1)S(1)}, bf16[576,512]{1,0:T(8,128)(2,1)S(1)}, u32[]{:S(2)}, u32[]{:S(2)}) collective-permute-start(bf16[576,512]{1,0:T(8,128)(2,1)S(1)} %collective-permute-done.4.refs_4_), channel_id=1, source_target_pairs={{0,2},{2,0},{4,6},{6,4},{8,10},{10,8},{12,14},{14,12},{16,18},{18,... | collective-permute-start | bytes 1769480 | tf_op jit(solution)/shard_map/ppermute | solution.py:353
  42.3 30.0 %collective-permute-start.6 = (bf16[576,512]{1,0:T(8,128)(2,1)S(1)}, bf16[576,512]{1,0:T(8,128)(2,1)S(1)}, u32[]{:S(2)}, u32[]{:S(2)}) collective-permute-start(bf16[576,512]{1,0:T(8,128)(2,1)S(1)} %collective-permute-done.4.refs_4_), channel_id=1, source_target_pairs={{0,4},{2,6},{4,0},{6,2},{8,12},{10,14},{12,8},{14,10},{16,20},{18,... | collective-permute-start | bytes 1769480 | tf_op jit(solution)/shard_map/ppermute | solution.py:353
  43.8 56.7 %collective-permute-start.3 = (bf16[576,512]{1,0:T(8,128)(2,1)}, bf16[576,512]{1,0:T(8,128)(2,1)S(1)}, u32[]{:S(2)}, u32[]{:S(2)}) collective-permute-start(bf16[576,512]{1,0:T(8,128)(2,1)} %collective-permute-done.2.refs_2_), channel_id=1, source_target_pairs={{0,2},{2,0},{4,6},{6,4},{8,10},{10,8},{12,14},{14,12},{16,18},{18,... | collective-permute-start | bytes 1769480 | tf_op jit(solution)/shard_map/ppermute | solution.py:353
  49.2 23.7 %collective-permute-start.10 = (bf16[576,512]{1,0:T(8,128)(2,1)}, bf16[576,512]{1,0:T(8,128)(2,1)}, u32[]{:S(2)}, u32[]{:S(2)}) collective-permute-start(bf16[576,512]{1,0:T(8,128)(2,1)} %collective-permute-done.8.refs_8_), channel_id=1, source_target_pairs={{0,4},{2,6},{4,0},{6,2},{8,12},{10,14},{12,8},{14,10},{16,20},{18,... | collective-permute-start | bytes 1769480 | tf_op jit(solution)/shard_map/ppermute | solution.py:353
  72.3 14.6 %copy-start.18 = (bf16[576,512]{1,0:T(8,128)(2,1)}, bf16[576,512]{1,0:T(8,128)(2,1)S(1)}, u32[]{:S(2)}) copy-start(bf16[576,512]{1,0:T(8,128)(2,1)S(1)} %collective-permute-done.1.refs_1_) | copy-start | bytes 1769476
  72.3 29.9 %collective-permute-start.9 = (bf16[576,512]{1,0:T(8,128)(2,1)}, bf16[576,512]{1,0:T(8,128)(2,1)S(1)}, u32[]{:S(2)}, u32[]{:S(2)}) collective-permute-start(bf16[576,512]{1,0:T(8,128)(2,1)} %collective-permute-done.8.refs_8_), channel_id=1, source_target_pairs={{0,2},{2,0},{4,6},{6,4},{8,10},{10,8},{12,14},{14,12},{16,18},{18,... | collective-permute-start | bytes 1769480 | tf_op jit(solution)/shard_map/ppermute | solution.py:353
  72.4 14.5 %copy-start.20 = (bf16[576,512]{1,0:T(8,128)(2,1)}, bf16[576,512]{1,0:T(8,128)(2,1)S(1)}, u32[]{:S(2)}) copy-start(bf16[576,512]{1,0:T(8,128)(2,1)S(1)} %collective-permute-done.6.refs_6_) | copy-start | bytes 1769476
  72.4 29.8 %collective-permute-start.7 = (bf16[576,512]{1,0:T(8,128)(2,1)S(1)}, bf16[576,512]{1,0:T(8,128)(2,1)S(1)}, u32[]{:S(2)}, u32[]{:S(2)}) collective-permute-start(bf16[576,512]{1,0:T(8,128)(2,1)S(1)} %collective-permute-done.6.refs_6_), channel_id=1, source_target_pairs={{0,2},{2,0},{4,6},{6,4},{8,10},{10,8},{12,14},{14,12},{16,18},{18,... | collective-permute-start | bytes 1769480 | tf_op jit(solution)/shard_map/ppermute | solution.py:353
  72.9 29.3 %collective-permute-start.11 = (bf16[576,512]{1,0:T(8,128)(2,1)}, bf16[576,512]{1,0:T(8,128)(2,1)S(1)}, u32[]{:S(2)}, u32[]{:S(2)}) collective-permute-start(bf16[576,512]{1,0:T(8,128)(2,1)} %collective-permute-done.10.refs_10_), channel_id=1, source_target_pairs={{0,2},{2,0},{4,6},{6,4},{8,10},{10,8},{12,14},{14,12},{16,18},{18,... | collective-permute-start | bytes 1769480 | tf_op jit(solution)/shard_map/ppermute | solution.py:353
  100.6 144.0 %collective-permute-start.19 = (bf16[704,2048]{1,0:T(8,128)(2,1)}, bf16[704,2048]{1,0:T(8,128)(2,1)}, u32[]{:S(2)}, u32[]{:S(2)}) collective-permute-start(bf16[704,2048]{1,0:T(8,128)(2,1)} %bitcast.16.refs_4_), channel_id=1, source_target_pairs={{0,1},{1,0},{2,3},{3,2},{4,5},{5,4},{6,7},{7,6},{8,9},{9,8},{10,11... | collective-permute-start | bytes 8650760 | tf_op jit(solution)/shard_map/ppermute | solution.py:378
  103.6 7.6 %copy-start = (bf16[1024,2048]{1,0:T(8,128)(2,1)S(1)}, bf16[1024,2048]{1,0:T(8,128)(2,1)}, u32[]{:S(2)}) copy-start(bf16[1024,2048]{1,0:T(8,128)(2,1)} %param.18) | copy-start | bytes 12582916
  113.5 74.6 %collective-permute-start.15 = (bf16[256,2048]{1,0:T(8,128)(2,1)S(1)}, bf16[256,2048]{1,0:T(8,128)(2,1)S(1)}, u32[]{:S(2)}, u32[]{:S(2)}) collective-permute-start(bf16[256,2048]{1,0:T(8,128)(2,1)S(1)} %convolution_convert_fusion), channel_id=1, source_target_pairs={{0,1},{1,0},{2,3},{3,2},{4,5},{5,4},{6,7},{7,6},{8,9},{9,8},{10,11... | collective-permute-start | bytes 3145736 | tf_op jit(solution)/shard_map/ppermute | solution.py:440
  114.1 74.1 %copy-start.5 = (bf16[256,2048]{1,0:T(8,128)(2,1)S(1)}, bf16[256,2048]{1,0:T(8,128)(2,1)}, u32[]{:S(2)}) copy-start(bf16[256,2048]{1,0:T(8,128)(2,1)} %param.19) | copy-start | bytes 3145732
  191.9 52.6 %copy-start.7 = (s32[256,6]{0,1:T(8,128)S(1)}, s32[256,6]{0,1:T(8,128)}, u32[]{:S(2)}) copy-start(s32[256,6]{0,1:T(8,128)} %param.24) | copy-start | bytes 18436
  191.9 76.8 %copy-start.6 = (f32[256,6]{0,1:T(8,128)S(1)}, f32[256,6]{0,1:T(8,128)}, u32[]{:S(2)}) copy-start(f32[256,6]{0,1:T(8,128)} %param.25) | copy-start | bytes 18436
  193.5 50.4 %collective-permute-start.24 = (bf16[256,2048]{1,0:T(8,128)(2,1)}, bf16[256,2048]{1,0:T(8,128)(2,1)}, u32[]{:S(2)}, u32[]{:S(2)}) collective-permute-start(bf16[256,2048]{1,0:T(8,128)(2,1)} %fusion.4.refs_0_), channel_id=1, source_target_pairs={{0,8},{2,10},{4,12},{6,14},{8,16},{10,18},{12,20},{14,22},{16,24},... | collective-permute-start | bytes 3145736 | tf_op jit(solution)/shard_map/ppermute | solution.py:361
  196.1 86.5 %collective-permute-start.20 = (bf16[704,2048]{1,0:T(8,128)(2,1)}, bf16[704,2048]{1,0:T(8,128)(2,1)}, u32[]{:S(2)}, u32[]{:S(2)}) collective-permute-start(bf16[704,2048]{1,0:T(8,128)(2,1)} %bitcast.18.refs_5_), channel_id=1, source_target_pairs={{0,1},{1,0},{2,3},{3,2},{4,5},{5,4},{6,7},{7,6},{8,9},{9,8},{10,11... | collective-permute-start | bytes 8650760 | tf_op jit(solution)/shard_map/ppermute | solution.py:378
  197.6 124.3 %collective-permute-start.21 = (bf16[704,2048]{1,0:T(8,128)(2,1)}, bf16[704,2048]{1,0:T(8,128)(2,1)}, u32[]{:S(2)}, u32[]{:S(2)}) collective-permute-start(bf16[704,2048]{1,0:T(8,128)(2,1)} %bitcast.20.refs_6_), channel_id=1, source_target_pairs={{0,1},{1,0},{2,3},{3,2},{4,5},{5,4},{6,7},{7,6},{8,9},{9,8},{10,11... | collective-permute-start | bytes 8650760 | tf_op jit(solution)/shard_map/ppermute | solution.py:378
  243.9 24.7 %collective-permute-start.37 = (bf16[256,2048]{1,0:T(8,128)(2,1)}, bf16[256,2048]{1,0:T(8,128)(2,1)}, u32[]{:S(2)}, u32[]{:S(2)}) collective-permute-start(bf16[256,2048]{1,0:T(8,128)(2,1)} %collective-permute-done.24.refs_0_), channel_id=1, source_target_pairs={{0,4},{2,6},{4,0},{6,2},{8,12},{10,14},{12,8},{14,10},{16,20},{18,... | collective-permute-start | bytes 3145736 | tf_op jit(solution)/shard_map/ppermute | solution.py:353
  244.5 77.4 %collective-permute-start.38 = (bf16[256,2048]{1,0:T(8,128)(2,1)}, bf16[256,2048]{1,0:T(8,128)(2,1)}, u32[]{:S(2)}, u32[]{:S(2)}) collective-permute-start(bf16[256,2048]{1,0:T(8,128)(2,1)} %collective-permute-done.24.refs_0_), channel_id=1, source_target_pairs={{0,2},{2,0},{4,6},{6,4},{8,10},{10,8},{12,14},{14,12},{16,18},{18,... | collective-permute-start | bytes 3145736 | tf_op jit(solution)/shard_map/ppermute | solution.py:353
  244.6 37.5 %collective-permute-start.25 = (bf16[256,2048]{1,0:T(8,128)(2,1)}, bf16[256,2048]{1,0:T(8,128)(2,1)S(1)}, u32[]{:S(2)}, u32[]{:S(2)}) collective-permute-start(bf16[256,2048]{1,0:T(8,128)(2,1)} %collective-permute-done.24.refs_0_), channel_id=1, source_target_pairs={{0,8},{2,10},{4,12},{6,14},{8,16},{10,18},{12,20},{14,22},{16,24},... | collective-permute-start | bytes 3145736 | tf_op jit(solution)/shard_map/ppermute | solution.py:361
  268.6 53.3 %collective-permute-start.39 = (bf16[256,2048]{1,0:T(8,128)(2,1)}, bf16[256,2048]{1,0:T(8,128)(2,1)}, u32[]{:S(2)}, u32[]{:S(2)}) collective-permute-start(bf16[256,2048]{1,0:T(8,128)(2,1)} %collective-permute-done.37.refs_1_), channel_id=1, source_target_pairs={{0,2},{2,0},{4,6},{6,4},{8,10},{10,8},{12,14},{14,12},{16,18},{18,... | collective-permute-start | bytes 3145736 | tf_op jit(solution)/shard_map/ppermute | solution.py:353
  269.5 10.1 %all-to-all-start = ((f32[16,2,256]{2,1,0:T(2,128)}), f32[16,2,256]{2,1,0:T(2,128)S(1)}, u32[]{:S(2)}, u32[]{:S(2)}) async-start(f32[16,2,256]{2,1,0:T(2,128)} %copy.27), calls=%async_computation | async-start | bytes 65536 | tf_op jit(solution)/shard_map/all_to_all | solution.py:395
  280.2 41.7 %copy-start.9 = (s32[4,256]{1,0:T(4,128)}, s32[4,256]{1,0:T(4,128)S(1)}, u32[]{:S(2)}) copy-start(s32[4,256]{1,0:T(4,128)S(1)} %gather_fusion.6) | copy-start | bytes 12292
  282.1 59.5 %copy-start.13 = (bf16[256,2048]{1,0:T(8,128)(2,1)}, bf16[256,2048]{1,0:T(8,128)(2,1)S(1)}, u32[]{:S(2)}) copy-start(bf16[256,2048]{1,0:T(8,128)(2,1)S(1)} %collective-permute-done.25.refs_0_) | copy-start | bytes 3145732
  282.1 60.0 %collective-permute-start.26 = (bf16[256,2048]{1,0:T(8,128)(2,1)S(1)}, bf16[256,2048]{1,0:T(8,128)(2,1)}, u32[]{:S(2)}, u32[]{:S(2)}) collective-permute-start(bf16[256,2048]{1,0:T(8,128)(2,1)S(1)} %collective-permute-done.25.refs_0_), channel_id=1, source_target_pairs={{0,8},{2,10},{4,12},{6,14},{8,16},{10,18},{12,20},{14,22},{16,24},... | collective-permute-start | bytes 3145736 | tf_op jit(solution)/shard_map/ppermute | solution.py:361
  282.6 60.0 %collective-permute-start.32 = (bf16[256,2048]{1,0:T(8,128)(2,1)S(1)}, bf16[256,2048]{1,0:T(8,128)(2,1)}, u32[]{:S(2)}, u32[]{:S(2)}) collective-permute-start(bf16[256,2048]{1,0:T(8,128)(2,1)S(1)} %collective-permute-done.25.refs_0_), channel_id=1, source_target_pairs={{0,4},{2,6},{4,0},{6,2},{8,12},{10,14},{12,8},{14,10},{16,20},{18,... | collective-permute-start | bytes 3145736 | tf_op jit(solution)/shard_map/ppermute | solution.py:353
  341.5 47.5 %collective-permute-start.40 = (bf16[2,256,2048]{2,1,0:T(8,128)(2,1)}, bf16[2,256,2048]{2,1,0:T(8,128)(2,1)}, u32[]{:S(2)}, u32[]{:S(2)}) collective-permute-start(bf16[2,256,2048]{2,1,0:T(8,128)(2,1)} %get-tuple-element.38), channel_id=1, source_target_pairs={{0,2},{2,0},{4,6},{6,4},{8,10},{10,8},{12,14},{14,12},{16,18},{18,... | collective-permute-start | bytes 6291464 | tf_op jit(solution)/shard_map/ppermute | solution.py:353
  341.6 6.0 %collective-permute-start.33 = (bf16[256,2048]{1,0:T(8,128)(2,1)S(1)}, bf16[256,2048]{1,0:T(8,128)(2,1)}, u32[]{:S(2)}, u32[]{:S(2)}) collective-permute-start(bf16[256,2048]{1,0:T(8,128)(2,1)S(1)} %collective-permute-done.25.refs_0_), channel_id=1, source_target_pairs={{0,2},{2,0},{4,6},{6,4},{8,10},{10,8},{12,14},{14,12},{16,18},{18,... | collective-permute-start | bytes 3145736 | tf_op jit(solution)/shard_map/ppermute | solution.py:353
  342.1 26.3 %collective-permute-start.27 = (bf16[256,2048]{1,0:T(8,128)(2,1)}, bf16[256,2048]{1,0:T(8,128)(2,1)}, u32[]{:S(2)}, u32[]{:S(2)}) collective-permute-start(bf16[256,2048]{1,0:T(8,128)(2,1)} %collective-permute-done.26.refs_0_), channel_id=1, source_target_pairs={{0,4},{2,6},{4,0},{6,2},{8,12},{10,14},{12,8},{14,10},{16,20},{18,... | collective-permute-start | bytes 3145736 | tf_op jit(solution)/shard_map/ppermute | solution.py:353
  342.6 25.8 %collective-permute-start.34 = (bf16[256,2048]{1,0:T(8,128)(2,1)}, bf16[256,2048]{1,0:T(8,128)(2,1)}, u32[]{:S(2)}, u32[]{:S(2)}) collective-permute-start(bf16[256,2048]{1,0:T(8,128)(2,1)} %collective-permute-done.32.refs_1_), channel_id=1, source_target_pairs={{0,2},{2,0},{4,6},{6,4},{8,10},{10,8},{12,14},{14,12},{16,18},{18,... | collective-permute-start | bytes 3145736 | tf_op jit(solution)/shard_map/ppermute | solution.py:353
  343.2 25.2 %copy-start.11 = (s32[4,256]{1,0:T(4,128)}, s32[4,256]{1,0:T(4,128)S(1)}, u32[]{:S(2)}) copy-start(s32[4,256]{1,0:T(4,128)S(1)} %gather_fusion.4) | copy-start | bytes 12292
  345.2 52.1 %collective-permute-start.16 = (bf16[256,2048]{1,0:T(8,128)(2,1)}, bf16[256,2048]{1,0:T(8,128)(2,1)}, u32[]{:S(2)}, u32[]{:S(2)}) collective-permute-start(bf16[256,2048]{1,0:T(8,128)(2,1)} %fusion.4.refs_0_), channel_id=1, source_target_pairs={{0,4},{2,6},{4,0},{6,2},{8,12},{10,14},{12,8},{14,10},{16,20},{18,... | collective-permute-start | bytes 3145736 | tf_op jit(solution)/shard_map/ppermute | solution.py:353
  347.6 49.7 %collective-permute-start.28 = (bf16[256,2048]{1,0:T(8,128)(2,1)}, bf16[256,2048]{1,0:T(8,128)(2,1)}, u32[]{:S(2)}, u32[]{:S(2)}) collective-permute-start(bf16[256,2048]{1,0:T(8,128)(2,1)} %collective-permute-done.26.refs_0_), channel_id=1, source_target_pairs={{0,2},{2,0},{4,6},{6,4},{8,10},{10,8},{12,14},{14,12},{16,18},{18,... | collective-permute-start | bytes 3145736 | tf_op jit(solution)/shard_map/ppermute | solution.py:353
  368.4 29.3 %collective-permute-start.29 = (bf16[256,2048]{1,0:T(8,128)(2,1)}, bf16[256,2048]{1,0:T(8,128)(2,1)}, u32[]{:S(2)}, u32[]{:S(2)}) collective-permute-start(bf16[256,2048]{1,0:T(8,128)(2,1)} %collective-permute-done.27.refs_1_), channel_id=1, source_target_pairs={{0,2},{2,0},{4,6},{6,4},{8,10},{10,8},{12,14},{14,12},{16,18},{18,... | collective-permute-start | bytes 3145736 | tf_op jit(solution)/shard_map/ppermute | solution.py:353
  368.4 20.6 %copy-start.3 = (bf16[2,256,2048]{2,1,0:T(8,128)(2,1)S(1)}, bf16[2,256,2048]{2,1,0:T(8,128)(2,1)}, u32[]{:S(2)}) copy-start(bf16[2,256,2048]{2,1,0:T(8,128)(2,1)} %get-tuple-element.37) | copy-start | bytes 6291460
  388.5 34.3 %collective-permute-start.35 = (bf16[2,256,2048]{2,1,0:T(8,128)(2,1)}, bf16[2,256,2048]{2,1,0:T(8,128)(2,1)S(1)}, u32[]{:S(2)}, u32[]{:S(2)}) collective-permute-start(bf16[2,256,2048]{2,1,0:T(8,128)(2,1)} %get-tuple-element.36), channel_id=1, source_target_pairs={{0,2},{2,0},{4,6},{6,4},{8,10},{10,8},{12,14},{14,12},{16,18},{18,... | collective-permute-start | bytes 6291464 | tf_op jit(solution)/shard_map/ppermute | solution.py:353
  391.7 25.9 %collective-permute-start.41 = (bf16[256,2048]{1,0:T(8,128)(2,1)}, bf16[256,2048]{1,0:T(8,128)(2,1)}, u32[]{:S(2)}, u32[]{:S(2)}) collective-permute-start(bf16[256,2048]{1,0:T(8,128)(2,1)} %fusion.18), channel_id=1, source_target_pairs={{0,4},{2,6},{4,0},{6,2},{8,12},{10,14},{12,8},{14,10},{16,20},{18,... | collective-permute-start | bytes 3145736 | tf_op jit(solution)/shard_map/ppermute | solution.py:353
  394.5 23.0 %copy-start.8 = (s32[4,256]{1,0:T(4,128)}, s32[4,256]{1,0:T(4,128)S(1)}, u32[]{:S(2)}) copy-start(s32[4,256]{1,0:T(4,128)S(1)} %gather_fusion) | copy-start | bytes 12292
  397.2 28.3 %collective-permute-start.17 = (bf16[256,2048]{1,0:T(8,128)(2,1)}, bf16[256,2048]{1,0:T(8,128)(2,1)}, u32[]{:S(2)}, u32[]{:S(2)}) collective-permute-start(bf16[256,2048]{1,0:T(8,128)(2,1)} %fusion.4.refs_0_), channel_id=1, source_target_pairs={{0,2},{2,0},{4,6},{6,4},{8,10},{10,8},{12,14},{14,12},{16,18},{18,... | collective-permute-start | bytes 3145736 | tf_op jit(solution)/shard_map/ppermute | solution.py:353
  397.2 28.3 %collective-permute-start.18 = (bf16[256,2048]{1,0:T(8,128)(2,1)}, bf16[256,2048]{1,0:T(8,128)(2,1)}, u32[]{:S(2)}, u32[]{:S(2)}) collective-permute-start(bf16[256,2048]{1,0:T(8,128)(2,1)} %collective-permute-done.16.refs_1_), channel_id=1, source_target_pairs={{0,2},{2,0},{4,6},{6,4},{8,10},{10,8},{12,14},{14,12},{16,18},{18,... | collective-permute-start | bytes 3145736 | tf_op jit(solution)/shard_map/ppermute | solution.py:353
  417.4 5.3 copy-start.1
  417.5 58.7 %collective-permute-start.30 = (bf16[2,256,2048]{2,1,0:T(8,128)(2,1)}, bf16[2,256,2048]{2,1,0:T(8,128)(2,1)}, u32[]{:S(2)}, u32[]{:S(2)}) collective-permute-start(bf16[2,256,2048]{2,1,0:T(8,128)(2,1)} %get-tuple-element.34), channel_id=1, source_target_pairs={{0,2},{2,0},{4,6},{6,4},{8,10},{10,8},{12,14},{14,12},{16,18},{18,... | collective-permute-start | bytes 6291464 | tf_op jit(solution)/shard_map/ppermute | solution.py:353
  421.1 49.0 %collective-permute-start.42 = (bf16[256,2048]{1,0:T(8,128)(2,1)}, bf16[256,2048]{1,0:T(8,128)(2,1)}, u32[]{:S(2)}, u32[]{:S(2)}) collective-permute-start(bf16[256,2048]{1,0:T(8,128)(2,1)} %fusion.6), channel_id=1, source_target_pairs={{0,8},{2,10},{4,12},{6,14},{8,16},{10,18},{12,20},{14,22},{16,24},... | collective-permute-start | bytes 3145736 | tf_op jit(solution)/shard_map/ppermute | solution.py:361
  424.1 46.0 %collective-permute-start.36 = (bf16[256,2048]{1,0:T(8,128)(2,1)}, bf16[256,2048]{1,0:T(8,128)(2,1)}, u32[]{:S(2)}, u32[]{:S(2)}) collective-permute-start(bf16[256,2048]{1,0:T(8,128)(2,1)} %fusion.17), channel_id=1, source_target_pairs={{0,4},{2,6},{4,0},{6,2},{8,12},{10,14},{12,8},{14,10},{16,20},{18,... | collective-permute-start | bytes 3145736 | tf_op jit(solution)/shard_map/ppermute | solution.py:353
  445.3 30.8 %copy-start.2 = (bf16[2,256,2048]{2,1,0:T(8,128)(2,1)S(1)}, bf16[2,256,2048]{2,1,0:T(8,128)(2,1)}, u32[]{:S(2)}) copy-start(bf16[2,256,2048]{2,1,0:T(8,128)(2,1)} %get-tuple-element.33) | copy-start | bytes 6291460
  445.3 34.0 %collective-permute-start.22 = (bf16[2,256,2048]{2,1,0:T(8,128)(2,1)}, bf16[2,256,2048]{2,1,0:T(8,128)(2,1)S(1)}, u32[]{:S(2)}, u32[]{:S(2)}) collective-permute-start(bf16[2,256,2048]{2,1,0:T(8,128)(2,1)} %get-tuple-element.32), channel_id=1, source_target_pairs={{0,2},{2,0},{4,6},{6,4},{8,10},{10,8},{12,14},{14,12},{16,18},{18,... | collective-permute-start | bytes 6291464 | tf_op jit(solution)/shard_map/ppermute | solution.py:353
  472.4 6.9 %copy-start.4 = (bf16[2,256,2048]{2,1,0:T(8,128)(2,1)S(1)}, bf16[2,256,2048]{2,1,0:T(8,128)(2,1)}, u32[]{:S(2)}) copy-start(bf16[2,256,2048]{2,1,0:T(8,128)(2,1)} %get-tuple-element.31) | copy-start | bytes 6291460
  472.4 26.8 %collective-permute-start.43 = (bf16[256,2048]{1,0:T(8,128)(2,1)S(1)}, bf16[256,2048]{1,0:T(8,128)(2,1)S(1)}, u32[]{:S(2)}, u32[]{:S(2)}) collective-permute-start(bf16[256,2048]{1,0:T(8,128)(2,1)S(1)} %fusion.8), channel_id=1, source_target_pairs={{0,8},{2,10},{4,12},{6,14},{8,16},{10,18},{12,20},{14,22},{16,24},... | collective-permute-start | bytes 3145736 | tf_op jit(solution)/shard_map/ppermute | solution.py:361
  477.8 26.1 %collective-permute-start.31 = (bf16[256,2048]{1,0:T(8,128)(2,1)S(1)}, bf16[256,2048]{1,0:T(8,128)(2,1)S(1)}, u32[]{:S(2)}, u32[]{:S(2)}) collective-permute-start(bf16[256,2048]{1,0:T(8,128)(2,1)S(1)} %fusion.16), channel_id=1, source_target_pairs={{0,4},{2,6},{4,0},{6,2},{8,12},{10,14},{12,8},{14,10},{16,20},{18,... | collective-permute-start | bytes 3145736 | tf_op jit(solution)/shard_map/ppermute | solution.py:353
  479.7 44.7 %collective-permute-start.23 = (bf16[256,2048]{1,0:T(8,128)(2,1)S(1)}, bf16[256,2048]{1,0:T(8,128)(2,1)S(1)}, u32[]{:S(2)}, u32[]{:S(2)}) collective-permute-start(bf16[256,2048]{1,0:T(8,128)(2,1)S(1)} %fusion.15), channel_id=1, source_target_pairs={{0,4},{2,6},{4,0},{6,2},{8,12},{10,14},{12,8},{14,10},{16,20},{18,... | collective-permute-start | bytes 3145736 | tf_op jit(solution)/shard_map/ppermute | solution.py:353
  505.8 23.1 %collective-permute-start.44 = (bf16[256,2048]{1,0:T(8,128)(2,1)S(1)}, bf16[256,2048]{1,0:T(8,128)(2,1)S(1)}, u32[]{:S(2)}, u32[]{:S(2)}) collective-permute-start(bf16[256,2048]{1,0:T(8,128)(2,1)S(1)} %fusion.10), channel_id=1, source_target_pairs={{0,8},{2,10},{4,12},{6,14},{8,16},{10,18},{12,20},{14,22},{16,24},... | collective-permute-start | bytes 3145736 | tf_op jit(solution)/shard_map/ppermute | solution.py:361
  (7 other events, 15.5 us)
